TPU v7x, 32 devices: a whole 2x2x4 slice. The times are simulated.
32 devices in a mesh: dp: 8 (over y, x, core), tensor: 4 (over z).
Axes of the slice: x: 2, y: 2, z: 4, core: 2. Of those that a mesh axis runs over, the one named last changes fastest.
Arguments:
- x_prompt: bfloat16 [8192, 768], P('dp'), may hold values from -6 to 6
- x_cont: bfloat16 [4096, 768], P('dp'), may hold values from -6 to 6
- enc_out: bfloat16 [4096, 768], P('dp'), may hold values from -6 to 6
- cot_prompt: bfloat16 [8192, 768], P(('dp', 'tensor')), may hold values from -6 to 6
- cot_cont: bfloat16 [4096, 768], P(('dp', 'tensor')), may hold values from -6 to 6
- teacher: bfloat16 [4096, 768], P(('dp', 'tensor')), may hold values from -6 to 6
- valid: int32 [4096], P('dp'), may hold values from 0 to 1, as said below
- prompt_of: int32 [32], P('dp'), may hold values from 0 to 7, as said below
- buckets: int32 [1152], replicated, may hold values from 0 to 31
- gain_self: float32 [768], replicated, may hold values from 0.5 to 1.5
- gain_cross: float32 [768], replicated, may hold values from 0.5 to 1.5
- gain_ffn: float32 [768], replicated, may hold values from 0.5 to 1.5
- rel_table: float32 [32, 12], P(None, 'tensor'), may hold values from -6 to 6
- w_q: bfloat16 [768, 768], P(None, 'tensor'), may hold values from -0.21875 to 0.21875
- w_k: bfloat16 [768, 768], P(None, 'tensor'), may hold values from -0.21875 to 0.21875
- w_v: bfloat16 [768, 768], P(None, 'tensor'), may hold values from -0.21875 to 0.21875
- w_o: bfloat16 [768, 768], P('tensor'), may hold values from -0.875 to 0.875
- c_q: bfloat16 [768, 768], P(None, 'tensor'), may hold values from -0.21875 to 0.21875
- c_k: bfloat16 [768, 768], P(None, 'tensor'), may hold values from -0.21875 to 0.21875
- c_v: bfloat16 [768, 768], P(None, 'tensor'), may hold values from -0.21875 to 0.21875
- c_o: bfloat16 [768, 768], P('tensor'), may hold values from -0.875 to 0.875
- w_gate: bfloat16 [768, 2048], P(None, 'tensor'), may hold values from -0.21875 to 0.21875
- w_up: bfloat16 [768, 2048], P(None, 'tensor'), may hold values from -0.21875 to 0.21875
- w_down: bfloat16 [2048, 768], P('tensor'), may hold values from -0.125 to 0.125
Outputs:
- y_prompt: bfloat16 [8192, 768], P(('dp', 'tensor'))
- y_cont: bfloat16 [4096, 768], P(('dp', 'tensor'))
- grad_x_prompt: float32 [8192, 768], P(('dp', 'tensor'))
- grad_x_cont: float32 [4096, 768], P(('dp', 'tensor'))
- grad_enc: float32 [4096, 768], P('dp')
- grad_gain_self: float32 [768], replicated
- grad_gain_cross: float32 [768], replicated
- grad_gain_ffn: float32 [768], replicated
- grad_rel_table: float32 [32, 12], P(None, 'tensor')
- grad_w_q: float32 [768, 768], P(None, 'tensor')
- grad_w_k: float32 [768, 768], P(None, 'tensor')
- grad_w_v: float32 [768, 768], P(None, 'tensor')
- grad_w_o: float32 [768, 768], P('tensor')
- grad_c_q: float32 [768, 768], P(None, 'tensor')
- grad_c_k: float32 [768, 768], P(None, 'tensor')
- grad_c_v: float32 [768, 768], P(None, 'tensor')
- grad_c_o: float32 [768, 768], P('tensor')
- grad_w_gate: float32 [768, 2048], P(None, 'tensor')
- grad_w_up: float32 [768, 2048], P(None, 'tensor')
- grad_w_down: float32 [2048, 768], P('tensor')
- loss: float32 [], replicated
Inputs may be any that keep to these rules, and one draw needn't show every extreme that they name: The valid tokens of each continuation are a prefix of it, of 1 to 128 tokens. `prompt_of`: in the k-th aligned block of 4 entries (the continuations of group k), two entries name group k and two name group k xor 1.
All inputs are finite; a program needn't handle non-finite values.
Results may differ from a plain program's by a relative error of at most 0.023.
Values may be sent and summed in bfloat16 or wider, within the bound.
A program may use at most 192 MiB of HBM per device.

v0:
```python
import jax
import jax.numpy as jnp
from jax import lax
from jax.sharding import PartitionSpec as P

HEAD = 64
PROMPT = 1024
CONT_LEN = 128
ENC_LEN = 512


norm_eps = 1e-06
masked_value = -1e30


def partner(block, axis, distance):
    count = lax.axis_size(axis)
    route = []
    for low in range(count):
        high = low | 1 << distance
        if high != low and high < count:
            route += [(low, high), (high, low)]
    return lax.ppermute(block, axis, route)


def rms_norm(values, weight):
    return values * lax.rsqrt(jnp.mean(values * values, axis=-1, keepdims=True) + norm_eps) * weight


def project(left_in, right_in):
    return jnp.dot(left_in, right_in, preferred_element_type=jnp.float32)


def weight_grad(left_in, right_in):
    return jnp.einsum("ri,ro->io", left_in, right_in, preferred_element_type=jnp.float32)


def input_grad(grad_in, weight):
    return jnp.einsum("ro,io->ri", grad_in, weight, preferred_element_type=jnp.float32)


def gather_groups(picker, group_table):
    return jnp.einsum(
        "bg,gkhe->bkhe", picker, group_table, preferred_element_type=jnp.float32
    ).astype(jnp.bfloat16)


def spread_groups(picker, grad_in):
    return jnp.einsum("bg,bkhe->gkhe", picker, grad_in, precision=lax.Precision.HIGHEST)


def skew_bias(table, row_start, rows, keys):
    width = rows + keys
    dist_idx = jnp.clip(row_start + rows - 1 - jnp.arange(width), 0, table.shape[1] - 1)
    line = jnp.take(table, dist_idx, axis=1)
    tiled = jnp.tile(line, (1, rows))[:, : rows * (width - 1)].reshape(
        table.shape[0], rows, width - 1
    )
    return tiled[:, :, rows - 1 : rows - 1 + keys]


def skew_grad(grad_scores, row_start, rows, keys, dist_count):
    summed = jnp.sum(grad_scores.astype(jnp.float32), axis=0)
    heads_here = summed.shape[0]
    width = rows + keys
    padded = jnp.pad(summed, ((0, 0), (0, 0), (rows - 1, 0)))
    flat = jnp.pad(padded.reshape(heads_here, rows * (width - 1)), ((0, 0), (0, rows)))
    folded = jnp.sum(flat.reshape(heads_here, rows, width), axis=1)
    top = row_start + rows
    return jnp.pad(jnp.flip(folded, 1)[:, width - top :], ((0, 0), (0, dist_count - top)))


def score_block(queries, keys_in, pos_bias, allowed, factor):
    scores = (
        jnp.einsum("brhe,bkhe->bhrk", queries, keys_in, preferred_element_type=jnp.float32) * factor
    )
    if pos_bias is not None:
        scores = scores + pos_bias[None]
    if allowed is not None:
        scores = jnp.where(allowed[:, None], scores, masked_value)
    return scores


def attend_fwd(queries, keys_in, values_in, pos_bias, allowed, factor):
    scores = score_block(queries, keys_in, pos_bias, allowed, factor)
    topmost = jnp.max(scores, axis=-1, keepdims=True)
    expsum = jnp.exp(scores - topmost)
    totals = jnp.sum(expsum, axis=-1, keepdims=True)
    probabilities = (expsum / totals).astype(jnp.bfloat16)
    mixture = jnp.einsum(
        "bhrk,bkhe->brhe", probabilities, values_in, preferred_element_type=jnp.float32
    )
    return (mixture, topmost + jnp.log(totals))


def attend_back(queries, keys_in, values_in, pos_bias, allowed, factor, logsum, grad_out):
    scores = score_block(queries, keys_in, pos_bias, allowed, factor)
    probabilities = jnp.exp(scores - logsum)
    grad_probs = jnp.einsum(
        "brhe,bkhe->bhrk", grad_out, values_in, preferred_element_type=jnp.float32
    )
    centre = jnp.sum(probabilities * grad_probs, axis=-1, keepdims=True)
    grad_scores = (probabilities * (grad_probs - centre)).astype(jnp.bfloat16)
    grad_query = (
        jnp.einsum("bhrk,bkhe->brhe", grad_scores, keys_in, preferred_element_type=jnp.float32)
        * factor
    )
    grad_keys = (
        jnp.einsum("bhrk,brhe->bkhe", grad_scores, queries, preferred_element_type=jnp.float32)
        * factor
    )
    grad_values = jnp.einsum(
        "bhrk,brhe->bkhe",
        probabilities.astype(jnp.bfloat16),
        grad_out,
        preferred_element_type=jnp.float32,
    )
    return (grad_query, grad_keys, grad_values, grad_scores)


def on_device(
    x_prompt,
    x_cont,
    enc_out,
    cot_prompt,
    cot_cont,
    teacher,
    valid,
    prompt_of,
    buckets,
    gain_self,
    gain_cross,
    gain_ffn,
    rel_table,
    w_q,
    w_k,
    w_v,
    w_o,
    c_q,
    c_k,
    c_v,
    c_o,
    w_gate,
    w_up,
    w_down,
):
    group_count = x_prompt.shape[0] // PROMPT
    cont_count = prompt_of.shape[0]
    heads_here = w_q.shape[1] // HEAD
    head_cols = heads_here * HEAD
    prompt_rows = group_count * PROMPT
    cont_total = cont_count * CONT_LEN
    dist_count = PROMPT + CONT_LEN
    factor = HEAD ** (-0.5)
    block_rows = min(512, PROMPT)
    block_count = PROMPT // block_rows
    cont_block = min(cont_count, max(1, 512 // CONT_LEN))
    cont_rows = cont_block * CONT_LEN
    tensor_parts = lax.axis_size("tensor")
    share_prompt = prompt_rows // tensor_parts
    share_cont = cont_total // tensor_parts
    tensor_rank = lax.axis_index("tensor")
    data_rank = lax.axis_index("dp")
    parity = data_rank % 2
    token_count = lax.psum(jnp.sum(valid.astype(jnp.float32)), "dp")
    local_of = prompt_of - data_rank // 2 * (2 * group_count)
    picked = local_of[:, None] == jnp.arange(2 * group_count)[None, :]
    pick_low = picked.astype(jnp.bfloat16)
    pick_full = picked.astype(jnp.float32)
    bucket_hot = (buckets[:, None] == jnp.arange(rel_table.shape[0])[None, :]).astype(jnp.float32)
    bias_table = jnp.dot(bucket_hot, rel_table, precision=lax.Precision.HIGHEST).T
    prompt_geo = []
    for block_idx in range(block_count):
        row_start = block_idx * block_rows
        row_pos = row_start + jnp.arange(block_rows)
        distance = row_pos[:, None] - jnp.arange(PROMPT)[None, :]
        prompt_geo.append(
            (skew_bias(bias_table, row_start, block_rows, PROMPT), (distance >= 0)[None])
        )
    cont_dist = PROMPT + jnp.arange(CONT_LEN)[:, None] - jnp.arange(dist_count)[None, :]
    cont_bias = skew_bias(bias_table, PROMPT, CONT_LEN, dist_count)
    valid_rows = valid.reshape(cont_count, CONT_LEN) > 0
    cont_allowed = []
    keys_ok = jnp.concatenate([jnp.ones((cont_block, PROMPT), jnp.bool_), valid_rows], axis=1)
    cont_allowed.append((cont_dist >= 0)[None] & keys_ok[:, None, :])

    def to_prompt(values):
        return values[:prompt_rows].reshape(group_count, PROMPT, heads_here, HEAD)

    def to_cont(values):
        return values[prompt_rows:].reshape(cont_count, CONT_LEN, heads_here, HEAD)

    def rows_of(full_rows):
        prompt_share = lax.dynamic_slice_in_dim(
            full_rows[:prompt_rows], tensor_rank * share_prompt, share_prompt, 0
        )
        cont_share = lax.dynamic_slice_in_dim(
            full_rows[prompt_rows:], tensor_rank * share_cont, share_cont, 0
        )
        return jnp.concatenate([prompt_share, cont_share])

    def pair_up(own_table, partner_table):
        lower = jnp.where(parity == 0, own_table, partner_table)
        upper_half = jnp.where(parity == 0, partner_table, own_table)
        return jnp.concatenate([lower, upper_half])

    def split_pair(pair_grads):
        lower = pair_grads[:group_count]
        upper_half = pair_grads[group_count:]
        return (
            jnp.where(parity == 0, lower, upper_half),
            jnp.where(parity == 0, upper_half, lower),
        )

    def cont_sets(pair_k, pair_v, key_cont, value_cont):
        keys_in = gather_groups(pick_low, pair_k)
        values_in = gather_groups(pick_low, pair_v)
        if key_cont is not None:
            keys_in = jnp.concatenate([keys_in, key_cont], axis=1)
            values_in = jnp.concatenate([values_in, value_cont], axis=1)
        return (keys_in, values_in)

    def attention_fwd(query_all, own_k, own_v, pair_k, pair_v, key_cont, value_cont, with_bias):
        q_prompt = to_prompt(query_all)
        q_cont = to_cont(query_all)
        outputs, logsums, kept_sets = ([], [], [])
        for block_idx in range(block_count):
            row_start = block_idx * block_rows
            pos_bias, allowed = prompt_geo[block_idx] if with_bias else (None, None)
            mixture, logsum = attend_fwd(
                q_prompt[0:1, row_start : row_start + block_rows],
                own_k,
                own_v,
                pos_bias,
                allowed,
                factor,
            )
            outputs.append(mixture.reshape(block_rows, head_cols))
            logsums.append(logsum)
        keys_in, values_in = cont_sets(pair_k, pair_v, key_cont, value_cont)
        kept_sets.append((keys_in, values_in))
        pos_bias = cont_bias if with_bias else None
        allowed = cont_allowed[0] if with_bias else None
        mixture, logsum = attend_fwd(q_cont, keys_in, values_in, pos_bias, allowed, factor)
        outputs.append(mixture.reshape(cont_rows, head_cols))
        logsums.append(logsum)
        mixed = jnp.concatenate(outputs).astype(jnp.bfloat16)
        return (mixed, logsums, None)

    def attention_back(
        query_all,
        own_k,
        own_v,
        pair_k,
        pair_v,
        key_cont,
        value_cont,
        with_bias,
        logsums,
        grad_mixed,
    ):
        q_prompt = to_prompt(query_all)
        q_cont = to_cont(query_all)
        g_prompt = to_prompt(grad_mixed)
        g_cont = to_cont(grad_mixed)
        key_len = pair_k.shape[1]
        grad_own_k = jnp.zeros(own_k.shape, jnp.float32)
        grad_own_v = jnp.zeros(own_v.shape, jnp.float32)
        grad_bias = jnp.zeros((heads_here, dist_count), jnp.float32)
        query_parts, key_parts, value_parts = ([], [], [])
        position = 0
        for block_idx in range(block_count):
            row_start = block_idx * block_rows
            pos_bias, allowed = prompt_geo[block_idx] if with_bias else (None, None)
            grad_query, grad_keys, grad_values, grad_scores = attend_back(
                q_prompt[0:1, row_start : row_start + block_rows],
                own_k,
                own_v,
                pos_bias,
                allowed,
                factor,
                logsums[position],
                g_prompt[0:1, row_start : row_start + block_rows],
            )
            position += 1
            query_parts.append(grad_query.reshape(block_rows, head_cols))
            grad_own_k = grad_own_k.at[0].add(grad_keys[0])
            grad_own_v = grad_own_v.at[0].add(grad_values[0])
            if with_bias:
                grad_bias = grad_bias + skew_grad(
                    grad_scores, row_start, block_rows, PROMPT, dist_count
                )
        keys_in, values_in = cont_sets(pair_k, pair_v, key_cont, value_cont)
        pos_bias = cont_bias if with_bias else None
        allowed = cont_allowed[0] if with_bias else None
        grad_query, grad_keys, grad_values, grad_scores = attend_back(
            q_cont, keys_in, values_in, pos_bias, allowed, factor, logsums[position], g_cont
        )
        position += 1
        query_parts.append(grad_query.reshape(cont_rows, head_cols))
        grad_pair_k = spread_groups(pick_full, grad_keys[:, :key_len])
        grad_pair_v = spread_groups(pick_full, grad_values[:, :key_len])
        if key_cont is not None:
            key_parts.append(grad_keys[:, key_len:].reshape(cont_rows, head_cols))
            value_parts.append(grad_values[:, key_len:].reshape(cont_rows, head_cols))
        if with_bias:
            grad_bias = grad_bias + skew_grad(grad_scores, PROMPT, CONT_LEN, dist_count, dist_count)
        return (
            jnp.concatenate(query_parts),
            grad_own_k,
            grad_own_v,
            grad_pair_k,
            grad_pair_v,
            key_parts,
            value_parts,
            grad_bias,
        )

    stream = jnp.concatenate([x_prompt, x_cont]).astype(jnp.float32)
    normed_self = rms_norm(stream, gain_self).astype(jnp.bfloat16)
    query_s = project(normed_self, w_q).astype(jnp.bfloat16)
    key_s = project(normed_self, w_k).astype(jnp.bfloat16)
    value_s = project(normed_self, w_v).astype(jnp.bfloat16)
    cross_keys = (
        project(enc_out, c_k).astype(jnp.bfloat16).reshape(group_count, ENC_LEN, heads_here, HEAD)
    )
    cross_values = (
        project(enc_out, c_v).astype(jnp.bfloat16).reshape(group_count, ENC_LEN, heads_here, HEAD)
    )
    own_kp = to_prompt(key_s)
    own_vp = to_prompt(value_s)
    far_kp, far_vp, far_ck, far_cv = partner((own_kp, own_vp, cross_keys, cross_values), "dp", 0)
    pair_kp = pair_up(own_kp, far_kp)
    pair_vp = pair_up(own_vp, far_vp)
    pair_ck = pair_up(cross_keys, far_ck)
    pair_cv = pair_up(cross_values, far_cv)
    mixed_self, logsum_self, kept_self = attention_fwd(
        query_s, own_kp, own_vp, pair_kp, pair_vp, to_cont(key_s), to_cont(value_s), True
    )
    after_self = stream + lax.psum(project(mixed_self, w_o), "tensor")
    normed_cross = rms_norm(after_self, gain_cross).astype(jnp.bfloat16)
    query_c = project(normed_cross, c_q).astype(jnp.bfloat16)
    mixed_cross, logsum_cross, kept_cross = attention_fwd(
        query_c, cross_keys, cross_values, pair_ck, pair_cv, None, None, False
    )
    cross_part = project(mixed_cross, c_o)
    cross_prompt_share, cross_cont_share = (
        lax.psum_scatter(cross_part[:prompt_rows], "tensor", scatter_dimension=0, tiled=True),
        lax.psum_scatter(cross_part[prompt_rows:], "tensor", scatter_dimension=0, tiled=True),
    )
    self_share = rows_of(after_self)
    mid_share = self_share + jnp.concatenate([cross_prompt_share, cross_cont_share])
    normed_share = rms_norm(mid_share, gain_ffn).astype(jnp.bfloat16)
    normed_prompt, normed_cont = (
        lax.all_gather(normed_share[:share_prompt], "tensor", axis=0, tiled=True),
        lax.all_gather(normed_share[share_prompt:], "tensor", axis=0, tiled=True),
    )
    normed_ffn = jnp.concatenate([normed_prompt, normed_cont])
    gate_pre = project(normed_ffn, w_gate)
    upper = project(normed_ffn, w_up)
    hidden = (jax.nn.gelu(gate_pre, approximate=True) * upper).astype(jnp.bfloat16)
    ffn_part = project(hidden, w_down)
    ffn_prompt_share, ffn_cont_share = (
        lax.psum_scatter(
            ffn_part[:prompt_rows].astype(jnp.bfloat16), "tensor", scatter_dimension=0, tiled=True
        ).astype(jnp.float32),
        lax.psum_scatter(
            ffn_part[prompt_rows:].astype(jnp.bfloat16), "tensor", scatter_dimension=0, tiled=True
        ).astype(jnp.float32),
    )
    out_share = mid_share + jnp.concatenate([ffn_prompt_share, ffn_cont_share])
    valid_share = lax.dynamic_slice_in_dim(valid, tensor_rank * share_cont, share_cont, 0).astype(
        jnp.float32
    )[:, None]
    deviation = out_share[share_prompt:] - teacher.astype(jnp.float32)
    loss_part = jnp.sum(valid_share * deviation * deviation)
    grad_share3 = jnp.concatenate(
        [
            cot_prompt.astype(jnp.float32),
            cot_cont.astype(jnp.float32) + 2.0 * valid_share * deviation / token_count,
        ]
    )
    low_share3 = grad_share3.astype(jnp.bfloat16)
    grad_prompt3, grad_cont3 = (
        lax.all_gather(low_share3[:share_prompt], "tensor", axis=0, tiled=True),
        lax.all_gather(low_share3[share_prompt:], "tensor", axis=0, tiled=True),
    )
    grad_low3 = jnp.concatenate([grad_prompt3, grad_cont3])
    grad_w_down = weight_grad(hidden, grad_low3)
    grad_hidden = lax.optimization_barrier(
        input_grad(grad_low3, w_down).astype(jnp.bfloat16)
    ).astype(jnp.float32)
    ignored, gelu_pull = jax.vjp(
        lambda first_in, second_in: jax.nn.gelu(first_in, approximate=True) * second_in,
        gate_pre,
        upper,
    )
    grad_gate, grad_upper = gelu_pull(grad_hidden)
    grad_gate = grad_gate.astype(jnp.bfloat16)
    grad_upper = grad_upper.astype(jnp.bfloat16)
    grad_w_gate = weight_grad(normed_ffn, grad_gate)
    grad_w_up = weight_grad(normed_ffn, grad_upper)
    ffn_in_part = input_grad(grad_gate, w_gate) + input_grad(grad_upper, w_up)
    dn3_prompt, dn3_cont = (
        lax.psum_scatter(ffn_in_part[:prompt_rows], "tensor", scatter_dimension=0, tiled=True),
        lax.psum_scatter(ffn_in_part[prompt_rows:], "tensor", scatter_dimension=0, tiled=True),
    )
    ignored, norm_pull3 = jax.vjp(rms_norm, mid_share, gain_ffn)
    back_three, gain_ffn_part = norm_pull3(jnp.concatenate([dn3_prompt, dn3_cont]))
    grad_share2 = grad_share3 + back_three
    low_share2 = grad_share2.astype(jnp.bfloat16)
    grad_prompt2, grad_cont2 = (
        lax.all_gather(low_share2[:share_prompt], "tensor", axis=0, tiled=True),
        lax.all_gather(low_share2[share_prompt:], "tensor", axis=0, tiled=True),
    )
    grad_low2 = jnp.concatenate([grad_prompt2, grad_cont2])
    grad_c_o = weight_grad(mixed_cross, grad_low2)
    grad_mix_cross = input_grad(grad_low2, c_o).astype(jnp.bfloat16)
    (
        grad_cq,
        own_ck_grad,
        own_cv_grad,
        pair_ck_grad,
        pair_cv_grad,
        ignored_keys,
        ignored_values,
        ignored_bias,
    ) = attention_back(
        query_c,
        cross_keys,
        cross_values,
        pair_ck,
        pair_cv,
        None,
        None,
        False,
        logsum_cross,
        grad_mix_cross,
    )
    grad_cq = grad_cq.astype(jnp.bfloat16)
    grad_c_q = weight_grad(normed_cross, grad_cq)
    cross_in_part = input_grad(grad_cq, c_q)
    dn2_prompt, dn2_cont = (
        lax.psum_scatter(cross_in_part[:prompt_rows], "tensor", scatter_dimension=0, tiled=True),
        lax.psum_scatter(cross_in_part[prompt_rows:], "tensor", scatter_dimension=0, tiled=True),
    )
    ignored, norm_pull2 = jax.vjp(rms_norm, self_share, gain_cross)
    back_two, gain_cross_part = norm_pull2(jnp.concatenate([dn2_prompt, dn2_cont]))
    grad_share1 = grad_share2 + back_two
    low_share1 = grad_share1.astype(jnp.bfloat16)
    grad_prompt1, grad_cont1 = (
        lax.all_gather(low_share1[:share_prompt], "tensor", axis=0, tiled=True),
        lax.all_gather(low_share1[share_prompt:], "tensor", axis=0, tiled=True),
    )
    grad_low1 = jnp.concatenate([grad_prompt1, grad_cont1])
    grad_w_o = weight_grad(mixed_self, grad_low1)
    grad_mix_self = input_grad(grad_low1, w_o).astype(jnp.bfloat16)
    (
        grad_qs,
        own_kp_grad,
        own_vp_grad,
        pair_kp_grad,
        pair_vp_grad,
        key_parts,
        value_parts,
        grad_bias,
    ) = attention_back(
        query_s,
        own_kp,
        own_vp,
        pair_kp,
        pair_vp,
        to_cont(key_s),
        to_cont(value_s),
        True,
        logsum_self,
        grad_mix_self,
    )
    mine_kp, lent_kp = split_pair(pair_kp_grad)
    mine_vp, lent_vp = split_pair(pair_vp_grad)
    mine_ck, lent_ck = split_pair(pair_ck_grad)
    mine_cv, lent_cv = split_pair(pair_cv_grad)
    back_kp, back_vp, back_ck, back_cv = (
        partner(lent_kp.astype(jnp.bfloat16), "dp", 0).astype(lent_kp.dtype),
        partner(lent_vp.astype(jnp.bfloat16), "dp", 0).astype(lent_vp.dtype),
        partner(lent_ck.astype(jnp.bfloat16), "dp", 0).astype(lent_ck.dtype),
        partner(lent_cv.astype(jnp.bfloat16), "dp", 0).astype(lent_cv.dtype),
    )
    total_kp = own_kp_grad + mine_kp + back_kp
    total_vp = own_vp_grad + mine_vp + back_vp
    total_ck = own_ck_grad + mine_ck + back_ck
    total_cv = own_cv_grad + mine_cv + back_cv
    grad_qs = grad_qs.astype(jnp.bfloat16)
    grad_ks = jnp.concatenate([total_kp.reshape(prompt_rows, head_cols)] + key_parts).astype(
        jnp.bfloat16
    )
    grad_vs = jnp.concatenate([total_vp.reshape(prompt_rows, head_cols)] + value_parts).astype(
        jnp.bfloat16
    )
    grad_ck = total_ck.reshape(-1, head_cols).astype(jnp.bfloat16)
    grad_cv = total_cv.reshape(-1, head_cols).astype(jnp.bfloat16)
    grad_w_q = weight_grad(normed_self, grad_qs)
    grad_w_k = weight_grad(normed_self, grad_ks)
    grad_w_v = weight_grad(normed_self, grad_vs)
    grad_c_k = weight_grad(enc_out, grad_ck)
    grad_c_v = weight_grad(enc_out, grad_cv)
    self_in_part = input_grad(grad_qs, w_q) + input_grad(grad_ks, w_k) + input_grad(grad_vs, w_v)
    enc_part = input_grad(grad_ck, c_k) + input_grad(grad_cv, c_v)
    grad_normed1, grad_enc, gain_cross_sum, gain_ffn_sum, loss_sum = (
        lax.psum(self_in_part.astype(jnp.bfloat16), "tensor").astype(jnp.float32),
        lax.psum(enc_part.astype(jnp.bfloat16), "tensor").astype(jnp.float32),
        lax.psum(gain_cross_part.astype(jnp.bfloat16), "tensor").astype(jnp.float32),
        lax.psum(gain_ffn_part.astype(jnp.bfloat16), "tensor").astype(jnp.float32),
        lax.psum(loss_part.astype(jnp.bfloat16), "tensor").astype(jnp.float32),
    )
    ignored, norm_pull1 = jax.vjp(rms_norm, stream, gain_self)
    back_one, grad_gain_self = norm_pull1(grad_normed1)
    grad_x_share = grad_share1 + rows_of(back_one)
    grad_table = jnp.dot(bucket_hot.T, grad_bias.T, precision=lax.Precision.HIGHEST)
    summed = lax.psum(
        (
            grad_gain_self,
            gain_cross_sum,
            gain_ffn_sum,
            grad_table,
            grad_w_q,
            grad_w_k,
            grad_w_v,
            grad_w_o,
            grad_c_q,
            grad_c_k,
            grad_c_v,
            grad_c_o,
            grad_w_gate,
            grad_w_up,
            grad_w_down,
            loss_sum,
        ),
        "dp",
    )
    return (
        out_share[:share_prompt].astype(jnp.bfloat16),
        out_share[share_prompt:].astype(jnp.bfloat16),
        grad_x_share[:share_prompt],
        grad_x_share[share_prompt:],
        grad_enc,
        summed[0],
        summed[1],
        summed[2],
        summed[3],
        summed[4],
        summed[5],
        summed[6],
        summed[7],
        summed[8],
        summed[9],
        summed[10],
        summed[11],
        summed[12],
        summed[13],
        summed[14],
        summed[15] / token_count,
    )


def solution(mesh):
    placed = (
        P("dp", None),
        P("dp", None),
        P("dp", None),
        P(("dp", "tensor"), None),
        P(("dp", "tensor"), None),
        P(("dp", "tensor"), None),
        P("dp"),
        P("dp"),
        P(),
        P(),
        P(),
        P(),
        P(None, "tensor"),
        P(None, "tensor"),
        P(None, "tensor"),
        P(None, "tensor"),
        P("tensor", None),
        P(None, "tensor"),
        P(None, "tensor"),
        P(None, "tensor"),
        P("tensor", None),
        P(None, "tensor"),
        P(None, "tensor"),
        P("tensor", None),
    )
    return jax.shard_map(
        on_device,
        mesh=mesh,
        in_specs=placed,
        out_specs=(
            P(("dp", "tensor"), None),
            P(("dp", "tensor"), None),
            P(("dp", "tensor"), None),
            P(("dp", "tensor"), None),
            P("dp", None),
            P(),
            P(),
            P(),
            P(None, "tensor"),
            P(None, "tensor"),
            P(None, "tensor"),
            P(None, "tensor"),
            P("tensor", None),
            P(None, "tensor"),
            P(None, "tensor"),
            P(None, "tensor"),
            P("tensor", None),
            P(None, "tensor"),
            P(None, "tensor"),
            P("tensor", None),
            P(),
        ),
        check_vma=False,
    )
```

profile of v0, /device:TPU:0, one launch (start us, length us, event | category | flops | bytes accessed | tf_op | source)
XLA Modules:
  0.0 1407.1 jit_solution(973452617765496951)
XLA Ops:
  82.4 19.9 %copy.318 = f32[1,3,512,1536]{3,1,2,0:T(4,128)S(1)} copy(f32[1,3,512,1536]{3,2,1,0:T(8,128)S(1)} %broadcast_bitcast_fusion.1) | data formatting | bytes 18874368
  121.5 15.5 %reshape.1025 = f32[3,512,1535]{2,1,0:T(8,128)} reshape(f32[2357760]{0:T(1024)} %reshape.1114) | data formatting | bytes 18862080 | tf_op jit(solution)/shard_map/reshape | solution.py:56
  139.0 20.3 %copy.319 = f32[1,3,512,1536]{3,1,2,0:T(4,128)S(1)} copy(f32[1,3,512,1536]{3,2,1,0:T(8,128)S(1)} %broadcast_bitcast_fusion) | data formatting | bytes 18874368
  165.1 13.3 reshape.1112
  178.4 15.7 %reshape.1028 = f32[3,512,1535]{2,1,0:T(8,128)} reshape(f32[2357760]{0:T(1024)} %reshape.1112) | data formatting | bytes 18862080 | tf_op jit(solution)/shard_map/reshape | solution.py:56
  242.7 162.2 %all-reduce.17.cloned.1.call-done = f32[1536,768]{1,0:T(8,128)} async-done(((f32[1536,768]{1,0:T(8,128)}), f32[1536,768]{1,0:T(8,128)}) %all-reduce.17.cloned.1.call-update) | async-done | bytes 4718608 | tf_op jit(solution)/shard_map/psum | solution.py:340
  434.5 26.8 %reduce-scatter.11.cloned.1.call-done = f32[128,768]{1,0:T(8,128)} async-done(((f32[512,768]{1,0:T(8,128)}), f32[128,768]{1,0:T(8,128)}) %reduce-scatter.11.cloned.1.call-update) | async-done | bytes 393232 | tf_op jit(solution)/shard_map/reduce_scatter | solution.py:349
  461.3 61.6 %reduce-scatter.9.cloned.1.call-done = f32[256,768]{1,0:T(8,128)} async-done(((f32[1024,768]{1,0:T(8,128)}), f32[256,768]{1,0:T(8,128)}) %reduce-scatter.9.cloned.1.call-update) | async-done | bytes 786448 | tf_op jit(solution)/shard_map/reduce_scatter | solution.py:348
  528.4 24.9 %all_gather.25 = bf16[512,768]{1,0:T(8,128)(2,1)} all-gather(bf16[128,768]{1,0:T(8,128)(2,1)S(1)} %slice.509), channel_id=1, replica_groups=mesh['dp'=8,'tensor'=4] {'tensor'}, dimensions={0}, use_global_device_ids=true | all-gather | bytes 983040 | tf_op jit(solution)/shard_map/all_gather | solution.py:356
  553.3 17.7 %all-gather.5.cloned.1.call-done = bf16[1024,768]{1,0:T(8,128)(2,1)} async-done(((bf16[256,768]{1,0:T(8,128)(2,1)}), bf16[1024,768]{1,0:T(8,128)(2,1)}) %all-gather.5.cloned.1.call-update) | async-done | bytes 1572880 | tf_op jit(solution)/shard_map/all_gather | solution.py:355
  585.9 14.5 %psum.162 = f32[]{:T(128)} all-reduce(f32[]{:T(128)} %convert_reduce_fusion.1), channel_id=1, replica_groups=mesh['dp'=8,'tensor'=4] {'dp'}, use_global_device_ids=true, to_apply=%region_21.23 | all-reduce | flops 1 | bytes 8 | tf_op jit(solution)/shard_map/psum | solution.py:165
  604.6 37.7 %reduce-scatter.13.cloned.1.call-done = bf16[256,768]{1,0:T(8,128)(2,1)} async-done(((bf16[1024,768]{1,0:T(8,128)(2,1)}), bf16[256,768]{1,0:T(8,128)(2,1)}) %reduce-scatter.13.cloned.1.call-update) | async-done | bytes 393232 | tf_op jit(solution)/shard_map/reduce_scatter | solution.py:364
  649.0 25.0 %all_gather.27 = bf16[512,768]{1,0:T(8,128)(2,1)} all-gather(bf16[128,768]{1,0:T(8,128)(2,1)S(1)} %slice.515), channel_id=1, replica_groups=mesh['dp'=8,'tensor'=4] {'tensor'}, dimensions={0}, use_global_device_ids=true | all-gather | bytes 983040 | tf_op jit(solution)/shard_map/all_gather | solution.py:386
  674.0 17.2 %all-gather.7.cloned.1.call-done = bf16[1024,768]{1,0:T(8,128)(2,1)} async-done(((bf16[256,768]{1,0:T(8,128)(2,1)}), bf16[1024,768]{1,0:T(8,128)(2,1)}) %all-gather.7.cloned.1.call-update) | async-done | bytes 1572880 | tf_op jit(solution)/shard_map/all_gather | solution.py:385
  709.4 57.1 %reduce-scatter.17.cloned.1.call-done = f32[256,768]{1,0:T(8,128)} async-done(((f32[1024,768]{1,0:T(8,128)}), f32[256,768]{1,0:T(8,128)}) %reduce-scatter.17.cloned.1.call-update) | async-done | bytes 786448 | tf_op jit(solution)/shard_map/reduce_scatter | solution.py:405
  768.6 36.2 %reduce-scatter.19.cloned.1.call-done = f32[128,768]{1,0:T(8,128)} async-done(((f32[512,768]{1,0:T(8,128)}), f32[128,768]{1,0:T(8,128)}) %reduce-scatter.19.cloned.1.call-update) | async-done | bytes 393232 | tf_op jit(solution)/shard_map/reduce_scatter | solution.py:406
  816.4 27.6 %all_gather.29 = bf16[512,768]{1,0:T(8,128)(2,1)S(1)} all-gather(bf16[128,768]{1,0:T(8,128)(2,1)S(1)} %slice.519), channel_id=1, replica_groups=mesh['dp'=8,'tensor'=4] {'tensor'}, dimensions={0}, use_global_device_ids=true | all-gather | bytes 983040 | tf_op jit(solution)/shard_map/all_gather | solution.py:414
  844.0 14.2 %all-gather.9.cloned.1.call-done = bf16[1024,768]{1,0:T(8,128)(2,1)} async-done(((bf16[256,768]{1,0:T(8,128)(2,1)}), bf16[1024,768]{1,0:T(8,128)(2,1)}) %all-gather.9.cloned.1.call-update) | async-done | bytes 1572880 | tf_op jit(solution)/shard_map/all_gather | solution.py:413
  916.0 23.5 %reduce-scatter.21.cloned.1.call-done = f32[256,768]{1,0:T(8,128)} async-done(((f32[1024,768]{1,0:T(8,128)}), f32[256,768]{1,0:T(8,128)}) %reduce-scatter.21.cloned.1.call-update) | async-done | bytes 786448 | tf_op jit(solution)/shard_map/reduce_scatter | solution.py:444
  940.6 36.9 %reduce-scatter.23.cloned.1.call-done = f32[128,768]{1,0:T(8,128)} async-done(((f32[512,768]{1,0:T(8,128)}), f32[128,768]{1,0:T(8,128)}) %reduce-scatter.23.cloned.1.call-update) | async-done | bytes 393232 | tf_op jit(solution)/shard_map/reduce_scatter | solution.py:445
  1005.7 28.0 %all_gather.31 = bf16[512,768]{1,0:T(8,128)(2,1)S(1)} all-gather(bf16[128,768]{1,0:T(8,128)(2,1)S(1)} %slice.527), channel_id=1, replica_groups=mesh['dp'=8,'tensor'=4] {'tensor'}, dimensions={0}, use_global_device_ids=true | all-gather | bytes 983040 | tf_op jit(solution)/shard_map/all_gather | solution.py:453
  1193.7 47.1 %all-reduce.21.cloned.1.call-done = (bf16[1536,768]{1,0:T(8,128)(2,1)}, bf16[512,768]{1,0:T(8,128)(2,1)}) async-done(((bf16[1536,768]{1,0:T(8,128)(2,1)}, bf16[512,768]{1,0:T(8,128)(2,1)}), (bf16[1536,768]{1,0:T(8,128)(2,1)}, bf16[512,768]{1,0:T(8,128)(2,1)})) %all-reduce.21.cloned.1.call-update) | async-done | bytes 3145744 | tf_op jit(solution)/shard_map/psum | solution.py:510
  1252.0 26.9 %all-reduce.9 = (f32[768]{0:T(1024)}, f32[768]{0:T(1024)}, f32[768]{0:T(1024)}, f32[32,3]{0,1:T(4,128)}, f32[]{:T(128)}) all-reduce(f32[768]{0:T(1024)S(1)} %get-tuple-element.118, bf16[768]{0:T(1024)(128)(2,1)S(1)} %copy-done.207, bf16[768]{0:T(1024)(128)(2,1)S(1)} %copy-done.208, ...), channel_id=1, replica_groups=mesh['dp'=8,'tensor'=4] {'dp'}, use_global_device_ids=true, to_apply=%region_39.41 | all-reduce | flops 2401 | bytes 16134 | tf_op jit(solution)/shard_map/psum | solution.py:520
  1280.2 105.5 %all-reduce.19.cloned.1.call-done = (f32[768,192]{0,1:T(8,128)}, f32[768,192]{0,1:T(8,128)}, f32[768,192]{0,1:T(8,128)}, f32[192,768]{1,0:T(8,128)}, f32[768,192...) async-done(((f32[768,192]{0,1:T(8,128)}, ...) | async-done | bytes 9437200 | tf_op jit(solution)/shard_map/psum | solution.py:520
  (795 shorter events, 512.1 us)
Async XLA Ops:
  7.2 567.1 %copy-start = (bf16[768,512]{1,0:T(8,128)(2,1)S(1)}, bf16[768,512]{1,0:T(8,128)(2,1)}, u32[]{:S(2)}) copy-start(bf16[768,512]{1,0:T(8,128)(2,1)} %param.64) | copy-start | bytes 2359300
  7.2 397.7 %all-reduce.17.cloned.1.call-start = ((), (), s32[]{:S(2)}) async-start(), calls=%async_computation.8 | async-start | bytes 9437184 | tf_op jit(solution)/shard_map/psum | solution.py:340
  13.0 200.1 %collective-permute-start.1 = (bf16[1,1024,3,64]{1,3,2,0:T(8,128)(2,1)S(1)}, bf16[1,1024,3,64]{1,3,2,0:T(8,128)(2,1)}, u32[]{:S(2)}, u32[]{:S(2)}) collective-permute-start(bf16[1,1024,3,64]{1,3,2,0:T(8,128)(2,1)S(1)} %bitcast.346), channel_id=1, source_target_pairs={{0,4},{4,0},{8,12},{12,8},{16,20},{20,16},{24,28},{28,24},{1,5},{5... | collective-permute-start | bytes 1179656 | tf_op jit(solution)/shard_map/ppermute | solution.py:23
  15.3 197.8 %collective-permute-start = (bf16[1,1024,3,64]{1,3,2,0:T(8,128)(2,1)S(1)}, bf16[1,1024,3,64]{1,3,2,0:T(8,128)(2,1)}, u32[]{:S(2)}, u32[]{:S(2)}) collective-permute-start(bf16[1,1024,3,64]{1,3,2,0:T(8,128)(2,1)S(1)} %bitcast.360), channel_id=1, source_target_pairs={{0,4},{4,0},{8,12},{12,8},{16,20},{20,16},{24,28},{28,24},{1,5},{5... | collective-permute-start | bytes 1179656 | tf_op jit(solution)/shard_map/ppermute | solution.py:23
  230.4 230.9 %reduce-scatter.11.cloned.1.call-start = ((), (), s32[]{:S(2)}) async-start(), calls=%async_computation.10 | async-start | bytes 1966080 | tf_op jit(solution)/shard_map/reduce_scatter | solution.py:349
  233.2 2.3 collective-permute-start.3
  235.1 1.8 collective-permute-start.2
  426.8 96.1 %reduce-scatter.9.cloned.1.call-start = ((), (), s32[]{:S(2)}) async-start(), calls=%async_computation.9 | async-start | bytes 3932160 | tf_op jit(solution)/shard_map/reduce_scatter | solution.py:348
  430.6 140.4 %all-gather.5.cloned.1.call-start = ((), (), s32[]{:S(2)}) async-start(), calls=%async_computation.11 | async-start | bytes 1966080 | tf_op jit(solution)/shard_map/all_gather | solution.py:355
  527.4 77.2 %reduce-scatter.15.cloned.1.call-start = ((), (), s32[]{:S(2)}) async-start(), calls=%async_computation.13 | async-start | bytes 983040 | tf_op jit(solution)/shard_map/reduce_scatter | solution.py:367
  581.8 60.6 %reduce-scatter.13.cloned.1.call-start = ((), (), s32[]{:S(2)}) async-start(), calls=%async_computation.12 | async-start | bytes 1966080 | tf_op jit(solution)/shard_map/reduce_scatter | solution.py:364
  584.6 106.6 %all-gather.7.cloned.1.call-start = ((), (), s32[]{:S(2)}) async-start(), calls=%async_computation.14 | async-start | bytes 1966080 | tf_op jit(solution)/shard_map/all_gather | solution.py:385
  648.0 118.6 %reduce-scatter.17.cloned.1.call-start = ((), (), s32[]{:S(2)}) async-start(), calls=%async_computation.15 | async-start | bytes 3932160 | tf_op jit(solution)/shard_map/reduce_scatter | solution.py:405
  706.6 98.1 %reduce-scatter.19.cloned.1.call-start = ((), (), s32[]{:S(2)}) async-start(), calls=%async_computation.16 | async-start | bytes 1966080 | tf_op jit(solution)/shard_map/reduce_scatter | solution.py:406
  709.4 148.9 %all-gather.9.cloned.1.call-start = ((), (), s32[]{:S(2)}) async-start(), calls=%async_computation.17 | async-start | bytes 1966080 | tf_op jit(solution)/shard_map/all_gather | solution.py:413
  813.2 126.2 %reduce-scatter.21.cloned.1.call-start = ((), (), s32[]{:S(2)}) async-start(), calls=%async_computation.18 | async-start | bytes 3932160 | tf_op jit(solution)/shard_map/reduce_scatter | solution.py:444
  879.2 98.4 %reduce-scatter.23.cloned.1.call-start = ((), (), s32[]{:S(2)}) async-start(), calls=%async_computation.19 | async-start | bytes 1966080 | tf_op jit(solution)/shard_map/reduce_scatter | solution.py:445
  897.6 136.0 %all-gather.11.cloned.1.call-start = ((), (), s32[]{:S(2)}) async-start(), calls=%async_computation.20 | async-start | bytes 1966080 | tf_op jit(solution)/shard_map/all_gather | solution.py:452
  905.2 81.6 %collective-permute-start.7 = (bf16[1,512,3,64]{1,0,3,2:T(2,128)(2,1)}, bf16[1,512,3,64]{1,0,3,2:T(2,128)(2,1)}, u32[]{:S(2)}, u32[]{:S(2)}) collective-permute-start(bf16[1,512,3,64]{1,0,3,2:T(2,128)(2,1)} %fusion.135), channel_id=1, source_target_pairs={{0,4},{4,0},{8,12},{12,8},{16,20},{20,16},{24,28},{28,24},{1,5},{5... | collective-permute-start | bytes 589832 | tf_op jit(solution)/shard_map/ppermute | solution.py:23
  984.3 256.5 %all-reduce.21.cloned.1.call-start = ((), (), s32[]{:S(2)}) async-start(), calls=%async_computation.22 | async-start | bytes 6291456 | tf_op jit(solution)/shard_map/psum | solution.py:510
  985.0 3.8 collective-permute-start.6
  1069.9 46.6 %collective-permute-start.5 = (bf16[1,1024,3,64]{1,3,2,0:T(8,128)(2,1)}, bf16[1,1024,3,64]{1,3,2,0:T(8,128)(2,1)}, u32[]{:S(2)}, u32[]{:S(2)}) collective-permute-start(bf16[1,1024,3,64]{1,3,2,0:T(8,128)(2,1)} %select_convert_fusion), channel_id=1, source_target_pairs={{0,4},{4,0},{8,12},{12,8},{16,20},{20,16},{24,28},{28,24},{1,5},{5... | collective-permute-start | bytes 1179656 | tf_op jit(solution)/shard_map/ppermute | solution.py:23
  1078.3 35.2 %collective-permute-start.4 = (bf16[1,1024,3,64]{1,3,2,0:T(8,128)(2,1)}, bf16[1,1024,3,64]{1,3,2,0:T(8,128)(2,1)}, u32[]{:S(2)}, u32[]{:S(2)}) collective-permute-start(bf16[1,1024,3,64]{1,3,2,0:T(8,128)(2,1)} %select_convert_fusion.1), channel_id=1, source_target_pairs={{0,4},{4,0},{8,12},{12,8},{16,20},{20,16},{24,28},{28,24},{1,5},{5... | collective-permute-start | bytes 1179656 | tf_op jit(solution)/shard_map/ppermute | solution.py:23
  1121.2 264.5 %all-reduce.19.cloned.1.call-start = ((), (), s32[]{:S(2)}) async-start(), calls=%async_computation.21 | async-start | bytes 18874368 | tf_op jit(solution)/shard_map/psum | solution.py:520
  (228 other events, 2927.3 us)
Sparse Core Ops, SparseCore 0:
  230.5 174.3 all-reduce.16
  426.9 34.3 reduce-scatter.10
  463.6 59.2 reduce-scatter.8
  527.5 43.4 all-gather.4
  581.9 22.6 reduce-scatter.14
  607.4 34.9 reduce-scatter.12
  648.1 43.0 all-gather.6
  706.8 59.7 reduce-scatter.16
  769.4 35.3 reduce-scatter.18
  813.3 44.8 all-gather.8
  879.3 60.1 reduce-scatter.20
  942.2 35.3 reduce-scatter.22
  984.4 48.2 all-gather.10
  1121.3 119.4 all-reduce.20
  1247.5 138.1 all-reduce.18
where the time goes:
time: 1410 us
  waiting for transfers between devices  647 us (46%)
  local copies, waits for them, and re-layouts  314 us (22%)
  blocking collectives  158 us (11%)
  matrix products  146 us (10%)
  other arithmetic  118 us (8%)
  between operations  19.9 us (1%)
    psum x1, waiting for transfers between devices, on_device(): after_self = stream + lax.psum(project(mixed_self, w_o), 'tensor')  162 us
    unnamed x489, local copies, waits for them, and re-layouts  156 us
    psum x1, waiting for transfers between devices, on_device(): lax.psum((grad_gain_self, gain_cross_sum, gain_ffn_sum, grad_table, grad_...  105 us
    reduce_scatter x1, waiting for transfers between devices, on_device(): lax.psum_scatter(cross_part[:prompt_rows], 'tensor', scatter_dimension=0,...  61.6 us
    reduce_scatter x1, waiting for transfers between devices, on_device(): lax.psum_scatter(ffn_in_part[:prompt_rows], 'tensor', scatter_dimension=0...  57.1 us
    psum x1, waiting for transfers between devices, on_device(): lax.psum(self_in_part.astype(jnp.bfloat16), 'tensor').astype(jnp.float32)  47.1 us
    reduce_scatter x1, waiting for transfers between devices, on_device(): lax.psum_scatter(ffn_part[:prompt_rows].astype(jnp.bfloat16), 'tensor', s...  37.7 us
    reduce_scatter x1, waiting for transfers between devices, on_device(): lax.psum_scatter(cross_in_part[prompt_rows:], 'tensor', scatter_dimension...  36.9 us
  transfers between devices with their start and end apart: 23, of which 15 were waited for; matrix products, arithmetic and copies ran while one was open for 29% of the time, Pallas kernels for 0%

commit v1 on v0

v1 whole, which is shorter than its diff:
```python
import functools

import jax
import jax.numpy as jnp
from jax import lax
from jax.experimental import pallas as pl
from jax.experimental.pallas import tpu as pltpu
from jax.sharding import PartitionSpec as P

HEAD = 64
PROMPT = 1024
CONT_LEN = 128
ENC_LEN = 512
TILE = 128
DIST = PROMPT + CONT_LEN
LINE = DIST + 2 * TILE
SLAB = DIST + TILE

norm_eps = 1e-06
masked_value = -1e30
BF = jnp.bfloat16
F32 = jnp.float32
NT = (((1,), (1,)), ((), ()))
TN = (((0,), (0,)), ((), ()))
NN = (((1,), (0,)), ((), ()))


def mm(left, right, dims=NN):
    return lax.dot_general(left, right, dims, preferred_element_type=F32)


def from_ahead(block, step):
    count = lax.axis_size("tensor")
    return lax.ppermute(block, "tensor", [((i + step) % count, i) for i in range(count)])


def to_ahead(block, step):
    count = lax.axis_size("tensor")
    return lax.ppermute(block, "tensor", [(i, (i + step) % count) for i in range(count)])


def flip_bit(block, bit, axis="dp"):
    count = lax.axis_size(axis)
    return lax.ppermute(block, axis, [(i, i ^ (1 << bit)) for i in range(count)])


def bit_lists():
    count = lax.axis_size("dp")
    bits = count.bit_length() - 1
    up = list(range(1, bits))
    return (up, up[::-1])


def slice_order(bits):
    order = [0]
    for bit in bits + [0]:
        order = order + [entry ^ (1 << bit) for entry in order]
    return order


def spread(block, bits, axis):
    for bit in bits:
        block = jnp.concatenate([block, flip_bit(block, bit)], axis=axis)
    return block


def gather_weights(own):
    up, down = bit_lists()
    pieces = [own] + [from_ahead(own, step) for step in range(1, 4)]
    first = spread(jnp.concatenate(pieces[:2], axis=1), up, 3)
    second = spread(jnp.concatenate(pieces[2:], axis=1), down, 3)
    first_far = flip_bit(first, 0)
    second_far = flip_bit(second, 0)
    return jnp.concatenate(
        [
            jnp.concatenate([first, first_far], axis=3),
            jnp.concatenate([second, second_far], axis=3),
        ],
        axis=1,
    )


def fold(block, bit, axis):
    half = block.shape[axis] // 2
    low = lax.slice_in_dim(block, 0, half, axis=axis)
    high = lax.slice_in_dim(block, half, 2 * half, axis=axis)
    return (low.astype(F32) + flip_bit(high, bit).astype(F32)).astype(BF)


def reduce_grads(grads):
    up, down = bit_lists()
    first, second = grads[:, :2], grads[:, 2:]
    for bit in [0] + down:
        first = fold(first, bit, 3)
    for bit in [0] + up:
        second = fold(second, bit, 3)
    total = first[:, 0].astype(F32)
    for step, piece in ((1, first[:, 1]), (2, second[:, 0]), (3, second[:, 1])):
        total = total + to_ahead(piece, step).astype(F32)
    total = total.astype(BF)
    half = total.shape[-1] // 2
    left = spread(total[..., :half], up + [0], 2)
    right = spread(total[..., half:], down + [0], 2)
    return (left, right)


def slice_hot(order, parts, rows, rank):
    count = len(order)
    size = parts * count * rows
    place = jnp.arange(size)
    slot = place // rows % count
    table = sum(jnp.where(slot == index, entry, 0) for index, entry in enumerate(order))
    natural = place // (count * rows) * (count * rows) + (rank ^ table) * rows + place % rows
    return (natural[:, None] == jnp.arange(size)[None, :]).astype(BF)


def norm_scale(values):
    return lax.rsqrt(jnp.mean(values * values, axis=-1, keepdims=True) + norm_eps)


def rms_norm(values, weight):
    return values * norm_scale(values) * weight


def norm_back(values, weight, grad):
    scale = norm_scale(values)
    unit = values * scale
    weighted = grad * weight
    inner = jnp.mean(weighted * unit, axis=-1, keepdims=True)
    return (scale * (weighted - unit * inner), jnp.sum(grad * unit, axis=0))


def make_slab(line):
    wide = jnp.broadcast_to(line, (TILE, LINE))
    return pltpu.roll(wide, LINE - (TILE - 1), 1, stride=1, stride_axis=0)[:, :SLAB]


def head_mask(head, width, dtype):
    lane = lax.broadcasted_iota(jnp.int32, (1, width), 1)
    return (lane // HEAD == head).astype(dtype)


def prompt_fwd(line_ref, q_ref, k_ref, v_ref, o_ref, lse_ref, slab):
    head = pl.program_id(0)
    slab[...] = make_slab(line_ref[0])
    width = q_ref.shape[1]
    mask = head_mask(head, width, BF)
    mask_f = head_mask(head, width, F32)

    @pl.when(head == 0)
    def _():
        o_ref[...] = jnp.zeros_like(o_ref)
        lse_ref[...] = jnp.zeros_like(lse_ref)

    vm = v_ref[0:PROMPT, :] * mask
    block = 2 * TILE
    for idx in range(PROMPT // block):
        keys = block * (idx + 1)
        rows = pl.ds(idx * block, block)
        q = q_ref[rows, :] * mask
        s = mm(q, k_ref[0:keys, :], NT)
        start = PROMPT - block * idx
        s = s + jnp.concatenate(
            [slab[:, start : start + keys], slab[:, start - TILE : start - TILE + keys]], axis=0
        )
        top = jnp.max(s, axis=-1, keepdims=True)
        e = jnp.exp(s - top)
        total = jnp.sum(e, axis=-1, keepdims=True)
        o = mm(e.astype(BF), vm[0:keys, :]) / total
        o_ref[rows, :] = o_ref[rows, :] + o.astype(BF)
        lse_ref[rows, :] = lse_ref[rows, :] + (top + jnp.log(total)) * mask_f


def cont_rows(slot):
    return pl.ds(pl.multiple_of(slot * CONT_LEN, CONT_LEN), CONT_LEN)


def late_rows(slot):
    return pl.ds(pl.multiple_of(PROMPT + slot * CONT_LEN, CONT_LEN), CONT_LEN)


def cont_fwd(
    slot_ref, line_ref, ok_ref, q_ref, k_ref, v_ref, kf_ref, vf_ref, o_ref, lse_ref, slab
):
    head = pl.program_id(0)
    slab[...] = make_slab(line_ref[0])
    width = q_ref.shape[1]
    mask = head_mask(head, width, BF)
    mask_f = head_mask(head, width, F32)

    @pl.when(head == 0)
    def _():
        o_ref[...] = jnp.zeros_like(o_ref)
        lse_ref[...] = jnp.zeros_like(lse_ref)

    for pair in range(2):
        keys_ref, values_ref = (k_ref, v_ref) if pair == 0 else (kf_ref, vf_ref)
        slots = [slot_ref[2 * pair], slot_ref[2 * pair + 1]]
        qs = [q_ref[late_rows(slot), :] * mask for slot in slots]
        s = mm(jnp.concatenate(qs, axis=0), keys_ref[0:PROMPT, :], NT)
        s = s + jnp.concatenate([slab[:, 0:PROMPT], slab[:, 0:PROMPT]], axis=0)
        own = jnp.concatenate(
            [
                mm(q, k_ref[late_rows(slot), :], NT) + slab[:, PROMPT:DIST] + ok_ref[slot]
                for q, slot in zip(qs, slots)
            ],
            axis=0,
        )
        top = jnp.maximum(
            jnp.max(s, axis=-1, keepdims=True), jnp.max(own, axis=-1, keepdims=True)
        )
        e = jnp.exp(s - top)
        e_own = jnp.exp(own - top)
        total = jnp.sum(e, axis=-1, keepdims=True) + jnp.sum(e_own, axis=-1, keepdims=True)
        o = mm(e.astype(BF), values_ref[0:PROMPT, :] * mask)
        low = e_own.astype(BF)
        o_own = [
            mm(low[CONT_LEN * i : CONT_LEN * (i + 1), :], v_ref[late_rows(slot), :] * mask)
            for i, slot in enumerate(slots)
        ]
        o = (o + jnp.concatenate(o_own, axis=0)) / total
        lse = (top + jnp.log(total)) * mask_f
        for i, slot in enumerate(slots):
            part = slice(CONT_LEN * i, CONT_LEN * (i + 1))
            o_ref[cont_rows(slot), :] = o_ref[cont_rows(slot), :] + o[part, :].astype(BF)
            lse_ref[cont_rows(slot), :] = lse_ref[cont_rows(slot), :] + lse[part, :]


def row_of(lse, head):
    width = lse.shape[1]
    lane = lax.broadcasted_iota(jnp.int32, (1, width), 1)
    column = jnp.sum(jnp.where(lane == head * HEAD, lse, 0.0), axis=-1, keepdims=True)
    return jnp.broadcast_to(column, (lse.shape[0], TILE)).T[0:1, :]


def fold_slab(block):
    rows = TILE
    block = jnp.concatenate([block, jnp.zeros((TILE, LINE - SLAB), F32)], axis=1)
    while rows > 8:
        rows //= 2
        block = pltpu.roll(block[:rows], rows, 1) + block[rows:]
    line = jnp.zeros((1, LINE), F32)
    for r in range(rows):
        line = line + pltpu.roll(block, rows - 1 - r, 1)[r : r + 1]
    return line


def prompt_back(
    line_ref, q_ref, k_ref, kt_ref, v_ref, do_ref, lse_ref, dq_ref, dk_ref, dv_ref, gl_ref,
    slab, gslab, dqt,
):
    head = pl.program_id(0)
    slab[...] = make_slab(line_ref[0]).T
    gslab[...] = jnp.zeros_like(gslab)
    width = q_ref.shape[1]
    mask = head_mask(head, width, BF)

    @pl.when(head == 0)
    def _():
        dk_ref[...] = jnp.zeros_like(dk_ref)
        dv_ref[...] = jnp.zeros_like(dv_ref)

    mine = pl.ds(pl.multiple_of(head * HEAD, HEAD), HEAD)
    block = 2 * TILE
    for idx in range(PROMPT // block):
        keys = block * (idx + 1)
        rows = pl.ds(idx * block, block)
        q = q_ref[rows, :] * mask
        do = do_ref[rows, :] * mask
        s = mm(k_ref[0:keys, :], q, NT)
        start = PROMPT - block * idx
        s = s + jnp.concatenate(
            [slab[start : start + keys, :], slab[start - TILE : start - TILE + keys, :]], axis=1
        )
        p = jnp.exp(s - row_of(lse_ref[rows, :], head))
        dp = mm(v_ref[0:keys, :], do, NT)
        centre = jnp.sum(p * dp, axis=0, keepdims=True)
        ds = p * (dp - centre)
        low = ds.astype(BF)
        dv_ref[0:keys, :] = dv_ref[0:keys, :] + mm(p.astype(BF), do)
        dk_ref[0:keys, :] = dk_ref[0:keys, :] + mm(low, q)
        dqt[mine, rows] = mm(kt_ref[mine, 0:keys], low)
        gslab[start : start + keys, :] = gslab[start : start + keys, :] + ds[:, 0:TILE]
        gslab[start - TILE : start - TILE + keys, :] = (
            gslab[start - TILE : start - TILE + keys, :] + ds[:, TILE:block]
        )
    gl_ref[0] = fold_slab(gslab[...].T)

    @pl.when(head == pl.num_programs(0) - 1)
    def _():
        dq_ref[...] = (dqt[...].T * HEAD ** (-0.5)).astype(BF)


def cont_back(
    slot_ref, line_ref, ok_ref, q_ref, k_ref, kt_ref, v_ref, kf_ref, ktf_ref, vf_ref, do_ref,
    lse_ref, dq_ref, dkc_ref, dvc_ref, dk_ref, dv_ref, dkf_ref, dvf_ref, gl_ref,
    slab, gslab, dqt, dkc, dvc, dkf, dvf,
):
    head = pl.program_id(0)
    slab[...] = make_slab(line_ref[0]).T
    gslab[...] = jnp.zeros_like(gslab)
    width = q_ref.shape[1]
    mask = head_mask(head, width, BF)

    @pl.when(head == 0)
    def _():
        for ref in (dk_ref, dv_ref, dkf, dvf, dkc, dvc):
            ref[...] = jnp.zeros_like(ref)

    mine = pl.ds(pl.multiple_of(head * HEAD, HEAD), HEAD)
    for pair in range(2):
        keys_ref, kt, values_ref = (
            (k_ref, kt_ref, v_ref) if pair == 0 else (kf_ref, ktf_ref, vf_ref)
        )
        gk, gv = (dk_ref, dv_ref) if pair == 0 else (dkf, dvf)
        slots = [slot_ref[2 * pair], slot_ref[2 * pair + 1]]
        qs = [q_ref[late_rows(slot), :] * mask for slot in slots]
        dos = [do_ref[cont_rows(slot), :] * mask for slot in slots]
        q = jnp.concatenate(qs, axis=0)
        do = jnp.concatenate(dos, axis=0)
        lse = row_of(
            jnp.concatenate([lse_ref[cont_rows(slot), :] for slot in slots], axis=0), head
        )
        s = mm(keys_ref[0:PROMPT, :], q, NT)
        s = s + jnp.concatenate([slab[0:PROMPT, :], slab[0:PROMPT, :]], axis=1)
        own = jnp.concatenate(
            [
                mm(k_ref[late_rows(slot), :], qc, NT) + slab[PROMPT:DIST, :] + ok_ref[slot]
                for qc, slot in zip(qs, slots)
            ],
            axis=1,
        )
        p = jnp.exp(s - lse)
        p_own = jnp.exp(own - lse)
        dp = mm(values_ref[0:PROMPT, :], do, NT)
        dp_own = jnp.concatenate(
            [mm(v_ref[late_rows(slot), :], doc, NT) for doc, slot in zip(dos, slots)], axis=1
        )
        centre = jnp.sum(p * dp, axis=0, keepdims=True) + jnp.sum(
            p_own * dp_own, axis=0, keepdims=True
        )
        ds = p * (dp - centre)
        ds_own = p_own * (dp_own - centre)
        low = ds.astype(BF)
        low_own = ds_own.astype(BF)
        p_low = p_own.astype(BF)
        gv[...] = gv[...] + mm(p.astype(BF), do)
        gk[...] = gk[...] + mm(low, q)
        dq = mm(kt[mine, 0:PROMPT], low)
        for i, slot in enumerate(slots):
            part = slice(CONT_LEN * i, CONT_LEN * (i + 1))
            here = cont_rows(slot)
            dvc[here, :] = dvc[here, :] + mm(p_low[:, part], dos[i])
            dkc[here, :] = dkc[here, :] + mm(low_own[:, part], qs[i])
            kown = k_ref[late_rows(slot), :].T
            head_keys = kown[0:HEAD, :]
            for other in range(1, width // HEAD):
                head_keys = jnp.where(
                    head == other, kown[HEAD * other : HEAD * (other + 1), :], head_keys
                )
            dqt[slot, mine, :] = dq[:, part] + mm(head_keys, low_own[:, part])
            gslab[0:PROMPT, :] = gslab[0:PROMPT, :] + ds[:, part]
            gslab[PROMPT:DIST, :] = gslab[PROMPT:DIST, :] + ds_own[:, part]
    gl_ref[0] = fold_slab(gslab[...].T)

    @pl.when(head == pl.num_programs(0) - 1)
    def _():
        for slot in range(dqt.shape[0]):
            dq_ref[slot * CONT_LEN : (slot + 1) * CONT_LEN, :] = (
                dqt[slot].T * HEAD ** (-0.5)
            ).astype(BF)
        dkf_ref[...] = dkf[...].astype(BF)
        dvf_ref[...] = dvf[...].astype(BF)
        dkc_ref[...] = dkc[...].astype(BF)
        dvc_ref[...] = dvc[...].astype(BF)


def cross_fwd(far_ref, q_ref, k_ref, v_ref, o_ref, lse_ref):
    rows = q_ref.shape[0] - CONT_LEN
    far = pl.ds(pl.multiple_of(far_ref[0] * ENC_LEN, ENC_LEN), ENC_LEN)
    for part, keys in ((pl.ds(0, rows), pl.ds(0, ENC_LEN)), (pl.ds(rows, CONT_LEN), far)):
        q = q_ref[part, :]
        k = k_ref[keys, :]
        v = v_ref[keys, :]
        o = 0.0
        lse = 0.0
        for head in range(2):
            mask = head_mask(head, TILE, BF)
            s = mm(q * mask, k, NT)
            top = jnp.max(s, axis=-1, keepdims=True)
            e = jnp.exp(s - top)
            total = jnp.sum(e, axis=-1, keepdims=True)
            o = o + mm(e.astype(BF), v * mask) / total
            lse = lse + (top + jnp.log(total)) * head_mask(head, TILE, F32)
        o_ref[part, :] = o.astype(BF)
        lse_ref[part, :] = lse


def cross_back(far_ref, q_ref, k_ref, v_ref, do_ref, lse_ref, dq_ref, dk_ref, dv_ref, dk, dv):
    rows = q_ref.shape[0] - CONT_LEN
    far = pl.ds(pl.multiple_of(far_ref[0] * ENC_LEN, ENC_LEN), ENC_LEN)
    dk[ENC_LEN : 2 * ENC_LEN, :] = jnp.zeros((ENC_LEN, TILE), F32)
    dv[ENC_LEN : 2 * ENC_LEN, :] = jnp.zeros((ENC_LEN, TILE), F32)
    for index, (part, keys) in enumerate(
        ((pl.ds(0, rows), pl.ds(0, ENC_LEN)), (pl.ds(rows, CONT_LEN), far))
    ):
        q = q_ref[part, :]
        k = k_ref[keys, :]
        kt = k.T
        v = v_ref[keys, :]
        do = do_ref[part, :]
        lse = lse_ref[part, :].T
        gk, gv = (0.0, 0.0)
        dq = []
        for head in range(2):
            mask = head_mask(head, TILE, BF)
            qm = q * mask
            dom = do * mask
            s = mm(k, qm, NT)
            p = jnp.exp(s - lse[HEAD * head : HEAD * head + 1, :])
            dp = mm(v, dom, NT)
            centre = jnp.sum(p * dp, axis=0, keepdims=True)
            low = (p * (dp - centre)).astype(BF)
            gv = gv + mm(p.astype(BF), dom)
            gk = gk + mm(low, qm)
            dq.append(mm(kt[HEAD * head : HEAD * (head + 1), :], low))
        dq_ref[part, :] = (jnp.concatenate(dq, axis=0).T * HEAD ** (-0.5)).astype(BF)
        if index == 0:
            dk[0:ENC_LEN, :] = gk
            dv[0:ENC_LEN, :] = gv
        else:
            dk[keys, :] = dk[keys, :] + gk
            dv[keys, :] = dv[keys, :] + gv
    dk_ref[...] = dk[...].astype(BF)
    dv_ref[...] = dv[...].astype(BF)


def whole(shape):
    return pl.BlockSpec(shape, lambda *_: (0,) * len(shape))


def by_head(shape):
    return pl.BlockSpec((1,) + shape[1:], lambda head, *_: (head,) + (0,) * (len(shape) - 1))


def cost(flops, transcendentals, arrays):
    return pl.CostEstimate(
        flops=int(flops),
        transcendentals=int(transcendentals),
        bytes_accessed=int(sum(a.size * a.dtype.itemsize for a in arrays)),
    )


def shaped(*pairs):
    return [jax.ShapeDtypeStruct(shape, dtype) for shape, dtype in pairs]


def run_heads(kernel, heads, scalars, lines, arrays, outs, scratch, out_heads, cells, name):
    in_specs = [by_head(a.shape) for a in lines] + [whole(a.shape) for a in arrays]
    out_specs = [
        by_head(o.shape) if i in out_heads else whole(o.shape) for i, o in enumerate(outs)
    ]
    return pl.pallas_call(
        kernel,
        out_shape=outs,
        grid_spec=pltpu.PrefetchScalarGridSpec(
            num_scalar_prefetch=len(scalars),
            grid=(heads,),
            in_specs=in_specs,
            out_specs=out_specs,
            scratch_shapes=scratch,
        ),
        compiler_params=pltpu.CompilerParams(dimension_semantics=("arbitrary",)),
        cost_estimate=cost(
            cells * heads * 256 * 2 * (2 if not out_heads else 5), cells * heads,
            list(lines) + list(arrays) + list(outs),
        ),
        name=name,
    )(*scalars, *lines, *arrays)


def on_device(
    x_prompt,
    x_cont,
    enc_out,
    cot_prompt,
    cot_cont,
    teacher,
    valid,
    prompt_of,
    buckets,
    gain_self,
    gain_cross,
    gain_ffn,
    rel_table,
    w_q,
    w_k,
    w_v,
    w_o,
    c_q,
    c_k,
    c_v,
    c_o,
    w_gate,
    w_up,
    w_down,
):
    width = x_prompt.shape[1]
    cont_count = prompt_of.shape[0]
    heads = w_q.shape[1] // HEAD
    cols = heads * HEAD
    hidden_here = w_gate.shape[1]
    ranks = lax.axis_size("tensor")
    data_size = lax.axis_size("dp")
    share = PROMPT // ranks
    tensor_rank = lax.axis_index("tensor")
    data_rank = lax.axis_index("dp")
    factor = HEAD ** (-0.5)
    up, down = bit_lists()
    order_up, order_down = slice_order(up), slice_order(down)

    far = (prompt_of != data_rank).astype(jnp.int32)
    index = jnp.arange(cont_count, dtype=jnp.int32)
    before = index[None, :] < index[:, None]
    near_rank = jnp.sum(jnp.where(before, 1 - far[None, :], 0), axis=1)
    far_rank = jnp.sum(jnp.where(before, far[None, :], 0), axis=1)
    spot = jnp.where(far == 0, near_rank, cont_count // 2 + far_rank)
    slots = jnp.sum(jnp.where(spot[None, :] == index[:, None], index[None, :], 0), axis=1)
    far_here = lax.dynamic_slice_in_dim(far, tensor_rank, 1, 0)

    def own_rows(prompt_rows, conts):
        return jnp.concatenate(
            [
                lax.dynamic_slice_in_dim(prompt_rows, tensor_rank * share, share, 0),
                lax.dynamic_slice_in_dim(conts, tensor_rank * CONT_LEN, CONT_LEN, 0),
            ]
        )

    head_rows = HEAD // data_size
    attn_shard = jnp.stack([w_o, c_q.T, c_k.T, c_v.T, c_o]).reshape(
        5, 1, heads, data_size, head_rows, width
    )
    attn_own = lax.dynamic_slice_in_dim(attn_shard, data_rank, 1, 3)
    hidden_rows = hidden_here // data_size
    ffn_own = jnp.stack(
        [
            lax.dynamic_slice_in_dim(w_gate, data_rank * hidden_rows, hidden_rows, 1).T,
            lax.dynamic_slice_in_dim(w_up, data_rank * hidden_rows, hidden_rows, 1).T,
            lax.dynamic_slice_in_dim(w_down, data_rank * hidden_rows, hidden_rows, 0),
        ]
    ).reshape(3, 1, 1, 1, hidden_rows, width)
    enc_far = flip_bit(enc_out, 0)
    attn_full = gather_weights(attn_own)
    ffn_full = gather_weights(ffn_own)

    count = jnp.broadcast_to(jnp.sum(valid.astype(F32)), (8, 128))
    for bit in range(data_size.bit_length() - 1):
        count = count + flip_bit(count, bit)
    token_count = count[0, 0]

    bucket_hot = (buckets[::-1][:, None] == jnp.arange(rel_table.shape[0])[None, :]).astype(F32)
    table = jnp.dot(bucket_hot, rel_table, precision=lax.Precision.HIGHEST).T
    line = jnp.concatenate(
        [table, jnp.full((heads, LINE - DIST), masked_value, F32)], axis=1
    ).reshape(heads, 1, LINE)
    ok = jnp.where(valid > 0, 0.0, masked_value).astype(F32)
    ok_rows = jnp.broadcast_to(
        ok.reshape(cont_count, 1, CONT_LEN), (cont_count, CONT_LEN, CONT_LEN)
    )
    ok_cols = jnp.broadcast_to(
        ok.reshape(cont_count, CONT_LEN, 1), (cont_count, CONT_LEN, CONT_LEN)
    )

    stream = jnp.concatenate([x_prompt, x_cont]).astype(F32)
    n1 = rms_norm(stream, gain_self).astype(BF)
    key_s = mm(n1, w_k).astype(BF)
    value_s = mm(n1, w_v).astype(BF)
    query_s = (mm(n1, w_q).astype(F32) * factor).astype(BF)
    key_t = mm(w_k, n1, (((0,), (1,)), ((), ()))).astype(BF)
    pair_far = flip_bit(
        jnp.concatenate([key_s[:PROMPT], value_s[:PROMPT]], axis=0), 0
    )
    key_far, value_far = pair_far[:PROMPT], pair_far[PROMPT:]
    rows_all = query_s.shape[0]
    rows_late = rows_all - PROMPT
    slab = pltpu.VMEM((TILE, SLAB), F32)
    slab_t = pltpu.VMEM((SLAB, TILE), F32)
    o_prompt, lse_prompt = run_heads(
        prompt_fwd, heads, [], [line], [query_s, key_s, value_s],
        shaped(((PROMPT, cols), BF), ((PROMPT, cols), F32)), [slab], (),
        PROMPT * PROMPT * 5 // 8, "prompt_fwd",
    )
    o_cont, lse_cont = run_heads(
        cont_fwd, heads, [slots], [line], [ok_rows, query_s, key_s, value_s, key_far, value_far],
        shaped(((rows_late, cols), BF), ((rows_late, cols), F32)), [slab], (),
        rows_late * DIST, "cont_fwd",
    )

    def heads_to_rows(block, rows):
        out = []
        for step in range(ranks):
            dest = (tensor_rank - step + ranks) % ranks
            piece = lax.dynamic_slice_in_dim(block, dest * rows, rows, 0)
            out.append(piece if step == 0 else from_ahead(piece, step))
        return jnp.concatenate(out, axis=1)

    def rows_to_heads(block):
        out = []
        for step in range(ranks):
            piece = block[:, step * cols : (step + 1) * cols]
            out.append(piece if step == 0 else to_ahead(piece, step))
        rows = block.shape[0]
        held = jnp.concatenate(out, axis=0).reshape(ranks, rows, cols)
        pick = (tensor_rank - jnp.arange(ranks) + ranks) % ranks
        return (held, pick)

    mixed_self = jnp.concatenate(
        [heads_to_rows(o_prompt, share), heads_to_rows(o_cont, CONT_LEN)]
    )

    hot_up = slice_hot(order_up, heads, head_rows, data_rank)
    hot_down = slice_hot(order_down, heads, head_rows, data_rank)
    hot_four = jnp.stack([hot_up, hot_up, hot_down, hot_down])
    attn_flat = attn_full.reshape(5, ranks * cols, width)
    wo_full = (
        jnp.einsum(
            "zrn,zrd->znd",
            hot_four,
            attn_flat[0].reshape(ranks, cols, width),
            preferred_element_type=F32,
        )
        .astype(BF)
        .reshape(ranks * cols, width)
    )
    cq_t, ck_t, cv_t, co_full = attn_flat[1], attn_flat[2], attn_flat[3], attn_flat[4]
    x_own = own_rows(x_prompt, x_cont).astype(F32)
    x1 = x_own + mm(mixed_self, wo_full)
    n2 = rms_norm(x1, gain_cross).astype(BF)
    query_c = (mm(n2, cq_t, NT) * factor).astype(BF)
    enc_pair = jnp.concatenate([enc_out, enc_far])
    key_c = mm(enc_pair, ck_t, NT).astype(BF)
    value_c = mm(enc_pair, cv_t, NT).astype(BF)
    own_count = query_c.shape[0]
    pairs = query_c.shape[1] // TILE

    def columns(rows):
        return pl.BlockSpec((rows, TILE), lambda i, *_: (0, i))

    cross_cells = own_count * ENC_LEN * pairs * 2
    mixed_cross, lse_cross = pl.pallas_call(
        cross_fwd,
        out_shape=shaped(((own_count, pairs * TILE), BF), ((own_count, pairs * TILE), F32)),
        grid_spec=pltpu.PrefetchScalarGridSpec(
            num_scalar_prefetch=1,
            grid=(pairs,),
            in_specs=[columns(own_count), columns(2 * ENC_LEN), columns(2 * ENC_LEN)],
            out_specs=[columns(own_count), columns(own_count)],
        ),
        compiler_params=pltpu.CompilerParams(dimension_semantics=("arbitrary",)),
        cost_estimate=cost(cross_cells * 256 * 2 * 2, cross_cells, [query_c, key_c, value_c]),
        name="cross_fwd",
    )(far_here, query_c, key_c, value_c)
    x2 = x1 + mm(mixed_cross, co_full)
    n3 = rms_norm(x2, gain_ffn).astype(BF)
    ffn_flat = ffn_full.reshape(3, ranks * hidden_here, width)
    wg_t, wu_t, wd = ffn_flat[0], ffn_flat[1], ffn_flat[2]
    gate_pre = mm(n3, wg_t, NT)
    upper = mm(n3, wu_t, NT)
    hidden, gelu_pull = jax.vjp(
        lambda first_in, second_in: jax.nn.gelu(first_in, approximate=True) * second_in,
        gate_pre,
        upper,
    )
    hidden = hidden.astype(BF)
    x3 = x2 + mm(hidden, wd)
    valid_own = lax.dynamic_slice_in_dim(valid, tensor_rank * CONT_LEN, CONT_LEN, 0).astype(F32)[
        :, None
    ]
    deviation = x3[share:] - teacher.astype(F32)
    loss_part = jnp.sum(valid_own * deviation * deviation)
    g3 = jnp.concatenate(
        [
            cot_prompt.astype(F32),
            cot_cont.astype(F32) + 2.0 * valid_own * deviation / token_count,
        ]
    )
    y_all = x3.astype(BF)

    g3_low = g3.astype(BF)
    d_hidden = mm(g3_low, wd, NT).astype(BF).astype(F32)
    d_gate, d_upper = gelu_pull(d_hidden)
    d_gate = d_gate.astype(BF)
    d_upper = d_upper.astype(BF)
    d_n3 = mm(d_gate, wg_t) + mm(d_upper, wu_t)
    ffn_grads = jnp.stack(
        [
            mm(d_gate, n3, TN).astype(BF),
            mm(d_upper, n3, TN).astype(BF),
            mm(hidden, g3_low, TN).astype(BF),
        ]
    ).reshape(3, ranks, 1, data_size, hidden_rows, width)
    ffn_left, ffn_right = reduce_grads(ffn_grads)
    back3, gain_ffn_part = norm_back(x2, gain_ffn, d_n3)
    g2 = g3 + back3

    g2_low = g2.astype(BF)
    d_mixed_c = mm(g2_low, co_full, NT).astype(BF)
    d_query_c, d_key_c, d_value_c = pl.pallas_call(
        cross_back,
        out_shape=shaped(
            ((own_count, pairs * TILE), BF),
            ((2 * ENC_LEN, pairs * TILE), BF),
            ((2 * ENC_LEN, pairs * TILE), BF),
        ),
        grid_spec=pltpu.PrefetchScalarGridSpec(
            num_scalar_prefetch=1,
            grid=(pairs,),
            in_specs=[
                columns(own_count), columns(2 * ENC_LEN), columns(2 * ENC_LEN),
                columns(own_count), columns(own_count),
            ],
            out_specs=[columns(own_count), columns(2 * ENC_LEN), columns(2 * ENC_LEN)],
            scratch_shapes=[pltpu.VMEM((2 * ENC_LEN, TILE), F32)] * 2,
        ),
        compiler_params=pltpu.CompilerParams(dimension_semantics=("arbitrary",)),
        cost_estimate=cost(cross_cells * 256 * 2 * 5, cross_cells, [query_c, key_c, value_c]),
        name="cross_back",
    )(far_here, query_c, key_c, value_c, d_mixed_c, lse_cross)
    d_n2 = mm(d_query_c, cq_t)
    back2, gain_cross_part = norm_back(x1, gain_cross, d_n2)
    g1 = g2 + back2
    g1_low = g1.astype(BF)

    d_mixed_s = mm(g1_low, wo_full, NT).astype(BF)
    held, pick = rows_to_heads(d_mixed_s)
    place = (pick[None, :] == jnp.arange(ranks)[:, None]).astype(BF)
    ordered = jnp.einsum("ns,src->nrc", place, held, preferred_element_type=F32).astype(BF)
    do_prompt = ordered[:, :share].reshape(PROMPT, cols)
    do_cont = ordered[:, share:].reshape(rows_late, cols)

    key_far_t = key_far.T
    (dq_cont, dk_cont, dv_cont, dk_near, dv_near, dk_far, dv_far, line_cont) = run_heads(
        cont_back, heads, [slots], [line],
        [ok_cols, query_s, key_s, key_t, value_s, key_far, key_far_t, value_far, do_cont, lse_cont],
        shaped(
            ((rows_late, cols), BF), ((rows_late, cols), BF), ((rows_late, cols), BF),
            ((PROMPT, cols), F32), ((PROMPT, cols), F32),
            ((PROMPT, cols), BF), ((PROMPT, cols), BF), ((heads, 1, LINE), F32),
        ),
        [slab_t, slab_t, pltpu.VMEM((cont_count, cols, CONT_LEN), F32)]
        + [pltpu.VMEM((rows_late, cols), F32)] * 2 + [pltpu.VMEM((PROMPT, cols), F32)] * 2,
        (7,), rows_late * DIST, "cont_back",
    )
    lent = flip_bit(jnp.concatenate([dk_far, dv_far], axis=0), 0)
    dq_prompt, dk_prompt, dv_prompt, line_prompt = run_heads(
        prompt_back, heads, [], [line],
        [query_s, key_s, key_t, value_s, do_prompt, lse_prompt],
        shaped(
            ((PROMPT, cols), BF), ((PROMPT, cols), F32), ((PROMPT, cols), F32),
            ((heads, 1, LINE), F32),
        ),
        [slab_t, slab_t, pltpu.VMEM((cols, PROMPT), F32)], (3,),
        PROMPT * PROMPT * 5 // 8, "prompt_back",
    )
    dk_prompt = (dk_prompt + dk_near + lent[:PROMPT].astype(F32)).astype(BF)
    dv_prompt = (dv_prompt + dv_near + lent[PROMPT:].astype(F32)).astype(BF)

    def three(q, k, v):
        return mm(q, w_q, NT) + mm(k, w_k, NT) + mm(v, w_v, NT)

    def scatter_rows(block, rows):
        total = lax.dynamic_slice_in_dim(block, tensor_rank * rows, rows, 0).astype(F32)
        for step in range(1, ranks):
            dest = (tensor_rank + step) % ranks
            piece = lax.dynamic_slice_in_dim(block, dest * rows, rows, 0)
            total = total + to_ahead(piece, step).astype(F32)
        return total

    part_cont = three(dq_cont, dk_cont, dv_cont).astype(BF)
    part_prompt = three(dq_prompt, dk_prompt, dv_prompt).astype(BF)
    d_n1 = jnp.concatenate([scatter_rows(part_prompt, share), scatter_rows(part_cont, CONT_LEN)])
    back1, ignored = norm_back(x_own, gain_self, d_n1)
    grad_x = g1 + back1
    unit = stream * norm_scale(stream)
    gain_self_part = jnp.sum(part_prompt.astype(F32) * unit[:PROMPT], axis=0) + jnp.sum(
        part_cont.astype(F32) * unit[PROMPT:], axis=0
    )

    enc_part = mm(d_key_c, ck_t) + mm(d_value_c, cv_t)
    enc_sum = (enc_part[:ENC_LEN] + flip_bit(enc_part[ENC_LEN:].astype(BF), 0).astype(F32)).astype(
        BF
    )
    enc_rows = ENC_LEN // ranks
    enc_own = scatter_rows(enc_sum, enc_rows).astype(BF)
    enc_all = jnp.concatenate(
        [enc_own] + [from_ahead(enc_own, step) for step in range(1, ranks)]
    )
    enc_place = jnp.arange(ENC_LEN)
    enc_from = (tensor_rank + enc_place // enc_rows) % ranks * enc_rows + enc_place % enc_rows
    enc_hot = (enc_from[:, None] == enc_place[None, :]).astype(BF)
    grad_enc = mm(enc_hot, enc_all, TN)

    grad_wo_part = mm(mixed_self, g1_low, TN).astype(BF).reshape(ranks, cols, width)
    grad_wo_part = jnp.einsum(
        "zrn,znd->zrd", hot_four, grad_wo_part, preferred_element_type=F32
    ).astype(BF)
    attn_grads = jnp.stack(
        [
            grad_wo_part.reshape(ranks * cols, width),
            mm(d_query_c, n2, TN).astype(BF),
            mm(d_key_c, enc_pair, TN).astype(BF),
            mm(d_value_c, enc_pair, TN).astype(BF),
            mm(mixed_cross, g2_low, TN).astype(BF),
        ]
    ).reshape(5, ranks, heads, data_size, head_rows, width)
    attn_left, attn_right = reduce_grads(attn_grads)

    def finish(left, right, hots, matrix, transposed):
        halves = [
            half[matrix].reshape(-1, half.shape[-1]) for half in (left, right)
        ]
        if transposed:
            return jnp.concatenate([mm(a, hot, TN) for a, hot in zip(halves, hots)], axis=0)
        return jnp.concatenate([mm(hot, a, TN) for a, hot in zip(halves, hots)], axis=1)

    attn_hots = (hot_up, hot_down)
    ffn_hots = (
        slice_hot(order_up, 1, hidden_rows, data_rank),
        slice_hot(order_down, 1, hidden_rows, data_rank),
    )
    grad_w_o = finish(attn_left, attn_right, attn_hots, 0, False)
    grad_c_q = finish(attn_left, attn_right, attn_hots, 1, True)
    grad_c_k = finish(attn_left, attn_right, attn_hots, 2, True)
    grad_c_v = finish(attn_left, attn_right, attn_hots, 3, True)
    grad_c_o = finish(attn_left, attn_right, attn_hots, 4, False)
    grad_w_gate = finish(ffn_left, ffn_right, ffn_hots, 0, True)
    grad_w_up = finish(ffn_left, ffn_right, ffn_hots, 1, True)
    grad_w_down = finish(ffn_left, ffn_right, ffn_hots, 2, False)

    def by_rows(prompt_part, cont_part):
        return mm(n1[:PROMPT], prompt_part, TN) + mm(n1[PROMPT:], cont_part, TN)

    qkv_grads = jnp.concatenate(
        [
            by_rows(dq_prompt, dq_cont),
            by_rows(dk_prompt, dk_cont),
            by_rows(dv_prompt, dv_cont),
        ],
        axis=1,
    ).astype(BF)
    feat_rows = width // data_size
    qkv_width = qkv_grads.shape[1]
    qkv_hots = (
        slice_hot(order_up, 1, feat_rows, data_rank),
        slice_hot(order_down, 1, feat_rows, data_rank),
    )
    half = qkv_width // 2
    qkv_parts = []
    for hot, bits, cut in (
        (qkv_hots[0], up, qkv_grads[:, :half]),
        (qkv_hots[1], down, qkv_grads[:, half:]),
    ):
        moved = mm(hot, cut).astype(BF).reshape(1, 1, 1, data_size, feat_rows, half)
        for bit in [0] + bits[::-1]:
            moved = fold(moved, bit, 3)
        moved = spread(moved, bits + [0], 3).reshape(width, half)
        qkv_parts.append(mm(hot, moved, TN))
    qkv_all = jnp.concatenate(qkv_parts, axis=1)

    line_grad = (line_cont + line_prompt).reshape(heads, LINE)[:, :DIST]
    table_part = jnp.dot(line_grad, bucket_hot, precision=lax.Precision.HIGHEST)
    small = jnp.zeros((8, width), F32)
    small = small.at[0].set(gain_self_part).at[1].set(gain_cross_part).at[2].set(gain_ffn_part)
    small = small.at[3, 0].set(loss_part)
    small = small.at[4, : table_part.size].set(table_part.reshape(-1))
    for bit in range(data_size.bit_length() - 1):
        small = small + flip_bit(small, bit)
    grad_table = small[4, : table_part.size].reshape(table_part.shape).T
    for bit in range(ranks.bit_length() - 1):
        small = small + flip_bit(small, bit, "tensor")
    return (
        y_all[:share],
        y_all[share:],
        grad_x[:share],
        grad_x[share:],
        grad_enc,
        small[0],
        small[1],
        small[2],
        grad_table,
        qkv_all[:, :cols],
        qkv_all[:, cols : 2 * cols],
        qkv_all[:, 2 * cols :],
        grad_w_o,
        grad_c_q,
        grad_c_k,
        grad_c_v,
        grad_c_o,
        grad_w_gate,
        grad_w_up,
        grad_w_down,
        small[3, 0] / token_count,
    )


def solution(mesh):
    rows = P("dp", None)
    both = P(("dp", "tensor"), None)
    columns = P(None, "tensor")
    shards = P("tensor", None)
    return jax.shard_map(
        on_device,
        mesh=mesh,
        in_specs=(
            (rows,) * 3 + (both,) * 3 + (P("dp"),) * 2 + (P(),) * 4 + (columns,) * 4
            + (shards,) + (columns,) * 3 + (shards,) + (columns,) * 2 + (shards,)
        ),
        out_specs=(
            (both,) * 4 + (rows,) + (P(),) * 3 + (columns,) * 4 + (shards,) + (columns,) * 3
            + (shards,) + (columns,) * 2 + (shards, P())
        ),
        check_vma=False,
    )
```

time: 1410 us -> 646 us (0.46)
  waiting for transfers between devices: 647 us -> 155 us
  local copies, waits for them, and re-layouts: 314 us -> 104 us
  blocking collectives: 158 us -> 0 us
  starting transfers between devices: 3.46 us -> 107 us
  Pallas kernels: 0 us -> 73.3 us
  matrix products: 146 us -> 96.8 us
  other arithmetic: 118 us -> 95.1 us
    psum x3 -> x0, waiting for transfers between devices: 315 us -> none  [the longest x1 162 us: on_device(): after_self = stream + lax.psum(project(mixed_self, w_o), 'tensor')]
    reduce_scatter x8 -> x0, waiting for transfers between devices: 282 us -> none  [the longest x1 61.6 us: on_device(): lax.psum_scatter(cross_part[:prompt_rows], 'tensor', scatter_dimension=0,...]
    ppermute x8 -> x93, waiting for transfers between devices: 1.42 us -> 155 us  [the longest x60 111 us: flip_bit(): return lax.ppermute(block, axis, [(i, i ^ 1 << bit) for i in range(count)])]
    unnamed x489 -> x303, local copies, waits for them, and re-layouts: 156 us -> 36 us
    all_gather x4 -> x0, blocking collectives: 106 us -> none  [the longest x1 28 us: on_device(): lax.all_gather(low_share1[share_prompt:], 'tensor', axis=0, tiled=True)]
    ppermute x8 -> x93, starting transfers between devices: 2.26 us -> 107 us  [the longest x60 42.8 us: flip_bit(): return lax.ppermute(block, axis, [(i, i ^ 1 << bit) for i in range(count)])]
    pallas_call x0 -> x6, Pallas kernels: none -> 73.3 us  [the longest x4 48.1 us: run_heads(): pl.pallas_call(kernel, out_shape=outs, grid_spec=pltpu.PrefetchScalarGrid...]
    psum x3 -> x0, blocking collectives: 52.4 us -> none  [the longest x1 26.9 us: on_device(): lax.psum((grad_gain_self, gain_cross_sum, gain_ffn_sum, grad_table, grad_...]
  transfers between devices with their start and end apart: 23 -> 93, of which waited for: 15 -> 34; matrix products, arithmetic and copies ran while one was open for 29% -> 34% of each run, Pallas kernels for 0% -> 9%
where the time goes in v1:
time: 646 us; the launch traced here: 637 us
  waiting for transfers between devices  155 us (24%)
  starting transfers between devices  107 us (17%)
  local copies, waits for them, and re-layouts  104 us (16%)
  matrix products  96.8 us (15%)
  other arithmetic  95.1 us (15%)
  Pallas kernels  73.3 us (11%)
    ppermute x60, waiting for transfers between devices, flip_bit(): return lax.ppermute(block, axis, [(i, i ^ 1 << bit) for i in range(count)])  111 us
    dot_general x60, matrix products, mm(): return lax.dot_general(left, right, dims, preferred_element_type=F32)  93.3 us
    pallas_call x4, Pallas kernels, run_heads(): pl.pallas_call(kernel, out_shape=outs, grid_spec=pltpu.PrefetchScalarGrid...  48.1 us
    ppermute x60, starting transfers between devices, flip_bit(): return lax.ppermute(block, axis, [(i, i ^ 1 << bit) for i in range(count)])  42.8 us
    ppermute x18, starting transfers between devices, to_ahead(): lax.ppermute(block, 'tensor', [(i, (i + step) % count) for i in range(cou...  38.3 us
    unnamed x303, local copies, waits for them, and re-layouts  36 us
    ppermute x18, waiting for transfers between devices, to_ahead(): lax.ppermute(block, 'tensor', [(i, (i + step) % count) for i in range(cou...  35.7 us
    ppermute x15, starting transfers between devices, from_ahead(): lax.ppermute(block, 'tensor', [((i + step) % count, i) for i in range(cou...  26.1 us
  transfers between devices with their start and end apart: 93, of which 34 were waited for; matrix products, arithmetic and copies ran while one was open for 34% of the time, Pallas kernels for 9%

profile of v1, /device:TPU:0, one launch (start us, length us, event | category | flops | bytes accessed | tf_op | source)
XLA Modules:
  0.0 637.1 jit_solution(338660121858888398)
XLA Ops:
  37.7 8.7 %prompt_fwd.1 = (bf16[1024,192]{1,0:T(8,128)(2,1)}, f32[1024,192]{1,0:T(8,128)}) custom-call(f32[3,1,1408]{2,1,0:T(1,128)} %reshape.707.line_ref, bf16[1536,192]{1,0:T(8,128)(2,1)} %fusion.10.q_ref, bf16[1536,192]{1,0:T(8,128)(2,1)} %copy-done.47, bf16[1536,192]{1,0:T(8,128)(2,1)} %copy-done.82), custom_call_target="tpu_custom_call" | custom-call | flops 2013265920 | bytes 2966016 | tf_op jit(solution)/shard_map/prompt_fwd/pallas_call | solution.py:463
  65.5 4.4 collective-permute-done.8
  74.3 13.7 %collective-permute-done.27 = f32[8,128]{1,0:T(8,128)S(1)} collective-permute-done((f32[8,128]{1,0:T(8,128)S(1)}, f32[8,128]{1,0:T(8,128)S(1)}, u32[]{:S(2)}, u32[]{:S(2)}) %collective-permute-start.27) | collective-permute-done | bytes 4128 | tf_op jit(solution)/shard_map/ppermute | solution.py:44
  97.2 7.1 %collective-permute-done.18 = bf16[3,2,1,1,64,768]{5,4,0,3,2,1:T(8,128)(2,1)S(1)} collective-permute-done((bf16[3,2,1,1,64,768]{5,4,0,3,2,1:T(8,128)(2,1)S(1)}, bf16[3,2,1,1,64,768]{5,4,0,3,2,1:T(8,128)(2,1)S(1)}, u32[]{:S(2)}, u32[]{:S(2)}) %collective-permute-start.18) | collective-permute-done | bytes 589856 | tf_op jit(solution)/shard_map/ppermute | solution.py:44
  119.2 9.3 %cont_fwd.1 = (bf16[512,192]{1,0:T(8,128)(2,1)}, f32[512,192]{1,0:T(8,128)}) custom-call(s32[4]{0:T(128)} %select_reduce_fusion.slot_ref, f32[3,1,1408]{2,1,0:T(1,128)} %reshape.707.line_ref, f32[4,128,128]{2,1,0:T(8,128)} %broadcast_in_dim.209.ok_ref, bf16[1536,192]{1,0:T(8,128)(2,1)} %fusion.10.q_ref, bf16[1536,192]{1,0:T(8,128)(2,1)} %copy-done.47, ...), custom_call_target="tpu_custom_call" | custom-call | flops 1811939328 | bytes 3424768 | tf_op jit(solution)/shard_map/cont_fwd/pallas_call | solution.py:463
  160.9 10.6 %cross_fwd.1 = (bf16[384,768]{1,0:T(8,128)(2,1)}, f32[384,768]{1,0:T(8,128)}) custom-call(s32[1]{0:T(128)} %dynamic_slice.95.far_ref, bf16[384,768]{1,0:T(8,128)(2,1)} %fusion.19.q_ref, bf16[1024,768]{1,0:T(8,128)(2,1)} %convolution_convert_fusion.7.k_ref, bf16[1024,768]{1,0:T(8,128)(2,1)} %convolution_convert_fusion.6.v_ref), custom_call_target="tpu_custom_call" | custom-call | flops 2415919104 | bytes 3735552 | tf_op jit(solution)/shard_map/cross_fwd/pallas_call | solution.py:650
  175.0 4.8 maximum_maximum_fusion
  198.3 14.5 %cross_back.1 = (bf16[384,768]{1,0:T(8,128)(2,1)}, bf16[1024,768]{1,0:T(8,128)(2,1)}, bf16[1024,768]{1,0:T(8,128)(2,1)}) custom-call(s32[1]{0:T(128)} %dynamic_slice.95.far_ref, bf16[384,768]{1,0:T(8,128)(2,1)} %fusion.19.q_ref, bf16[1024,768]{1,0:T(8,128)(2,1)} %convolution_convert_fusion.7.k_ref, bf16[1024,768]{1,0:T(8,128)(2,1)} %convolution_convert_fusion.6.v_ref, ...), custom_call_target="tpu_custom_call" | custom-call | flops 6039797760 | bytes 3735552 | tf_op jit(solution)/shard_map/cross_back/pallas_call | solution.py:708
  236.1 4.2 collective-permute-start.31
  249.7 8.3 %pad_maximum_fusion = bf16[3,4,1,8,64,768]{5,4,3,1,2,0:T(8,128)(2,1)} fusion(bf16[1,4,1,8,64,768]{5,4,3,1,2,0:T(8,128)(2,1)} %bitcast.207, bf16[1,4,1,8,64,768]{5,4,3,1,2,0:T(8,128)(2,1)} %bitcast.208, bf16[1,4,1,8,64,768]{5,4,3,1,2,0:T(8,128)(2,1)} %bitcast.209), kind=kLoop, calls=%fused_computation.1 | loop fusion | flops 9437184 | bytes 18874368 | tf_op jit(solution)/shard_map/stack | solution.py:695
  258.0 5.2 fusion.167
  280.3 15.5 %cont_back.1 = (bf16[512,192]{1,0:T(8,128)(2,1)}, bf16[512,192]{1,0:T(8,128)(2,1)}, bf16[512,192]{1,0:T(8,128)(2,1)}, f32[1024,192]{1,0:T(8,128)}, f32[1024,192]...) custom-call(s32[4]{0:T(128)} %select_reduce_fusion.slot_ref, ...), custom_call_target="tpu_custom_call" | custom-call | flops 4529848320 | bytes 7373824 | tf_op jit(solution)/shard_map/cont_back/pallas_call | solution.py:463
  310.8 14.6 %prompt_back.1 = (bf16[1024,192]{1,0:T(8,128)(2,1)}, f32[1024,192]{1,0:T(8,128)}, f32[1024,192]{1,0:T(8,128)}, f32[3,1,1408]{2,1,0:T(1,128)}) custom-call(f32[3,1,1408]{2,1,0:T(1,128)} %reshape.707.line_ref, bf16[1536,192]{1,0:T(8,128)(2,1)} %fusion.10.q_ref, bf16[1536,192]{1,0:T(8,128)(2,1)} %copy-done.47, bf16[192,1536]{1,0:T(8,128)(2,1)} %copy.122.kt_ref, ...), custom_call_target="tpu_custom_call" | custom-call | flops 5033164800 | bytes 5538816 | tf_op jit(solution)/shard_map/prompt_back/pallas_call | solution.py:463
  389.7 6.1 collective-permute-done.49
  412.0 7.0 %collective-permute-done.44 = bf16[128,768]{1,0:T(8,128)(2,1)S(1)} collective-permute-done((bf16[128,768]{1,0:T(8,128)(2,1)}, bf16[128,768]{1,0:T(8,128)(2,1)S(1)}, u32[]{:S(2)}, u32[]{:S(2)}) %collective-permute-start.44) | collective-permute-done | bytes 196640 | tf_op jit(solution)/shard_map/ppermute | solution.py:34
  419.0 10.6 %collective-permute-start.33 = (bf16[256,768]{1,0:T(8,128)(2,1)}, bf16[256,768]{1,0:T(8,128)(2,1)S(1)}, u32[]{:S(2)}, u32[]{:S(2)}) collective-permute-start(bf16[256,768]{1,0:T(8,128)(2,1)} %get-tuple-element.237), channel_id=1, source_target_pairs={{0,1},{1,2},{2,3},{3,0},{4,5},{5,6},{6,7},{7,4},{8,9},{9,10},{10,1... | collective-permute-start | bytes 1179656 | tf_op jit(solution)/shard_map/ppermute | solution.py:39
  435.6 5.7 collective-permute-done.52
  442.2 4.3 collective-permute-done.59
  480.8 5.2 collective-permute-done.68
  509.9 11.0 %collective-permute-done.70 = bf16[5,3,1,8,768]{4,3,1,0,2:T(8,128)(2,1)S(1)} collective-permute-done((bf16[5,3,1,8,768]{4,3,1,0,2:T(8,128)(2,1)S(1)}, bf16[5,3,1,8,768]{4,3,1,0,2:T(8,128)(2,1)S(1)}, u32[]{:S(2)}, u32[]{:S(2)}) %collective-permute-start.70) | collective-permute-done | bytes 184352 | tf_op jit(solution)/shard_map/ppermute | solution.py:39
  540.2 16.4 %collective-permute-done.83 = bf16[3,2,1,2,64,768]{5,4,3,1,2,0:T(8,128)(2,1)S(1)} collective-permute-done((bf16[3,2,1,2,64,768]{5,4,3,1,2,0:T(8,128)(2,1)S(1)}, bf16[3,2,1,2,64,768]{5,4,3,1,2,0:T(8,128)(2,1)S(1)}, u32[]{:S(2)}, u32[]{:S(2)}) %collective-permute-start.83) | collective-permute-done | bytes 1179680 | tf_op jit(solution)/shard_map/ppermute | solution.py:44
  558.1 6.2 collective-permute-done.79
  565.9 10.6 %collective-permute-done.84 = bf16[3,2,1,1,64,768]{5,4,3,1,2,0:T(8,128)(2,1)S(1)} collective-permute-done((bf16[3,2,1,1,64,768]{5,4,3,1,2,0:T(8,128)(2,1)S(1)}, bf16[3,2,1,1,64,768]{5,4,3,1,2,0:T(8,128)(2,1)S(1)}, u32[]{:S(2)}, u32[]{:S(2)}) %collective-permute-start.84) | collective-permute-done | bytes 589856 | tf_op jit(solution)/shard_map/ppermute | solution.py:44
  585.7 18.9 %collective-permute-done.85 = bf16[3,1,1,64,768]{4,3,0,2,1:T(8,128)(2,1)S(1)} collective-permute-done((bf16[3,1,1,64,768]{4,3,0,2,1:T(8,128)(2,1)S(1)}, bf16[3,1,1,64,768]{4,3,0,2,1:T(8,128)(2,1)S(1)}, u32[]{:S(2)}, u32[]{:S(2)}) %collective-permute-start.85) | collective-permute-done | bytes 294944 | tf_op jit(solution)/shard_map/ppermute | solution.py:39
  (735 shorter events, 408.1 us)
Async XLA Ops:
  8.5 41.0 %collective-permute-start.11 = (bf16[5,1,3,1,8,768]{5,4,3,2,1,0:T(8,128)(2,1)S(1)}, bf16[5,1,3,1,8,768]{5,4,3,2,1,0:T(8,128)(2,1)}, u32[]{:S(2)}, u32[]{:S(2)}) collective-permute-start(bf16[5,1,3,1,8,768]{5,4,3,2,1,0:T(8,128)(2,1)S(1)} %constant_dynamic-slice_fusion.11), channel_id=1, source_target_pairs={{2,0},{3,1},{0,2},{1,3},{6,4},{7,5},{4,6},{5,7},{10,8},{11,9},{8,1... | collective-permute-start | bytes 552968 | tf_op jit(solution)/shard_map/ppermute | solution.py:34
  12.6 41.4 %collective-permute-start.12 = (bf16[5,1,3,1,8,768]{5,4,3,2,1,0:T(8,128)(2,1)S(1)}, bf16[5,1,3,1,8,768]{5,4,3,2,1,0:T(8,128)(2,1)}, u32[]{:S(2)}, u32[]{:S(2)}) collective-permute-start(bf16[5,1,3,1,8,768]{5,4,3,2,1,0:T(8,128)(2,1)S(1)} %constant_dynamic-slice_fusion.11), channel_id=1, source_target_pairs={{3,0},{0,1},{1,2},{2,3},{7,4},{4,5},{5,6},{6,7},{11,8},{8,9},{9,10... | collective-permute-start | bytes 552968 | tf_op jit(solution)/shard_map/ppermute | solution.py:34
  14.2 43.7 %collective-permute-start.7 = (bf16[5,1,3,1,8,768]{5,4,3,2,1,0:T(8,128)(2,1)S(1)}, bf16[5,1,3,1,8,768]{5,4,3,2,1,0:T(8,128)(2,1)}, u32[]{:S(2)}, u32[]{:S(2)}) collective-permute-start(bf16[5,1,3,1,8,768]{5,4,3,2,1,0:T(8,128)(2,1)S(1)} %constant_dynamic-slice_fusion.11), channel_id=1, source_target_pairs={{1,0},{2,1},{3,2},{0,3},{5,4},{6,5},{7,6},{4,7},{9,8},{10,9},{11,1... | collective-permute-start | bytes 552968 | tf_op jit(solution)/shard_map/ppermute | solution.py:34
  19.5 39.3 %collective-permute-start.21 = (bf16[3,1,1,1,64,768]{5,4,0,3,2,1:T(8,128)(2,1)S(1)}, bf16[3,1,1,1,64,768]{5,4,0,3,2,1:T(8,128)(2,1)}, u32[]{:S(2)}, u32[]{:S(2)}) collective-permute-start(bf16[3,1,1,1,64,768]{5,4,0,3,2,1:T(8,128)(2,1)S(1)} %maximum_bitcast_fusion), channel_id=1, source_target_pairs={{2,0},{3,1},{0,2},{1,3},{6,4},{7,5},{4,6},{5,7},{10,8},{11,9},{8,1... | collective-permute-start | bytes 884744 | tf_op jit(solution)/shard_map/ppermute | solution.py:34
  19.6 41.8 %collective-permute-start.22 = (bf16[3,1,1,1,64,768]{5,4,0,3,2,1:T(8,128)(2,1)S(1)}, bf16[3,1,1,1,64,768]{5,4,0,3,2,1:T(8,128)(2,1)}, u32[]{:S(2)}, u32[]{:S(2)}) collective-permute-start(bf16[3,1,1,1,64,768]{5,4,0,3,2,1:T(8,128)(2,1)S(1)} %maximum_bitcast_fusion), channel_id=1, source_target_pairs={{3,0},{0,1},{1,2},{2,3},{7,4},{4,5},{5,6},{6,7},{11,8},{8,9},{9,10... | collective-permute-start | bytes 884744 | tf_op jit(solution)/shard_map/ppermute | solution.py:34
  57.8 48.0 %collective-permute-start.3 = (bf16[2048,192]{0,1:T(8,128)(2,1)}, bf16[2048,192]{0,1:T(8,128)(2,1)}, u32[]{:S(2)}, u32[]{:S(2)}) collective-permute-start(bf16[2048,192]{0,1:T(8,128)(2,1)} %copy.115), channel_id=1, source_target_pairs={{0,4},{4,0},{8,12},{12,8},{16,20},{20,16},{24,28},{28,24},{1,5},{5... | collective-permute-start | bytes 2359304 | tf_op jit(solution)/shard_map/ppermute | solution.py:44
  91.9 39.8 %collective-permute-start.24 = (bf16[3,2,1,2,64,768]{5,4,0,3,2,1:T(8,128)(2,1)}, bf16[3,2,1,2,64,768]{5,4,0,3,2,1:T(8,128)(2,1)}, u32[]{:S(2)}, u32[]{:S(2)}) collective-permute-start(bf16[3,2,1,2,64,768]{5,4,0,3,2,1:T(8,128)(2,1)} %pad_maximum_fusion.10), channel_id=1, source_target_pairs={{0,8},{4,12},{8,0},{12,4},{16,24},{20,28},{24,16},{28,20},{1,9},{5... | collective-permute-start | bytes 3538952 | tf_op jit(solution)/shard_map/ppermute | solution.py:44
  94.8 46.9 %collective-permute-start.15 = (bf16[5,2,3,4,8,768]{5,4,3,2,1,0:T(8,128)(2,1)}, bf16[5,2,3,4,8,768]{5,4,3,2,1,0:T(8,128)(2,1)}, u32[]{:S(2)}, u32[]{:S(2)}) collective-permute-start(bf16[5,2,3,4,8,768]{5,4,3,2,1,0:T(8,128)(2,1)} %pad_maximum_fusion.8), channel_id=1, source_target_pairs={{0,4},{4,0},{8,12},{12,8},{16,20},{20,16},{24,28},{28,24},{1,5},{5... | collective-permute-start | bytes 4423688 | tf_op jit(solution)/shard_map/ppermute | solution.py:44
  104.2 38.0 %collective-permute-start.10 = (bf16[5,2,3,4,8,768]{5,4,3,2,1,0:T(8,128)(2,1)}, bf16[5,2,3,4,8,768]{5,4,3,2,1,0:T(8,128)(2,1)}, u32[]{:S(2)}, u32[]{:S(2)}) collective-permute-start(bf16[5,2,3,4,8,768]{5,4,3,2,1,0:T(8,128)(2,1)} %pad_maximum_fusion.7), channel_id=1, source_target_pairs={{0,4},{4,0},{8,12},{12,8},{16,20},{20,16},{24,28},{28,24},{1,5},{5... | collective-permute-start | bytes 4423688 | tf_op jit(solution)/shard_map/ppermute | solution.py:44
  236.1 36.2 %collective-permute-start.31 = (bf16[384,192]{1,0:T(8,128)(2,1)}, bf16[384,192]{1,0:T(8,128)(2,1)S(1)}, u32[]{:S(2)}, u32[]{:S(2)}) collective-permute-start(bf16[384,192]{1,0:T(8,128)(2,1)} %get-tuple-element.275), channel_id=1, source_target_pairs={{0,3},{1,0},{2,1},{3,2},{4,7},{5,4},{6,5},{7,6},{8,11},{9,8},{10,9... | collective-permute-start | bytes 442376 | tf_op jit(solution)/shard_map/ppermute | solution.py:39
  240.3 32.1 %collective-permute-start.30 = (bf16[384,192]{1,0:T(8,128)(2,1)S(1)}, bf16[384,192]{1,0:T(8,128)(2,1)}, u32[]{:S(2)}, u32[]{:S(2)}) collective-permute-start(bf16[384,192]{1,0:T(8,128)(2,1)S(1)} %get-tuple-element.276), channel_id=1, source_target_pairs={{0,2},{1,3},{2,0},{3,1},{4,6},{5,7},{6,4},{7,5},{8,10},{9,11},{10,... | collective-permute-start | bytes 442376 | tf_op jit(solution)/shard_map/ppermute | solution.py:39
  240.3 32.1 %collective-permute-start.29 = (bf16[384,192]{1,0:T(8,128)(2,1)S(1)}, bf16[384,192]{1,0:T(8,128)(2,1)}, u32[]{:S(2)}, u32[]{:S(2)}) collective-permute-start(bf16[384,192]{1,0:T(8,128)(2,1)S(1)} %get-tuple-element.277), channel_id=1, source_target_pairs={{0,1},{1,2},{2,3},{3,0},{4,5},{5,6},{6,7},{7,4},{8,9},{9,10},{10,1... | collective-permute-start | bytes 442376 | tf_op jit(solution)/shard_map/ppermute | solution.py:39
  246.0 89.2 %collective-permute-start.39 = (bf16[512,768]{1,0:T(8,128)(2,1)}, bf16[512,768]{1,0:T(8,128)(2,1)}, u32[]{:S(2)}, u32[]{:S(2)}) collective-permute-start(bf16[512,768]{1,0:T(8,128)(2,1)} %slice.709), channel_id=1, source_target_pairs={{0,4},{4,0},{8,12},{12,8},{16,20},{20,16},{24,28},{28,24},{1,5},{5... | collective-permute-start | bytes 2359304 | tf_op jit(solution)/shard_map/ppermute | solution.py:44
  301.9 31.4 %collective-permute-start.38 = (bf16[128,768]{1,0:T(8,128)(2,1)}, bf16[128,768]{1,0:T(8,128)(2,1)}, u32[]{:S(2)}, u32[]{:S(2)}) collective-permute-start(bf16[128,768]{1,0:T(8,128)(2,1)} %get-tuple-element.257), channel_id=1, source_target_pairs={{0,3},{1,0},{2,1},{3,2},{4,7},{5,4},{6,5},{7,6},{8,11},{9,8},{10,9... | collective-permute-start | bytes 589832 | tf_op jit(solution)/shard_map/ppermute | solution.py:39
  309.7 33.5 %collective-permute-start.32 = (bf16[2048,192]{0,1:T(8,128)(2,1)}, bf16[2048,192]{0,1:T(8,128)(2,1)}, u32[]{:S(2)}, u32[]{:S(2)}) collective-permute-start(bf16[2048,192]{0,1:T(8,128)(2,1)} %copy.126), channel_id=1, source_target_pairs={{0,4},{4,0},{8,12},{12,8},{16,20},{20,16},{24,28},{28,24},{1,5},{5... | collective-permute-start | bytes 2359304 | tf_op jit(solution)/shard_map/ppermute | solution.py:44
  333.3 132.5 %collective-permute-start.67 = (bf16[5,2,3,4,8,768]{5,4,2,0,3,1:T(8,128)(2,1)}, bf16[5,2,3,4,8,768]{5,4,2,0,3,1:T(8,128)(2,1)}, u32[]{:S(2)}, u32[]{:S(2)}) collective-permute-start(bf16[5,2,3,4,8,768]{5,4,2,0,3,1:T(8,128)(2,1)} %copy.154), channel_id=1, source_target_pairs={{0,4},{4,0},{8,12},{12,8},{16,20},{20,16},{24,28},{28,24},{1,5},{5... | collective-permute-start | bytes 4423688 | tf_op jit(solution)/shard_map/ppermute | solution.py:44
  338.6 48.5 %collective-permute-start.42 = (bf16[128,768]{1,0:T(8,128)(2,1)}, bf16[128,768]{1,0:T(8,128)(2,1)}, u32[]{:S(2)}, u32[]{:S(2)}) collective-permute-start(bf16[128,768]{1,0:T(8,128)(2,1)} %get-tuple-element.252), channel_id=1, source_target_pairs={{0,3},{1,0},{2,1},{3,2},{4,7},{5,4},{6,5},{7,6},{8,11},{9,8},{10,9... | collective-permute-start | bytes 589832 | tf_op jit(solution)/shard_map/ppermute | solution.py:39
  342.6 44.6 %collective-permute-start.41 = (bf16[128,768]{1,0:T(8,128)(2,1)}, bf16[128,768]{1,0:T(8,128)(2,1)}, u32[]{:S(2)}, u32[]{:S(2)}) collective-permute-start(bf16[128,768]{1,0:T(8,128)(2,1)} %get-tuple-element.253), channel_id=1, source_target_pairs={{0,2},{1,3},{2,0},{3,1},{4,6},{5,7},{6,4},{7,5},{8,10},{9,11},{10,... | collective-permute-start | bytes 589832 | tf_op jit(solution)/shard_map/ppermute | solution.py:39
  342.6 45.1 %collective-permute-start.40 = (bf16[128,768]{1,0:T(8,128)(2,1)}, bf16[128,768]{1,0:T(8,128)(2,1)}, u32[]{:S(2)}, u32[]{:S(2)}) collective-permute-start(bf16[128,768]{1,0:T(8,128)(2,1)} %get-tuple-element.251), channel_id=1, source_target_pairs={{0,1},{1,2},{2,3},{3,0},{4,5},{5,6},{6,7},{7,4},{8,9},{9,10},{10,1... | collective-permute-start | bytes 589832 | tf_op jit(solution)/shard_map/ppermute | solution.py:39
  383.9 67.9 %collective-permute-start.35 = (bf16[256,768]{1,0:T(8,128)(2,1)}, bf16[256,768]{1,0:T(8,128)(2,1)}, u32[]{:S(2)}, u32[]{:S(2)}) collective-permute-start(bf16[256,768]{1,0:T(8,128)(2,1)} %get-tuple-element.238), channel_id=1, source_target_pairs={{0,3},{1,0},{2,1},{3,2},{4,7},{5,4},{6,5},{7,6},{8,11},{9,8},{10,9... | collective-permute-start | bytes 1179656 | tf_op jit(solution)/shard_map/ppermute | solution.py:39
  411.0 41.4 %collective-permute-start.34 = (bf16[256,768]{1,0:T(8,128)(2,1)}, bf16[256,768]{1,0:T(8,128)(2,1)S(1)}, u32[]{:S(2)}, u32[]{:S(2)}) collective-permute-start(bf16[256,768]{1,0:T(8,128)(2,1)} %get-tuple-element.239), channel_id=1, source_target_pairs={{0,2},{1,3},{2,0},{3,1},{4,6},{5,7},{6,4},{7,5},{8,10},{9,11},{10,... | collective-permute-start | bytes 1179656 | tf_op jit(solution)/shard_map/ppermute | solution.py:39
  419.0 33.5 %collective-permute-start.33 = (bf16[256,768]{1,0:T(8,128)(2,1)}, bf16[256,768]{1,0:T(8,128)(2,1)S(1)}, u32[]{:S(2)}, u32[]{:S(2)}) collective-permute-start(bf16[256,768]{1,0:T(8,128)(2,1)} %get-tuple-element.237), channel_id=1, source_target_pairs={{0,1},{1,2},{2,3},{3,0},{4,5},{5,6},{6,7},{7,4},{8,9},{9,10},{10,1... | collective-permute-start | bytes 1179656 | tf_op jit(solution)/shard_map/ppermute | solution.py:39
  451.8 74.6 %collective-permute-start.82 = (bf16[3,2,1,4,64,768]{5,4,3,1,2,0:T(8,128)(2,1)}, bf16[3,2,1,4,64,768]{5,4,3,1,2,0:T(8,128)(2,1)}, u32[]{:S(2)}, u32[]{:S(2)}) collective-permute-start(bf16[3,2,1,4,64,768]{5,4,3,1,2,0:T(8,128)(2,1)} %get-tuple-element.219), channel_id=1, source_target_pairs={{0,4},{4,0},{8,12},{12,8},{16,20},{20,16},{24,28},{28,24},{1,5},{5... | collective-permute-start | bytes 7077896 | tf_op jit(solution)/shard_map/ppermute | solution.py:44
  452.4 80.4 %collective-permute-start.78 = (bf16[3,2,1,4,64,768]{5,4,0,3,2,1:T(8,128)(2,1)}, bf16[3,2,1,4,64,768]{5,4,0,3,2,1:T(8,128)(2,1)}, u32[]{:S(2)}, u32[]{:S(2)}) collective-permute-start(bf16[3,2,1,4,64,768]{5,4,0,3,2,1:T(8,128)(2,1)} %copy.156), channel_id=1, source_target_pairs={{0,4},{4,0},{8,12},{12,8},{16,20},{20,16},{24,28},{28,24},{1,5},{5... | collective-permute-start | bytes 7077896 | tf_op jit(solution)/shard_map/ppermute | solution.py:44
  (211 other events, 1967.9 us)

commit v2 on v1

--- a/solution.py
+++ b/solution.py
@@ -87,21 +87,30 @@
     return (low.astype(F32) + flip_bit(high, bit).astype(F32)).astype(BF)
 
 
-def reduce_grads(grads):
+def reduce_stages(grads):
     up, down = bit_lists()
+    grads = fold(grads, 0, 3)
+    yield grads
     first, second = grads[:, :2], grads[:, 2:]
-    for bit in [0] + down:
-        first = fold(first, bit, 3)
-    for bit in [0] + up:
-        second = fold(second, bit, 3)
+    for one, two in zip(down, up):
+        first = fold(first, one, 3)
+        second = fold(second, two, 3)
+        yield (first, second)
     total = first[:, 0].astype(F32)
     for step, piece in ((1, first[:, 1]), (2, second[:, 0]), (3, second[:, 1])):
         total = total + to_ahead(piece, step).astype(F32)
     total = total.astype(BF)
+    yield total
     half = total.shape[-1] // 2
-    left = spread(total[..., :half], up + [0], 2)
-    right = spread(total[..., half:], down + [0], 2)
-    return (left, right)
+    left, right = total[..., :half], total[..., half:]
+    for one, two in zip(up + [0], down + [0]):
+        left = spread(left, [one], 2)
+        right = spread(right, [two], 2)
+        yield (left, right)
+
+
+def after(value, *others):
+    return lax.optimization_barrier((value, others))[0]
 
 
 def slice_hot(order, parts, rows, rank):
@@ -691,7 +700,6 @@
     d_gate, d_upper = gelu_pull(d_hidden)
     d_gate = d_gate.astype(BF)
     d_upper = d_upper.astype(BF)
-    d_n3 = mm(d_gate, wg_t) + mm(d_upper, wu_t)
     ffn_grads = jnp.stack(
         [
             mm(d_gate, n3, TN).astype(BF),
@@ -699,12 +707,16 @@
             mm(hidden, g3_low, TN).astype(BF),
         ]
     ).reshape(3, ranks, 1, data_size, hidden_rows, width)
-    ffn_left, ffn_right = reduce_grads(ffn_grads)
+    ffn_steps = reduce_stages(ffn_grads)
+    ffn_core = next(ffn_steps)
+    d_gate, d_upper = after((d_gate, d_upper), ffn_grads)
+    d_n3 = mm(d_gate, wg_t) + mm(d_upper, wu_t)
     back3, gain_ffn_part = norm_back(x2, gain_ffn, d_n3)
     g2 = g3 + back3
 
     g2_low = g2.astype(BF)
-    d_mixed_c = mm(g2_low, co_full, NT).astype(BF)
+    d_mixed_c = after(mm(g2_low, co_full, NT).astype(BF), ffn_core)
+    ffn_plane = next(ffn_steps)
     d_query_c, d_key_c, d_value_c = pl.pallas_call(
         cross_back,
         out_shape=shaped(
@@ -731,75 +743,6 @@
     g1 = g2 + back2
     g1_low = g1.astype(BF)
 
-    d_mixed_s = mm(g1_low, wo_full, NT).astype(BF)
-    held, pick = rows_to_heads(d_mixed_s)
-    place = (pick[None, :] == jnp.arange(ranks)[:, None]).astype(BF)
-    ordered = jnp.einsum("ns,src->nrc", place, held, preferred_element_type=F32).astype(BF)
-    do_prompt = ordered[:, :share].reshape(PROMPT, cols)
-    do_cont = ordered[:, share:].reshape(rows_late, cols)
-
-    key_far_t = key_far.T
-    (dq_cont, dk_cont, dv_cont, dk_near, dv_near, dk_far, dv_far, line_cont) = run_heads(
-        cont_back, heads, [slots], [line],
-        [ok_cols, query_s, key_s, key_t, value_s, key_far, key_far_t, value_far, do_cont, lse_cont],
-        shaped(
-            ((rows_late, cols), BF), ((rows_late, cols), BF), ((rows_late, cols), BF),
-            ((PROMPT, cols), F32), ((PROMPT, cols), F32),
-            ((PROMPT, cols), BF), ((PROMPT, cols), BF), ((heads, 1, LINE), F32),
-        ),
-        [slab_t, slab_t, pltpu.VMEM((cont_count, cols, CONT_LEN), F32)]
-        + [pltpu.VMEM((rows_late, cols), F32)] * 2 + [pltpu.VMEM((PROMPT, cols), F32)] * 2,
-        (7,), rows_late * DIST, "cont_back",
-    )
-    lent = flip_bit(jnp.concatenate([dk_far, dv_far], axis=0), 0)
-    dq_prompt, dk_prompt, dv_prompt, line_prompt = run_heads(
-        prompt_back, heads, [], [line],
-        [query_s, key_s, key_t, value_s, do_prompt, lse_prompt],
-        shaped(
-            ((PROMPT, cols), BF), ((PROMPT, cols), F32), ((PROMPT, cols), F32),
-            ((heads, 1, LINE), F32),
-        ),
-        [slab_t, slab_t, pltpu.VMEM((cols, PROMPT), F32)], (3,),
-        PROMPT * PROMPT * 5 // 8, "prompt_back",
-    )
-    dk_prompt = (dk_prompt + dk_near + lent[:PROMPT].astype(F32)).astype(BF)
-    dv_prompt = (dv_prompt + dv_near + lent[PROMPT:].astype(F32)).astype(BF)
-
-    def three(q, k, v):
-        return mm(q, w_q, NT) + mm(k, w_k, NT) + mm(v, w_v, NT)
-
-    def scatter_rows(block, rows):
-        total = lax.dynamic_slice_in_dim(block, tensor_rank * rows, rows, 0).astype(F32)
-        for step in range(1, ranks):
-            dest = (tensor_rank + step) % ranks
-            piece = lax.dynamic_slice_in_dim(block, dest * rows, rows, 0)
-            total = total + to_ahead(piece, step).astype(F32)
-        return total
-
-    part_cont = three(dq_cont, dk_cont, dv_cont).astype(BF)
-    part_prompt = three(dq_prompt, dk_prompt, dv_prompt).astype(BF)
-    d_n1 = jnp.concatenate([scatter_rows(part_prompt, share), scatter_rows(part_cont, CONT_LEN)])
-    back1, ignored = norm_back(x_own, gain_self, d_n1)
-    grad_x = g1 + back1
-    unit = stream * norm_scale(stream)
-    gain_self_part = jnp.sum(part_prompt.astype(F32) * unit[:PROMPT], axis=0) + jnp.sum(
-        part_cont.astype(F32) * unit[PROMPT:], axis=0
-    )
-
-    enc_part = mm(d_key_c, ck_t) + mm(d_value_c, cv_t)
-    enc_sum = (enc_part[:ENC_LEN] + flip_bit(enc_part[ENC_LEN:].astype(BF), 0).astype(F32)).astype(
-        BF
-    )
-    enc_rows = ENC_LEN // ranks
-    enc_own = scatter_rows(enc_sum, enc_rows).astype(BF)
-    enc_all = jnp.concatenate(
-        [enc_own] + [from_ahead(enc_own, step) for step in range(1, ranks)]
-    )
-    enc_place = jnp.arange(ENC_LEN)
-    enc_from = (tensor_rank + enc_place // enc_rows) % ranks * enc_rows + enc_place % enc_rows
-    enc_hot = (enc_from[:, None] == enc_place[None, :]).astype(BF)
-    grad_enc = mm(enc_hot, enc_all, TN)
-
     grad_wo_part = mm(mixed_self, g1_low, TN).astype(BF).reshape(ranks, cols, width)
     grad_wo_part = jnp.einsum(
         "zrn,znd->zrd", hot_four, grad_wo_part, preferred_element_type=F32
@@ -813,7 +756,86 @@
             mm(mixed_cross, g2_low, TN).astype(BF),
         ]
     ).reshape(5, ranks, heads, data_size, head_rows, width)
-    attn_left, attn_right = reduce_grads(attn_grads)
+    attn_steps = reduce_stages(attn_grads)
+    attn_core = next(attn_steps)
+    d_mixed_s = after(mm(g1_low, wo_full, NT).astype(BF), ffn_plane)
+    ffn_line = next(ffn_steps)
+    held, pick = rows_to_heads(d_mixed_s)
+    place = (pick[None, :] == jnp.arange(ranks)[:, None]).astype(BF)
+    ordered = jnp.einsum("ns,src->nrc", place, held, preferred_element_type=F32).astype(BF)
+    do_prompt = ordered[:, :share].reshape(PROMPT, cols)
+    do_cont = ordered[:, share:].reshape(rows_late, cols)
+
+    do_cont = after(do_cont, ffn_line, attn_core)
+    ffn_tensor = next(ffn_steps)
+    attn_plane = next(attn_steps)
+    key_far_t = key_far.T
+    (dq_cont, dk_cont, dv_cont, dk_near, dv_near, dk_far, dv_far, line_cont) = run_heads(
+        cont_back, heads, [slots], [line],
+        [ok_cols, query_s, key_s, key_t, value_s, key_far, key_far_t, value_far, do_cont, lse_cont],
+        shaped(
+            ((rows_late, cols), BF), ((rows_late, cols), BF), ((rows_late, cols), BF),
+            ((PROMPT, cols), F32), ((PROMPT, cols), F32),
+            ((PROMPT, cols), BF), ((PROMPT, cols), BF), ((heads, 1, LINE), F32),
+        ),
+        [slab_t, slab_t, pltpu.VMEM((cont_count, cols, CONT_LEN), F32)]
+        + [pltpu.VMEM((rows_late, cols), F32)] * 2 + [pltpu.VMEM((PROMPT, cols), F32)] * 2,
+        (7,), rows_late * DIST, "cont_back",
+    )
+    lent = flip_bit(jnp.concatenate([dk_far, dv_far], axis=0), 0)
+    do_prompt = after(do_prompt, dq_cont, ffn_tensor, attn_plane)
+    ffn_back = next(ffn_steps)
+    attn_line = next(attn_steps)
+    dq_prompt, dk_prompt, dv_prompt, line_prompt = run_heads(
+        prompt_back, heads, [], [line],
+        [query_s, key_s, key_t, value_s, do_prompt, lse_prompt],
+        shaped(
+            ((PROMPT, cols), BF), ((PROMPT, cols), F32), ((PROMPT, cols), F32),
+            ((heads, 1, LINE), F32),
+        ),
+        [slab_t, slab_t, pltpu.VMEM((cols, PROMPT), F32)], (3,),
+        PROMPT * PROMPT * 5 // 8, "prompt_back",
+    )
+    dk_prompt = (dk_prompt + dk_near + lent[:PROMPT].astype(F32)).astype(BF)
+    dv_prompt = (dv_prompt + dv_near + lent[PROMPT:].astype(F32)).astype(BF)
+
+    def three(q, k, v):
+        return mm(q, w_q, NT) + mm(k, w_k, NT) + mm(v, w_v, NT)
+
+    def scatter_rows(block, rows):
+        total = lax.dynamic_slice_in_dim(block, tensor_rank * rows, rows, 0).astype(F32)
+        for step in range(1, ranks):
+            dest = (tensor_rank + step) % ranks
+            piece = lax.dynamic_slice_in_dim(block, dest * rows, rows, 0)
+            total = total + to_ahead(piece, step).astype(F32)
+        return total
+
+    part_cont = three(dq_cont, dk_cont, dv_cont).astype(BF)
+    part_prompt = three(dq_prompt, dk_prompt, dv_prompt).astype(BF)
+    d_n1 = jnp.concatenate([scatter_rows(part_prompt, share), scatter_rows(part_cont, CONT_LEN)])
+    back1, ignored = norm_back(x_own, gain_self, d_n1)
+    grad_x = g1 + back1
+    unit = stream * norm_scale(stream)
+    gain_self_part = jnp.sum(part_prompt.astype(F32) * unit[:PROMPT], axis=0) + jnp.sum(
+        part_cont.astype(F32) * unit[PROMPT:], axis=0
+    )
+
+    enc_part = mm(d_key_c, ck_t) + mm(d_value_c, cv_t)
+    enc_sum = (enc_part[:ENC_LEN] + flip_bit(enc_part[ENC_LEN:].astype(BF), 0).astype(F32)).astype(
+        BF
+    )
+    enc_rows = ENC_LEN // ranks
+    enc_own = scatter_rows(enc_sum, enc_rows).astype(BF)
+    enc_all = jnp.concatenate(
+        [enc_own] + [from_ahead(enc_own, step) for step in range(1, ranks)]
+    )
+    enc_place = jnp.arange(ENC_LEN)
+    enc_from = (tensor_rank + enc_place // enc_rows) % ranks * enc_rows + enc_place % enc_rows
+    enc_hot = (enc_from[:, None] == enc_place[None, :]).astype(BF)
+    grad_enc = mm(enc_hot, enc_all, TN)
+
+    ffn_left, ffn_right = list(ffn_steps)[-1]
+    attn_left, attn_right = list(attn_steps)[-1]
 
     def finish(left, right, hots, matrix, transposed):
         halves = [

time: 646 us -> 589 us (0.912)
  waiting for transfers between devices: 155 us -> 116 us
  matrix products: 96.8 us -> 84 us
  local copies, waits for them, and re-layouts: 104 us -> 95.1 us
    ppermute x60 -> x58, waiting for transfers between devices: 111 us -> 66.2 us  [flip_bit(): return lax.ppermute(block, axis, [(i, i ^ 1 << bit) for i in range(count)])]
    dot_general x60, matrix products: 93.3 us -> 81.6 us  [mm(): return lax.dot_general(left, right, dims, preferred_element_type=F32)]
    ppermute x18, waiting for transfers between devices: 35.7 us -> 45.4 us  [to_ahead(): lax.ppermute(block, 'tensor', [(i, (i + step) % count) for i in range(cou...]
    slice x14 -> x13, local copies, waits for them, and re-layouts: 7.42 us -> 13.6 us  [fold(): high = lax.slice_in_dim(block, half, 2 * half, axis=axis)]
    ppermute x60 -> x58, starting transfers between devices: 42.8 us -> 44.9 us  [flip_bit(): return lax.ppermute(block, axis, [(i, i ^ 1 << bit) for i in range(count)])]
    convert_element_type x18 -> x15, other arithmetic: 16 us -> 17.2 us  [fold(): return (low.astype(F32) + flip_bit(high, bit).astype(F32)).astype(BF)]
    unnamed x303 -> x336, local copies, waits for them, and re-layouts: 36 us -> 35.8 us
  transfers between devices with their start and end apart: 93 -> 91, of which waited for: 34 -> 26; matrix products, arithmetic and copies ran while one was open for 34% -> 33% of each run, Pallas kernels for 9% -> 10%
where the time goes in v2:
time: 589 us; the launch traced here: 581 us
  waiting for transfers between devices  116 us (20%)
  starting transfers between devices  113 us (19%)
  local copies, waits for them, and re-layouts  95.1 us (16%)
  other arithmetic  92.8 us (16%)
  matrix products  84 us (14%)
  Pallas kernels  73.6 us (12%)
  between operations  6.31 us (1%)
    dot_general x60, matrix products, mm(): return lax.dot_general(left, right, dims, preferred_element_type=F32)  81.6 us
    ppermute x58, waiting for transfers between devices, flip_bit(): return lax.ppermute(block, axis, [(i, i ^ 1 << bit) for i in range(count)])  66.2 us
    pallas_call x4, Pallas kernels, run_heads(): pl.pallas_call(kernel, out_shape=outs, grid_spec=pltpu.PrefetchScalarGrid...  48.4 us
    ppermute x18, waiting for transfers between devices, to_ahead(): lax.ppermute(block, 'tensor', [(i, (i + step) % count) for i in range(cou...  45.4 us
    ppermute x58, starting transfers between devices, flip_bit(): return lax.ppermute(block, axis, [(i, i ^ 1 << bit) for i in range(count)])  44.9 us
    ppermute x18, starting transfers between devices, to_ahead(): lax.ppermute(block, 'tensor', [(i, (i + step) % count) for i in range(cou...  41 us
    unnamed x336, local copies, waits for them, and re-layouts  35.8 us
    ppermute x15, starting transfers between devices, from_ahead(): lax.ppermute(block, 'tensor', [((i + step) % count, i) for i in range(cou...  27.3 us
  transfers between devices with their start and end apart: 91, of which 26 were waited for; matrix products, arithmetic and copies ran while one was open for 33% of the time, Pallas kernels for 10%

profile of v2, /device:TPU:0, one launch (start us, length us, event | category | flops | bytes accessed | tf_op | source)
XLA Modules:
  0.0 580.7 jit_solution(15105297726004532867)
XLA Ops:
  8.5 4.1 collective-permute-start.11
  34.3 8.7 %prompt_fwd.1 = (bf16[1024,192]{1,0:T(8,128)(2,1)}, f32[1024,192]{1,0:T(8,128)}) custom-call(f32[3,1,1408]{2,1,0:T(1,128)} %reshape.707.line_ref, bf16[1536,192]{1,0:T(8,128)(2,1)} %fusion.10.q_ref, bf16[1536,192]{1,0:T(8,128)(2,1)} %copy-done.52, bf16[1536,192]{1,0:T(8,128)(2,1)} %copy-done.88), custom_call_target="tpu_custom_call" | custom-call | flops 2013265920 | bytes 2966016 | tf_op jit(solution)/shard_map/prompt_fwd/pallas_call | solution.py:472
  70.0 14.6 %collective-permute-done.27 = f32[8,128]{1,0:T(8,128)S(1)} collective-permute-done((f32[8,128]{1,0:T(8,128)S(1)}, f32[8,128]{1,0:T(8,128)S(1)}, u32[]{:S(2)}, u32[]{:S(2)}) %collective-permute-start.27) | collective-permute-done | bytes 4128 | tf_op jit(solution)/shard_map/ppermute | solution.py:44
  92.7 8.1 %collective-permute-done.18 = bf16[3,2,1,1,64,768]{5,4,0,3,2,1:T(8,128)(2,1)S(1)} collective-permute-done((bf16[3,2,1,1,64,768]{5,4,0,3,2,1:T(8,128)(2,1)S(1)}, bf16[3,2,1,1,64,768]{5,4,0,3,2,1:T(8,128)(2,1)S(1)}, u32[]{:S(2)}, u32[]{:S(2)}) %collective-permute-start.18) | collective-permute-done | bytes 589856 | tf_op jit(solution)/shard_map/ppermute | solution.py:44
  114.4 9.3 %cont_fwd.1 = (bf16[512,192]{1,0:T(8,128)(2,1)}, f32[512,192]{1,0:T(8,128)}) custom-call(s32[4]{0:T(128)} %select_reduce_fusion.slot_ref, f32[3,1,1408]{2,1,0:T(1,128)} %reshape.707.line_ref, f32[4,128,128]{2,1,0:T(8,128)} %broadcast_in_dim.209.ok_ref, bf16[1536,192]{1,0:T(8,128)(2,1)} %fusion.10.q_ref, bf16[1536,192]{1,0:T(8,128)(2,1)} %copy-done.52, ...), custom_call_target="tpu_custom_call" | custom-call | flops 1811939328 | bytes 3424768 | tf_op jit(solution)/shard_map/cont_fwd/pallas_call | solution.py:472
  156.0 10.6 %cross_fwd.1 = (bf16[384,768]{1,0:T(8,128)(2,1)}, f32[384,768]{1,0:T(8,128)}) custom-call(s32[1]{0:T(128)} %dynamic_slice.95.far_ref, bf16[384,768]{1,0:T(8,128)(2,1)} %fusion.19.q_ref, bf16[1024,768]{1,0:T(8,128)(2,1)} %convolution_convert_fusion.7.k_ref, bf16[1024,768]{1,0:T(8,128)(2,1)} %convolution_convert_fusion.6.v_ref), custom_call_target="tpu_custom_call" | custom-call | flops 2415919104 | bytes 3735552 | tf_op jit(solution)/shard_map/cross_fwd/pallas_call | solution.py:659
  170.3 4.8 maximum_maximum_fusion
  186.9 4.1 fusion.1
  198.2 8.4 %pad_maximum_fusion = bf16[3,4,1,8,64,768]{5,4,3,1,2,0:T(8,128)(2,1)} fusion(bf16[1,4,1,8,64,768]{5,4,3,1,2,0:T(8,128)(2,1)} %bitcast.215, bf16[1,4,1,8,64,768]{5,4,3,1,2,0:T(8,128)(2,1)} %bitcast.216, bf16[1,4,1,8,64,768]{5,4,3,1,2,0:T(8,128)(2,1)} %bitcast.217), kind=kLoop, calls=%fused_computation.1 | loop fusion | flops 9437184 | bytes 18874368 | tf_op jit(solution)/shard_map/stack | solution.py:703
  206.6 5.1 slice.537
  228.4 4.1 add_convert_fusion
  235.7 14.5 %cross_back.1 = (bf16[384,768]{1,0:T(8,128)(2,1)}, bf16[1024,768]{1,0:T(8,128)(2,1)}, bf16[1024,768]{1,0:T(8,128)(2,1)}) custom-call(s32[1]{0:T(128)} %dynamic_slice.95.far_ref, bf16[384,768]{1,0:T(8,128)(2,1)} %fusion.19.q_ref, bf16[1024,768]{1,0:T(8,128)(2,1)} %convolution_convert_fusion.7.k_ref, bf16[1024,768]{1,0:T(8,128)(2,1)} %convolution_convert_fusion.6.v_ref, ...), custom_call_target="tpu_custom_call" | custom-call | flops 6039797760 | bytes 3735552 | tf_op jit(solution)/shard_map/cross_back/pallas_call | solution.py:720
  275.0 11.7 %collective-permute-done.31 = bf16[3,2,1,2,64,768]{5,4,3,1,2,0:T(8,128)(2,1)S(1)} collective-permute-done((bf16[3,2,1,2,64,768]{5,4,3,1,2,0:T(8,128)(2,1)S(1)}, bf16[3,2,1,2,64,768]{5,4,3,1,2,0:T(8,128)(2,1)S(1)}, u32[]{:S(2)}, u32[]{:S(2)}) %collective-permute-start.31) | collective-permute-done | bytes 1179680 | tf_op jit(solution)/shard_map/ppermute | solution.py:44
  289.9 4.2 collective-permute-start.53
  295.1 4.3 collective-permute-done.53
  300.9 9.2 %collective-permute-done.52 = bf16[128,768]{1,0:T(8,128)(2,1)S(1)} collective-permute-done((bf16[128,768]{1,0:T(8,128)(2,1)S(1)}, bf16[128,768]{1,0:T(8,128)(2,1)S(1)}, u32[]{:S(2)}, u32[]{:S(2)}) %collective-permute-start.52) | collective-permute-done | bytes 196640 | tf_op jit(solution)/shard_map/ppermute | solution.py:39
  320.4 18.7 %collective-permute-start.39 = (bf16[3,1,1,64,768]{4,3,0,2,1:T(8,128)(2,1)S(1)}, bf16[3,1,1,64,768]{4,3,0,2,1:T(8,128)(2,1)S(1)}, u32[]{:S(2)}, u32[]{:S(2)}) collective-permute-start(bf16[3,1,1,64,768]{4,3,0,2,1:T(8,128)(2,1)S(1)} %get-tuple-element.286), channel_id=1, source_target_pairs={{0,2},{1,3},{2,0},{3,1},{4,6},{5,7},{6,4},{7,5},{8,10},{9,11},{10,... | collective-permute-start | bytes 884744 | tf_op jit(solution)/shard_map/ppermute | solution.py:39
  346.9 14.0 %collective-permute-done.39 = bf16[3,1,1,64,768]{4,3,0,2,1:T(8,128)(2,1)S(1)} collective-permute-done((bf16[3,1,1,64,768]{4,3,0,2,1:T(8,128)(2,1)S(1)}, bf16[3,1,1,64,768]{4,3,0,2,1:T(8,128)(2,1)S(1)}, u32[]{:S(2)}, u32[]{:S(2)}) %collective-permute-start.39) | collective-permute-done | bytes 294944 | tf_op jit(solution)/shard_map/ppermute | solution.py:39
  363.1 10.1 %collective-permute-done.33 = bf16[384,192]{1,0:T(8,128)(2,1)S(1)} collective-permute-done((bf16[384,192]{1,0:T(8,128)(2,1)S(1)}, bf16[384,192]{1,0:T(8,128)(2,1)S(1)}, u32[]{:S(2)}, u32[]{:S(2)}) %collective-permute-start.33) | collective-permute-done | bytes 147488 | tf_op jit(solution)/shard_map/ppermute | solution.py:39
  379.5 4.2 collective-permute-done.89
  386.0 5.0 add_convert_fusion.1
  391.9 15.5 %cont_back.1 = (bf16[512,192]{1,0:T(8,128)(2,1)}, bf16[512,192]{1,0:T(8,128)(2,1)}, bf16[512,192]{1,0:T(8,128)(2,1)}, f32[1024,192]{1,0:T(8,128)}, f32[1024,192]...) custom-call(s32[4]{0:T(128)} %select_reduce_fusion.slot_ref, ...), custom_call_target="tpu_custom_call" | custom-call | flops 4529848320 | bytes 7373824 | tf_op jit(solution)/shard_map/cont_back/pallas_call | solution.py:472
  443.1 14.9 %prompt_back.1 = (bf16[1024,192]{1,0:T(8,128)(2,1)}, f32[1024,192]{1,0:T(8,128)}, f32[1024,192]{1,0:T(8,128)}, f32[3,1,1408]{2,1,0:T(1,128)}) custom-call(f32[3,1,1408]{2,1,0:T(1,128)} %reshape.707.line_ref, bf16[1536,192]{1,0:T(8,128)(2,1)} %fusion.10.q_ref, bf16[1536,192]{1,0:T(8,128)(2,1)} %copy-done.52, bf16[192,1536]{1,0:T(8,128)(2,1)} %copy.134.kt_ref, ...), custom_call_target="tpu_custom_call" | custom-call | flops 5033164800 | bytes 5538816 | tf_op jit(solution)/shard_map/prompt_back/pallas_call | solution.py:472
  537.1 7.7 %collective-permute-done.45 = bf16[256,768]{1,0:T(8,128)(2,1)} collective-permute-done((bf16[256,768]{1,0:T(8,128)(2,1)}, bf16[256,768]{1,0:T(8,128)(2,1)}, u32[]{:S(2)}, u32[]{:S(2)}) %collective-permute-start.45) | collective-permute-done | bytes 393248 | tf_op jit(solution)/shard_map/ppermute | solution.py:39
  (760 shorter events, 358.2 us)
Async XLA Ops:
  8.5 38.1 %collective-permute-start.11 = (bf16[5,1,3,1,8,768]{5,4,3,2,1,0:T(8,128)(2,1)S(1)}, bf16[5,1,3,1,8,768]{5,4,3,2,1,0:T(8,128)(2,1)}, u32[]{:S(2)}, u32[]{:S(2)}) collective-permute-start(bf16[5,1,3,1,8,768]{5,4,3,2,1,0:T(8,128)(2,1)S(1)} %constant_dynamic-slice_fusion.11), channel_id=1, source_target_pairs={{2,0},{3,1},{0,2},{1,3},{6,4},{7,5},{4,6},{5,7},{10,8},{11,9},{8,1... | collective-permute-start | bytes 552968 | tf_op jit(solution)/shard_map/ppermute | solution.py:34
  12.6 38.4 %collective-permute-start.12 = (bf16[5,1,3,1,8,768]{5,4,3,2,1,0:T(8,128)(2,1)S(1)}, bf16[5,1,3,1,8,768]{5,4,3,2,1,0:T(8,128)(2,1)}, u32[]{:S(2)}, u32[]{:S(2)}) collective-permute-start(bf16[5,1,3,1,8,768]{5,4,3,2,1,0:T(8,128)(2,1)S(1)} %constant_dynamic-slice_fusion.11), channel_id=1, source_target_pairs={{3,0},{0,1},{1,2},{2,3},{7,4},{4,5},{5,6},{6,7},{11,8},{8,9},{9,10... | collective-permute-start | bytes 552968 | tf_op jit(solution)/shard_map/ppermute | solution.py:34
  14.2 41.2 %collective-permute-start.7 = (bf16[5,1,3,1,8,768]{5,4,3,2,1,0:T(8,128)(2,1)S(1)}, bf16[5,1,3,1,8,768]{5,4,3,2,1,0:T(8,128)(2,1)S(1)}, u32[]{:S(2)}, u32[]{:S(2)}) collective-permute-start(bf16[5,1,3,1,8,768]{5,4,3,2,1,0:T(8,128)(2,1)S(1)} %constant_dynamic-slice_fusion.11), channel_id=1, source_target_pairs={{1,0},{2,1},{3,2},{0,3},{5,4},{6,5},{7,6},{4,7},{9,8},{10,9},{11,1... | collective-permute-start | bytes 552968 | tf_op jit(solution)/shard_map/ppermute | solution.py:34
  19.5 35.9 %collective-permute-start.21 = (bf16[3,1,1,1,64,768]{5,4,0,3,2,1:T(8,128)(2,1)S(1)}, bf16[3,1,1,1,64,768]{5,4,0,3,2,1:T(8,128)(2,1)}, u32[]{:S(2)}, u32[]{:S(2)}) collective-permute-start(bf16[3,1,1,1,64,768]{5,4,0,3,2,1:T(8,128)(2,1)S(1)} %maximum_bitcast_fusion), channel_id=1, source_target_pairs={{2,0},{3,1},{0,2},{1,3},{6,4},{7,5},{4,6},{5,7},{10,8},{11,9},{8,1... | collective-permute-start | bytes 884744 | tf_op jit(solution)/shard_map/ppermute | solution.py:34
  19.6 38.4 %collective-permute-start.22 = (bf16[3,1,1,1,64,768]{5,4,0,3,2,1:T(8,128)(2,1)S(1)}, bf16[3,1,1,1,64,768]{5,4,0,3,2,1:T(8,128)(2,1)}, u32[]{:S(2)}, u32[]{:S(2)}) collective-permute-start(bf16[3,1,1,1,64,768]{5,4,0,3,2,1:T(8,128)(2,1)S(1)} %maximum_bitcast_fusion), channel_id=1, source_target_pairs={{3,0},{0,1},{1,2},{2,3},{7,4},{4,5},{5,6},{6,7},{11,8},{8,9},{9,10... | collective-permute-start | bytes 884744 | tf_op jit(solution)/shard_map/ppermute | solution.py:34
  55.4 47.1 %collective-permute-start.3 = (bf16[2048,192]{0,1:T(8,128)(2,1)}, bf16[2048,192]{0,1:T(8,128)(2,1)}, u32[]{:S(2)}, u32[]{:S(2)}) collective-permute-start(bf16[2048,192]{0,1:T(8,128)(2,1)} %copy.115), channel_id=1, source_target_pairs={{0,4},{4,0},{8,12},{12,8},{16,20},{20,16},{24,28},{28,24},{1,5},{5... | collective-permute-start | bytes 2359304 | tf_op jit(solution)/shard_map/ppermute | solution.py:44
  88.5 38.3 %collective-permute-start.24 = (bf16[3,2,1,2,64,768]{5,4,0,3,2,1:T(8,128)(2,1)}, bf16[3,2,1,2,64,768]{5,4,0,3,2,1:T(8,128)(2,1)}, u32[]{:S(2)}, u32[]{:S(2)}) collective-permute-start(bf16[3,2,1,2,64,768]{5,4,0,3,2,1:T(8,128)(2,1)} %pad_maximum_fusion.10), channel_id=1, source_target_pairs={{0,8},{4,12},{8,0},{12,4},{16,24},{20,28},{24,16},{28,20},{1,9},{5... | collective-permute-start | bytes 3538952 | tf_op jit(solution)/shard_map/ppermute | solution.py:44
  91.4 45.4 %collective-permute-start.15 = (bf16[5,2,3,4,8,768]{5,4,3,2,1,0:T(8,128)(2,1)}, bf16[5,2,3,4,8,768]{5,4,3,2,1,0:T(8,128)(2,1)}, u32[]{:S(2)}, u32[]{:S(2)}) collective-permute-start(bf16[5,2,3,4,8,768]{5,4,3,2,1,0:T(8,128)(2,1)} %pad_maximum_fusion.8), channel_id=1, source_target_pairs={{0,4},{4,0},{8,12},{12,8},{16,20},{20,16},{24,28},{28,24},{1,5},{5... | collective-permute-start | bytes 4423688 | tf_op jit(solution)/shard_map/ppermute | solution.py:44
  100.8 36.5 %collective-permute-start.10 = (bf16[5,2,3,4,8,768]{5,4,3,2,1,0:T(8,128)(2,1)}, bf16[5,2,3,4,8,768]{5,4,3,2,1,0:T(8,128)(2,1)}, u32[]{:S(2)}, u32[]{:S(2)}) collective-permute-start(bf16[5,2,3,4,8,768]{5,4,3,2,1,0:T(8,128)(2,1)} %pad_maximum_fusion.7), channel_id=1, source_target_pairs={{0,4},{4,0},{8,12},{12,8},{16,20},{20,16},{24,28},{28,24},{1,5},{5... | collective-permute-start | bytes 4423688 | tf_op jit(solution)/shard_map/ppermute | solution.py:44
  102.5 28.3 %collective-permute-start.19 = (bf16[3,2,1,2,64,768]{5,4,0,3,2,1:T(8,128)(2,1)}, bf16[3,2,1,2,64,768]{5,4,0,3,2,1:T(8,128)(2,1)}, u32[]{:S(2)}, u32[]{:S(2)}) collective-permute-start(bf16[3,2,1,2,64,768]{5,4,0,3,2,1:T(8,128)(2,1)} %pad_maximum_fusion.9), channel_id=1, source_target_pairs={{0,16},{4,20},{8,24},{12,28},{16,0},{20,4},{24,8},{28,12},{1,17},{... | collective-permute-start | bytes 3538952 | tf_op jit(solution)/shard_map/ppermute | solution.py:44
  257.0 37.0 %collective-permute-start.30 = (bf16[3,2,1,2,64,768]{5,4,0,3,2,1:T(8,128)(2,1)S(1)}, bf16[3,2,1,2,64,768]{5,4,0,3,2,1:T(8,128)(2,1)S(1)}, u32[]{:S(2)}, u32[]{:S(2)}) collective-permute-start(bf16[3,2,1,2,64,768]{5,4,0,3,2,1:T(8,128)(2,1)S(1)} %copy.150), channel_id=1, source_target_pairs={{0,16},{4,20},{8,24},{12,28},{16,0},{20,4},{24,8},{28,12},{1,17},{... | collective-permute-start | bytes 3538952 | tf_op jit(solution)/shard_map/ppermute | solution.py:44
  258.6 28.1 %collective-permute-start.31 = (bf16[3,2,1,2,64,768]{5,4,3,1,2,0:T(8,128)(2,1)S(1)}, bf16[3,2,1,2,64,768]{5,4,3,1,2,0:T(8,128)(2,1)S(1)}, u32[]{:S(2)}, u32[]{:S(2)}) collective-permute-start(bf16[3,2,1,2,64,768]{5,4,3,1,2,0:T(8,128)(2,1)S(1)} %copy-done.61), channel_id=1, source_target_pairs={{0,8},{4,12},{8,0},{12,4},{16,24},{20,28},{24,16},{28,20},{1,9},{5... | collective-permute-start | bytes 3538952 | tf_op jit(solution)/shard_map/ppermute | solution.py:44
  273.1 112.9 %collective-permute-start.37 = (bf16[5,4,3,4,8,768]{5,4,2,0,3,1:T(8,128)(2,1)}, bf16[5,4,3,4,8,768]{5,4,2,0,3,1:T(8,128)(2,1)}, u32[]{:S(2)}, u32[]{:S(2)}) collective-permute-start(bf16[5,4,3,4,8,768]{5,4,2,0,3,1:T(8,128)(2,1)} %copy.152), channel_id=1, source_target_pairs={{0,4},{4,0},{8,12},{12,8},{16,20},{20,16},{24,28},{28,24},{1,5},{5... | collective-permute-start | bytes 8847368 | tf_op jit(solution)/shard_map/ppermute | solution.py:44
  316.7 29.6 %collective-permute-start.40 = (bf16[3,1,1,64,768]{4,3,0,2,1:T(8,128)(2,1)S(1)}, bf16[3,1,1,64,768]{4,3,0,2,1:T(8,128)(2,1)S(1)}, u32[]{:S(2)}, u32[]{:S(2)}) collective-permute-start(bf16[3,1,1,64,768]{4,3,0,2,1:T(8,128)(2,1)S(1)} %get-tuple-element.287), channel_id=1, source_target_pairs={{0,3},{1,0},{2,1},{3,2},{4,7},{5,4},{6,5},{7,6},{8,11},{9,8},{10,9... | collective-permute-start | bytes 884744 | tf_op jit(solution)/shard_map/ppermute | solution.py:39
  320.4 40.6 %collective-permute-start.39 = (bf16[3,1,1,64,768]{4,3,0,2,1:T(8,128)(2,1)S(1)}, bf16[3,1,1,64,768]{4,3,0,2,1:T(8,128)(2,1)S(1)}, u32[]{:S(2)}, u32[]{:S(2)}) collective-permute-start(bf16[3,1,1,64,768]{4,3,0,2,1:T(8,128)(2,1)S(1)} %get-tuple-element.286), channel_id=1, source_target_pairs={{0,2},{1,3},{2,0},{3,1},{4,6},{5,7},{6,4},{7,5},{8,10},{9,11},{10,... | collective-permute-start | bytes 884744 | tf_op jit(solution)/shard_map/ppermute | solution.py:39
  384.5 34.4 %collective-permute-start.90 = (bf16[3,1,4,64,384]{4,3,0,2,1:T(8,128)(2,1)}, bf16[3,1,4,64,384]{4,3,0,2,1:T(8,128)(2,1)}, u32[]{:S(2)}, u32[]{:S(2)}) collective-permute-start(bf16[3,1,4,64,384]{4,3,0,2,1:T(8,128)(2,1)} %pad_maximum_fusion.32), channel_id=1, source_target_pairs={{0,4},{4,0},{8,12},{12,8},{16,20},{20,16},{24,28},{28,24},{1,5},{5... | collective-permute-start | bytes 1769480 | tf_op jit(solution)/shard_map/ppermute | solution.py:44
  385.7 36.2 %collective-permute-start.87 = (bf16[3,1,4,64,384]{4,3,0,2,1:T(8,128)(2,1)}, bf16[3,1,4,64,384]{4,3,0,2,1:T(8,128)(2,1)}, u32[]{:S(2)}, u32[]{:S(2)}) collective-permute-start(bf16[3,1,4,64,384]{4,3,0,2,1:T(8,128)(2,1)} %pad_maximum_fusion.31), channel_id=1, source_target_pairs={{0,4},{4,0},{8,12},{12,8},{16,20},{20,16},{24,28},{28,24},{1,5},{5... | collective-permute-start | bytes 1769480 | tf_op jit(solution)/shard_map/ppermute | solution.py:44
  433.6 31.9 %collective-permute-start.43 = (bf16[2048,192]{0,1:T(8,128)(2,1)}, bf16[2048,192]{0,1:T(8,128)(2,1)}, u32[]{:S(2)}, u32[]{:S(2)}) collective-permute-start(bf16[2048,192]{0,1:T(8,128)(2,1)} %copy.135), channel_id=1, source_target_pairs={{0,4},{4,0},{8,12},{12,8},{16,20},{20,16},{24,28},{28,24},{1,5},{5... | collective-permute-start | bytes 2359304 | tf_op jit(solution)/shard_map/ppermute | solution.py:44
  459.3 56.5 %collective-permute-start.76 = (bf16[5,2,3,1,8,768]{5,4,2,0,3,1:T(8,128)(2,1)}, bf16[5,2,3,1,8,768]{5,4,2,0,3,1:T(8,128)(2,1)}, u32[]{:S(2)}, u32[]{:S(2)}) collective-permute-start(bf16[5,2,3,1,8,768]{5,4,2,0,3,1:T(8,128)(2,1)} %slice.592), channel_id=1, source_target_pairs={{0,16},{4,20},{8,24},{12,28},{16,0},{20,4},{24,8},{28,12},{1,17},{... | collective-permute-start | bytes 1105928 | tf_op jit(solution)/shard_map/ppermute | solution.py:44
  459.7 58.6 %collective-permute-start.74 = (bf16[5,2,3,1,8,768]{5,4,2,0,3,1:T(8,128)(2,1)}, bf16[5,2,3,1,8,768]{5,4,2,0,3,1:T(8,128)(2,1)}, u32[]{:S(2)}, u32[]{:S(2)}) collective-permute-start(bf16[5,2,3,1,8,768]{5,4,2,0,3,1:T(8,128)(2,1)} %slice.588), channel_id=1, source_target_pairs={{0,8},{4,12},{8,0},{12,4},{16,24},{20,28},{24,16},{28,20},{1,9},{5... | collective-permute-start | bytes 1105928 | tf_op jit(solution)/shard_map/ppermute | solution.py:44
  486.4 48.7 %collective-permute-start.46 = (bf16[256,768]{1,0:T(8,128)(2,1)}, bf16[256,768]{1,0:T(8,128)(2,1)}, u32[]{:S(2)}, u32[]{:S(2)}) collective-permute-start(bf16[256,768]{1,0:T(8,128)(2,1)} %get-tuple-element.252), channel_id=1, source_target_pairs={{0,3},{1,0},{2,1},{3,2},{4,7},{5,4},{6,5},{7,6},{8,11},{9,8},{10,9... | collective-permute-start | bytes 1179656 | tf_op jit(solution)/shard_map/ppermute | solution.py:39
  508.9 36.0 %collective-permute-start.45 = (bf16[256,768]{1,0:T(8,128)(2,1)}, bf16[256,768]{1,0:T(8,128)(2,1)}, u32[]{:S(2)}, u32[]{:S(2)}) collective-permute-start(bf16[256,768]{1,0:T(8,128)(2,1)} %get-tuple-element.253), channel_id=1, source_target_pairs={{0,2},{1,3},{2,0},{3,1},{4,6},{5,7},{6,4},{7,5},{8,10},{9,11},{10,... | collective-permute-start | bytes 1179656 | tf_op jit(solution)/shard_map/ppermute | solution.py:39
  513.7 31.5 %collective-permute-start.44 = (bf16[256,768]{1,0:T(8,128)(2,1)}, bf16[256,768]{1,0:T(8,128)(2,1)S(1)}, u32[]{:S(2)}, u32[]{:S(2)}) collective-permute-start(bf16[256,768]{1,0:T(8,128)(2,1)} %get-tuple-element.251), channel_id=1, source_target_pairs={{0,1},{1,2},{2,3},{3,0},{4,5},{5,6},{6,7},{7,4},{8,9},{9,10},{10,1... | collective-permute-start | bytes 1179656 | tf_op jit(solution)/shard_map/ppermute | solution.py:39
  521.5 32.2 %collective-permute-start.78 = (bf16[5,3,1,8,768]{4,3,2,1,0:T(8,128)(2,1)S(1)}, bf16[5,3,1,8,768]{4,3,2,1,0:T(8,128)(2,1)S(1)}, u32[]{:S(2)}, u32[]{:S(2)}) collective-permute-start(bf16[5,3,1,8,768]{4,3,2,1,0:T(8,128)(2,1)S(1)} %get-tuple-element.297), channel_id=1, source_target_pairs={{0,3},{1,0},{2,1},{3,2},{4,7},{5,4},{6,5},{7,6},{8,11},{9,8},{10,9... | collective-permute-start | bytes 552968 | tf_op jit(solution)/shard_map/ppermute | solution.py:39
  (226 other events, 2111.1 us)

commit v3 on v1

--- a/solution.py
+++ b/solution.py
@@ -42,76 +42,6 @@
 def flip_bit(block, bit, axis="dp"):
     count = lax.axis_size(axis)
     return lax.ppermute(block, axis, [(i, i ^ (1 << bit)) for i in range(count)])
-
-
-def bit_lists():
-    count = lax.axis_size("dp")
-    bits = count.bit_length() - 1
-    up = list(range(1, bits))
-    return (up, up[::-1])
-
-
-def slice_order(bits):
-    order = [0]
-    for bit in bits + [0]:
-        order = order + [entry ^ (1 << bit) for entry in order]
-    return order
-
-
-def spread(block, bits, axis):
-    for bit in bits:
-        block = jnp.concatenate([block, flip_bit(block, bit)], axis=axis)
-    return block
-
-
-def gather_weights(own):
-    up, down = bit_lists()
-    pieces = [own] + [from_ahead(own, step) for step in range(1, 4)]
-    first = spread(jnp.concatenate(pieces[:2], axis=1), up, 3)
-    second = spread(jnp.concatenate(pieces[2:], axis=1), down, 3)
-    first_far = flip_bit(first, 0)
-    second_far = flip_bit(second, 0)
-    return jnp.concatenate(
-        [
-            jnp.concatenate([first, first_far], axis=3),
-            jnp.concatenate([second, second_far], axis=3),
-        ],
-        axis=1,
-    )
-
-
-def fold(block, bit, axis):
-    half = block.shape[axis] // 2
-    low = lax.slice_in_dim(block, 0, half, axis=axis)
-    high = lax.slice_in_dim(block, half, 2 * half, axis=axis)
-    return (low.astype(F32) + flip_bit(high, bit).astype(F32)).astype(BF)
-
-
-def reduce_grads(grads):
-    up, down = bit_lists()
-    first, second = grads[:, :2], grads[:, 2:]
-    for bit in [0] + down:
-        first = fold(first, bit, 3)
-    for bit in [0] + up:
-        second = fold(second, bit, 3)
-    total = first[:, 0].astype(F32)
-    for step, piece in ((1, first[:, 1]), (2, second[:, 0]), (3, second[:, 1])):
-        total = total + to_ahead(piece, step).astype(F32)
-    total = total.astype(BF)
-    half = total.shape[-1] // 2
-    left = spread(total[..., :half], up + [0], 2)
-    right = spread(total[..., half:], down + [0], 2)
-    return (left, right)
-
-
-def slice_hot(order, parts, rows, rank):
-    count = len(order)
-    size = parts * count * rows
-    place = jnp.arange(size)
-    slot = place // rows % count
-    table = sum(jnp.where(slot == index, entry, 0) for index, entry in enumerate(order))
-    natural = place // (count * rows) * (count * rows) + (rank ^ table) * rows + place % rows
-    return (natural[:, None] == jnp.arange(size)[None, :]).astype(BF)
 
 
 def norm_scale(values):
@@ -455,6 +385,326 @@
     return [jax.ShapeDtypeStruct(shape, dtype) for shape, dtype in pairs]
 
 
+MESH = pl.DeviceIdType.MESH
+
+
+class Links:
+    def __init__(self, sends, receives, local, bits):
+        self.sends, self.receives, self.local_sems = sends, receives, local
+        self.used = 0
+        self.used_local = 0
+        self.bits = bits
+        self.data = lax.axis_index("dp")
+        self.tensor = lax.axis_index("tensor")
+        self.ranks = lax.axis_size("tensor")
+
+    def bit(self, index):
+        return self.data // (1 << index) % 2
+
+    def partner(self, index):
+        return (self.data + (1 << index) * (1 - 2 * self.bit(index)), self.tensor)
+
+    def ahead(self, step):
+        return (self.data, (self.tensor + step) % self.ranks)
+
+    def across(self, index):
+        here = self.tensor // (1 << index) % 2
+        return (self.data, self.tensor + (1 << index) * (1 - 2 * here))
+
+    def barrier(self):
+        sem = pltpu.get_barrier_semaphore()
+        others = [self.partner(index) for index in range(self.bits)]
+        others += [self.ahead(step) for step in range(1, self.ranks)]
+        for other in others:
+            pl.semaphore_signal(sem, inc=1, device_id=other, device_id_type=MESH)
+        pl.semaphore_wait(sem, len(others))
+
+    def send(self, source, target, device):
+        copy = pltpu.make_async_remote_copy(
+            src_ref=source,
+            dst_ref=target,
+            send_sem=self.sends.at[self.used],
+            recv_sem=self.receives.at[self.used],
+            device_id=device,
+            device_id_type=MESH,
+        )
+        self.used += 1
+        copy.start()
+        return copy
+
+    def local(self, source, target):
+        copy = pltpu.make_async_copy(source, target, self.local_sems.at[self.used_local])
+        self.used_local += 1
+        copy.start()
+        return copy
+
+
+def span(start, size, step):
+    return pl.ds(pl.multiple_of(start, step), size)
+
+
+def run_pairs(streams, stages):
+    pairs = [streams[i : i + 2] for i in range(0, len(streams), 2)]
+    for step in range(len(pairs) + stages):
+        for index in reversed(range(len(pairs))):
+            if 0 <= step - index <= stages:
+                for stream in pairs[index]:
+                    next(stream, None)
+
+
+def bit_order(place):
+    return (1, 2) if place % 2 == 0 else (2, 1)
+
+
+def split_chunks(sizes, unit):
+    chunks = []
+    for index, rows in enumerate(sizes):
+        step = rows
+        while step > unit:
+            step //= 2
+        chunks += [(index, start, step) for start in range(0, rows, step)]
+    return chunks
+
+
+def gather_stream(links, own, full, stage, first, rows, place):
+    one, two = bit_order(place)
+    width = own.shape[1]
+    half = width // 2
+    cols = span(links.bit(0) * half, half, 128)
+    base = first + links.bit(one) * (rows // 2)
+    quarter = span(base + links.bit(two) * (rows // 4), rows // 4, 16)
+    mine = links.local(own.at[pl.ds(first, rows), :], stage)
+    ranks = links.ranks
+    copies = [
+        links.send(own.at[quarter, cols], full.at[ranks - step, quarter, cols], links.ahead(step))
+        for step in range(1, ranks)
+    ]
+    yield
+    mine.wait()
+    home = links.local(stage, full.at[0, pl.ds(first, rows), :])
+    for copy in copies:
+        copy.wait()
+    others = pl.ds(1, ranks - 1)
+    part = full.at[others, quarter, cols]
+    copy = links.send(part, part, links.partner(two))
+    yield
+    copy.wait()
+    part = full.at[others, span(base, rows // 2, 16), cols]
+    copy = links.send(part, part, links.partner(one))
+    yield
+    copy.wait()
+    part = full.at[others, pl.ds(first, rows), cols]
+    copy = links.send(part, part, links.partner(0))
+    yield
+    copy.wait()
+    home.wait()
+
+
+def gather_kernel(count, bits, chunks, *refs):
+    own, full = refs[:count], refs[count : 2 * count]
+    scratch = refs[2 * count :]
+    stages, (sends, receives, local) = scratch[:-3], scratch[-3:]
+    links = Links(sends, receives, local, bits)
+    links.barrier()
+    streams = [
+        gather_stream(links, own[index], full[index], stages[place], first, rows, place)
+        for place, (index, first, rows) in enumerate(chunks)
+    ]
+    run_pairs(streams, 4)
+
+
+def gather_all(own, bits):
+    ranks = lax.axis_size("tensor")
+    chunks = split_chunks([a.shape[0] for a in own], 256)
+    any_space = pl.BlockSpec(memory_space=pl.ANY)
+    copies = len(chunks) * (ranks + 2)
+    return pl.pallas_call(
+        functools.partial(gather_kernel, len(own), bits, chunks),
+        out_shape=[jax.ShapeDtypeStruct((ranks,) + a.shape, a.dtype) for a in own],
+        in_specs=[any_space] * len(own),
+        out_specs=[any_space] * len(own),
+        scratch_shapes=[pltpu.VMEM((rows, own[0].shape[1]), BF) for _, _, rows in chunks]
+        + [
+            pltpu.SemaphoreType.DMA((copies,)),
+            pltpu.SemaphoreType.DMA((copies,)),
+            pltpu.SemaphoreType.DMA((2 * len(chunks),)),
+        ],
+        compiler_params=pltpu.CompilerParams(
+            collective_id=1, has_side_effects=True, vmem_limit_bytes=60 * 2**20
+        ),
+        name="gather_all",
+    )(*own)
+
+
+def reduce_stream(links, grad, total, room, first, rows, place, slabs):
+    mine, from_core, from_one, from_two, from_far, from_more = room
+    one, two = bit_order(place)
+    half = grad.shape[2] // 2
+    whole_rows = pl.ds(first, rows)
+    here = span(links.bit(0) * half, half, 128)
+    there = span((1 - links.bit(0)) * half, half, 128)
+    kept = links.local(grad.at[:, whole_rows, here], mine)
+    copy = links.send(grad.at[:, whole_rows, there], from_core, links.partner(0))
+    yield
+    kept.wait()
+    copy.wait()
+    mine[...] = mine[...] + from_core[...]
+    base = links.bit(one) * (rows // 2)
+    given = (1 - links.bit(one)) * (rows // 2)
+    copy = links.send(
+        mine.at[:, span(given, rows // 2, 16), :], from_one, links.partner(one)
+    )
+    yield
+    copy.wait()
+    keep = span(base, rows // 2, 16)
+    mine[:, keep, :] = mine[:, keep, :] + from_one[...]
+    given = base + (1 - links.bit(two)) * (rows // 4)
+    base_two = base + links.bit(two) * (rows // 4)
+    copy = links.send(
+        mine.at[:, span(given, rows // 4, 16), :], from_two, links.partner(two)
+    )
+    yield
+    copy.wait()
+    keep = span(base_two, rows // 4, 16)
+    if slabs > 1:
+        mine[:, keep, :] = mine[:, keep, :] + from_two[...]
+        copies = [
+            links.send(mine.at[step, keep, :], from_far.at[step - 1], links.ahead(step))
+            for step in range(1, slabs)
+        ]
+        yield
+        for copy in copies:
+            copy.wait()
+        value = mine[0, keep, :].astype(F32)
+        for step in range(slabs - 1):
+            value = value + from_far[step].astype(F32)
+        value = value.astype(BF)
+    else:
+        yield
+        value = mine[0, keep, :] + from_two[0]
+    quarter = span(first + base_two, rows // 4, 16)
+    for index in range(3, links.bits):
+        total[quarter, here] = value
+        copy = links.send(
+            total.at[quarter, here], from_more.at[index - 3], links.partner(index)
+        )
+        copy.wait()
+        value = value + from_more[index - 3]
+    total[quarter, here] = value
+    copy = links.send(total.at[quarter, here], total.at[quarter, here], links.partner(two))
+    yield
+    copy.wait()
+    part = total.at[span(first + base, rows // 2, 16), here]
+    copy = links.send(part, part, links.partner(one))
+    yield
+    copy.wait()
+    part = total.at[whole_rows, here]
+    copy = links.send(part, part, links.partner(0))
+    yield
+    copy.wait()
+
+
+def small_stream(links, small, held, came, grouped, final):
+    held[0] = small[...]
+    tensor_bits = links.ranks.bit_length() - 1
+    for index in range(links.bits + tensor_bits):
+        device = links.partner(index) if index < links.bits else links.across(index - links.bits)
+        copy = links.send(held.at[index], came.at[index], device)
+        yield
+        copy.wait()
+        value = held[index] + came[index]
+        held[index + 1] = value
+        if index == links.bits - 1:
+            grouped[...] = value
+    final[...] = value
+    yield
+
+
+def reduce_kernel(count, bits, chunks, parts, *refs):
+    refs = list(refs)
+    grads = [refs.pop(0) for _ in range(count)]
+    sends_in = [refs.pop(0) for _ in range(parts)]
+    small = refs.pop(0)
+    totals = [refs.pop(0) for _ in range(count)]
+    came_in = [refs.pop(0) for _ in range(parts)]
+    grouped, final = refs.pop(0), refs.pop(0)
+    local, receives, sends = refs.pop(), refs.pop(), refs.pop()
+    came, held = refs.pop(), refs.pop()
+    rooms = [refs[6 * i : 6 * i + 6] for i in range(len(chunks))]
+    links = Links(sends, receives, local, bits)
+    links.barrier()
+    rows_moved = [
+        links.send(source.at[(links.tensor + step) % links.ranks], target.at[step - 1],
+                   links.ahead(step))
+        for source, target in zip(sends_in, came_in)
+        for step in range(1, links.ranks)
+    ]
+    streams = [small_stream(links, small, held, came, grouped, final)]
+    streams = [
+        reduce_stream(
+            links, grads[index], totals[index], rooms[place], first, rows, place,
+            grads[index].shape[0],
+        )
+        for place, (index, first, rows) in enumerate(chunks)
+    ] + streams
+    run_pairs(streams, max(7, bits + links.ranks.bit_length() - 1))
+    for copy in rows_moved:
+        copy.wait()
+
+
+def reduce_all(grads, parts, small, bits):
+    ranks = lax.axis_size("tensor")
+    chunks = split_chunks([a.shape[1] for a in grads], 200)
+    chunks = [c for c in chunks if grads[c[0]].shape[0] > 1] + [
+        c for c in chunks if grads[c[0]].shape[0] == 1
+    ]
+    width = small.shape[1]
+    half = width // 2
+    more = max(bits - 3, 1)
+    rooms = []
+    for index, _, rows in chunks:
+        slabs = grads[index].shape[0]
+        rooms += [
+            pltpu.VMEM((slabs, rows, half), BF),
+            pltpu.VMEM((slabs, rows, half), BF),
+            pltpu.VMEM((slabs, rows // 2, half), BF),
+            pltpu.VMEM((slabs, rows // 4, half), BF),
+            pltpu.VMEM((ranks - 1, rows // 4, half), BF),
+            pltpu.VMEM((more, rows // 4, half), BF),
+        ]
+    small_steps = bits + ranks.bit_length() - 1
+    copies = (
+        len(chunks) * (6 + ranks - 1 + bits - 3) + len(parts) * (ranks - 1) + small_steps
+    )
+    any_space = pl.BlockSpec(memory_space=pl.ANY)
+    vmem = pl.BlockSpec(memory_space=pltpu.VMEM)
+    out = pl.pallas_call(
+        functools.partial(reduce_kernel, len(grads), bits, chunks, len(parts)),
+        out_shape=shaped(
+            *[(a.shape[1:], BF) for a in grads],
+            *[((ranks - 1,) + a.shape[1:], a.dtype) for a in parts],
+            (small.shape, F32),
+            (small.shape, F32),
+        ),
+        in_specs=[any_space] * (len(grads) + len(parts)) + [vmem],
+        out_specs=[vmem] * len(grads) + [any_space] * len(parts) + [vmem] * 2,
+        scratch_shapes=rooms
+        + [
+            pltpu.VMEM((small_steps + 1,) + small.shape, F32),
+            pltpu.VMEM((small_steps,) + small.shape, F32),
+            pltpu.SemaphoreType.DMA((copies,)),
+            pltpu.SemaphoreType.DMA((copies,)),
+            pltpu.SemaphoreType.DMA((len(chunks),)),
+        ],
+        compiler_params=pltpu.CompilerParams(
+            collective_id=2, has_side_effects=True, vmem_limit_bytes=60 * 2**20
+        ),
+        name="reduce_all",
+    )(*grads, *parts, small)
+    count = len(grads)
+    return out[:count], out[count:-2], out[-2], out[-1]
+
+
 def run_heads(kernel, heads, scalars, lines, arrays, outs, scratch, out_heads, cells, name):
     in_specs = [by_head(a.shape) for a in lines] + [whole(a.shape) for a in arrays]
     out_specs = [
@@ -516,8 +766,7 @@
     tensor_rank = lax.axis_index("tensor")
     data_rank = lax.axis_index("dp")
     factor = HEAD ** (-0.5)
-    up, down = bit_lists()
-    order_up, order_down = slice_order(up), slice_order(down)
+    bits = data_size.bit_length() - 1
 
     far = (prompt_of != data_rank).astype(jnp.int32)
     index = jnp.arange(cont_count, dtype=jnp.int32)
@@ -536,25 +785,13 @@
             ]
         )
 
-    head_rows = HEAD // data_size
-    attn_shard = jnp.stack([w_o, c_q.T, c_k.T, c_v.T, c_o]).reshape(
-        5, 1, heads, data_size, head_rows, width
-    )
-    attn_own = lax.dynamic_slice_in_dim(attn_shard, data_rank, 1, 3)
-    hidden_rows = hidden_here // data_size
-    ffn_own = jnp.stack(
-        [
-            lax.dynamic_slice_in_dim(w_gate, data_rank * hidden_rows, hidden_rows, 1).T,
-            lax.dynamic_slice_in_dim(w_up, data_rank * hidden_rows, hidden_rows, 1).T,
-            lax.dynamic_slice_in_dim(w_down, data_rank * hidden_rows, hidden_rows, 0),
-        ]
-    ).reshape(3, 1, 1, 1, hidden_rows, width)
     enc_far = flip_bit(enc_out, 0)
-    attn_full = gather_weights(attn_own)
-    ffn_full = gather_weights(ffn_own)
+    wo_all, cq_all, ck_all, cv_all, co_all, wg_all, wu_all, wd_all = gather_all(
+        [w_o, c_q.T, c_k.T, c_v.T, c_o, w_gate.T, w_up.T, w_down], bits
+    )
 
     count = jnp.broadcast_to(jnp.sum(valid.astype(F32)), (8, 128))
-    for bit in range(data_size.bit_length() - 1):
+    for bit in range(bits):
         count = count + flip_bit(count, bit)
     token_count = count[0, 0]
 
@@ -618,21 +855,9 @@
         [heads_to_rows(o_prompt, share), heads_to_rows(o_cont, CONT_LEN)]
     )
 
-    hot_up = slice_hot(order_up, heads, head_rows, data_rank)
-    hot_down = slice_hot(order_down, heads, head_rows, data_rank)
-    hot_four = jnp.stack([hot_up, hot_up, hot_down, hot_down])
-    attn_flat = attn_full.reshape(5, ranks * cols, width)
-    wo_full = (
-        jnp.einsum(
-            "zrn,zrd->znd",
-            hot_four,
-            attn_flat[0].reshape(ranks, cols, width),
-            preferred_element_type=F32,
-        )
-        .astype(BF)
-        .reshape(ranks * cols, width)
-    )
-    cq_t, ck_t, cv_t, co_full = attn_flat[1], attn_flat[2], attn_flat[3], attn_flat[4]
+    wo_full, cq_t, ck_t, cv_t, co_full = (
+        a.reshape(ranks * cols, width) for a in (wo_all, cq_all, ck_all, cv_all, co_all)
+    )
     x_own = own_rows(x_prompt, x_cont).astype(F32)
     x1 = x_own + mm(mixed_self, wo_full)
     n2 = rms_norm(x1, gain_cross).astype(BF)
@@ -662,8 +887,7 @@
     )(far_here, query_c, key_c, value_c)
     x2 = x1 + mm(mixed_cross, co_full)
     n3 = rms_norm(x2, gain_ffn).astype(BF)
-    ffn_flat = ffn_full.reshape(3, ranks * hidden_here, width)
-    wg_t, wu_t, wd = ffn_flat[0], ffn_flat[1], ffn_flat[2]
+    wg_t, wu_t, wd = (a.reshape(ranks * hidden_here, width) for a in (wg_all, wu_all, wd_all))
     gate_pre = mm(n3, wg_t, NT)
     upper = mm(n3, wu_t, NT)
     hidden, gelu_pull = jax.vjp(
@@ -691,15 +915,12 @@
     d_gate, d_upper = gelu_pull(d_hidden)
     d_gate = d_gate.astype(BF)
     d_upper = d_upper.astype(BF)
+    ffn_grads = [
+        mm(d_gate, n3, TN).astype(BF),
+        mm(d_upper, n3, TN).astype(BF),
+        mm(hidden, g3_low, TN).astype(BF),
+    ]
     d_n3 = mm(d_gate, wg_t) + mm(d_upper, wu_t)
-    ffn_grads = jnp.stack(
-        [
-            mm(d_gate, n3, TN).astype(BF),
-            mm(d_upper, n3, TN).astype(BF),
-            mm(hidden, g3_low, TN).astype(BF),
-        ]
-    ).reshape(3, ranks, 1, data_size, hidden_rows, width)
-    ffn_left, ffn_right = reduce_grads(ffn_grads)
     back3, gain_ffn_part = norm_back(x2, gain_ffn, d_n3)
     g2 = g3 + back3
 
@@ -731,6 +952,13 @@
     g1 = g2 + back2
     g1_low = g1.astype(BF)
 
+    attn_grads = [
+        mm(mixed_self, g1_low, TN).astype(BF),
+        mm(d_query_c, n2, TN).astype(BF),
+        mm(d_key_c, enc_pair, TN).astype(BF),
+        mm(d_value_c, enc_pair, TN).astype(BF),
+        mm(mixed_cross, g2_low, TN).astype(BF),
+    ]
     d_mixed_s = mm(g1_low, wo_full, NT).astype(BF)
     held, pick = rows_to_heads(d_mixed_s)
     place = (pick[None, :] == jnp.arange(ranks)[:, None]).astype(BF)
@@ -778,9 +1006,6 @@
 
     part_cont = three(dq_cont, dk_cont, dv_cont).astype(BF)
     part_prompt = three(dq_prompt, dk_prompt, dv_prompt).astype(BF)
-    d_n1 = jnp.concatenate([scatter_rows(part_prompt, share), scatter_rows(part_cont, CONT_LEN)])
-    back1, ignored = norm_back(x_own, gain_self, d_n1)
-    grad_x = g1 + back1
     unit = stream * norm_scale(stream)
     gain_self_part = jnp.sum(part_prompt.astype(F32) * unit[:PROMPT], axis=0) + jnp.sum(
         part_cont.astype(F32) * unit[PROMPT:], axis=0
@@ -800,72 +1025,14 @@
     enc_hot = (enc_from[:, None] == enc_place[None, :]).astype(BF)
     grad_enc = mm(enc_hot, enc_all, TN)
 
-    grad_wo_part = mm(mixed_self, g1_low, TN).astype(BF).reshape(ranks, cols, width)
-    grad_wo_part = jnp.einsum(
-        "zrn,znd->zrd", hot_four, grad_wo_part, preferred_element_type=F32
-    ).astype(BF)
-    attn_grads = jnp.stack(
-        [
-            grad_wo_part.reshape(ranks * cols, width),
-            mm(d_query_c, n2, TN).astype(BF),
-            mm(d_key_c, enc_pair, TN).astype(BF),
-            mm(d_value_c, enc_pair, TN).astype(BF),
-            mm(mixed_cross, g2_low, TN).astype(BF),
-        ]
-    ).reshape(5, ranks, heads, data_size, head_rows, width)
-    attn_left, attn_right = reduce_grads(attn_grads)
-
-    def finish(left, right, hots, matrix, transposed):
-        halves = [
-            half[matrix].reshape(-1, half.shape[-1]) for half in (left, right)
-        ]
-        if transposed:
-            return jnp.concatenate([mm(a, hot, TN) for a, hot in zip(halves, hots)], axis=0)
-        return jnp.concatenate([mm(hot, a, TN) for a, hot in zip(halves, hots)], axis=1)
-
-    attn_hots = (hot_up, hot_down)
-    ffn_hots = (
-        slice_hot(order_up, 1, hidden_rows, data_rank),
-        slice_hot(order_down, 1, hidden_rows, data_rank),
-    )
-    grad_w_o = finish(attn_left, attn_right, attn_hots, 0, False)
-    grad_c_q = finish(attn_left, attn_right, attn_hots, 1, True)
-    grad_c_k = finish(attn_left, attn_right, attn_hots, 2, True)
-    grad_c_v = finish(attn_left, attn_right, attn_hots, 3, True)
-    grad_c_o = finish(attn_left, attn_right, attn_hots, 4, False)
-    grad_w_gate = finish(ffn_left, ffn_right, ffn_hots, 0, True)
-    grad_w_up = finish(ffn_left, ffn_right, ffn_hots, 1, True)
-    grad_w_down = finish(ffn_left, ffn_right, ffn_hots, 2, False)
-
     def by_rows(prompt_part, cont_part):
-        return mm(n1[:PROMPT], prompt_part, TN) + mm(n1[PROMPT:], cont_part, TN)
-
-    qkv_grads = jnp.concatenate(
-        [
-            by_rows(dq_prompt, dq_cont),
-            by_rows(dk_prompt, dk_cont),
-            by_rows(dv_prompt, dv_cont),
-        ],
-        axis=1,
-    ).astype(BF)
-    feat_rows = width // data_size
-    qkv_width = qkv_grads.shape[1]
-    qkv_hots = (
-        slice_hot(order_up, 1, feat_rows, data_rank),
-        slice_hot(order_down, 1, feat_rows, data_rank),
-    )
-    half = qkv_width // 2
-    qkv_parts = []
-    for hot, bits, cut in (
-        (qkv_hots[0], up, qkv_grads[:, :half]),
-        (qkv_hots[1], down, qkv_grads[:, half:]),
-    ):
-        moved = mm(hot, cut).astype(BF).reshape(1, 1, 1, data_size, feat_rows, half)
-        for bit in [0] + bits[::-1]:
-            moved = fold(moved, bit, 3)
-        moved = spread(moved, bits + [0], 3).reshape(width, half)
-        qkv_parts.append(mm(hot, moved, TN))
-    qkv_all = jnp.concatenate(qkv_parts, axis=1)
+        return mm(prompt_part, n1[:PROMPT], TN) + mm(cont_part, n1[PROMPT:], TN)
+
+    qkv_grads = [
+        by_rows(dq_prompt, dq_cont).astype(BF),
+        by_rows(dk_prompt, dk_cont).astype(BF),
+        by_rows(dv_prompt, dv_cont).astype(BF),
+    ]
 
     line_grad = (line_cont + line_prompt).reshape(heads, LINE)[:, :DIST]
     table_part = jnp.dot(line_grad, bucket_hot, precision=lax.Precision.HIGHEST)
@@ -873,11 +1040,27 @@
     small = small.at[0].set(gain_self_part).at[1].set(gain_cross_part).at[2].set(gain_ffn_part)
     small = small.at[3, 0].set(loss_part)
     small = small.at[4, : table_part.size].set(table_part.reshape(-1))
-    for bit in range(data_size.bit_length() - 1):
-        small = small + flip_bit(small, bit)
-    grad_table = small[4, : table_part.size].reshape(table_part.shape).T
-    for bit in range(ranks.bit_length() - 1):
-        small = small + flip_bit(small, bit, "tensor")
+
+    totals, came, grouped, small = reduce_all(
+        [a.reshape(ranks, hidden_here, width) for a in ffn_grads]
+        + [a.reshape(ranks, cols, width) for a in attn_grads]
+        + [a.reshape(1, cols, width) for a in qkv_grads],
+        [part_prompt.reshape(ranks, share, width), part_cont.reshape(ranks, CONT_LEN, width)],
+        small,
+        bits,
+    )
+    totals = [total.astype(F32) for total in totals]
+    grad_table = grouped[4, : table_part.size].reshape(table_part.shape).T
+
+    def own_total(block, rows, others):
+        total = lax.dynamic_slice_in_dim(block, tensor_rank * rows, rows, 0).astype(F32)
+        return total + jnp.sum(others.astype(F32), axis=0)
+
+    d_n1 = jnp.concatenate(
+        [own_total(part_prompt, share, came[0]), own_total(part_cont, CONT_LEN, came[1])]
+    )
+    back1, ignored = norm_back(x_own, gain_self, d_n1)
+    grad_x = g1 + back1
     return (
         y_all[:share],
         y_all[share:],
@@ -888,17 +1071,17 @@
         small[1],
         small[2],
         grad_table,
-        qkv_all[:, :cols],
-        qkv_all[:, cols : 2 * cols],
-        qkv_all[:, 2 * cols :],
-        grad_w_o,
-        grad_c_q,
-        grad_c_k,
-        grad_c_v,
-        grad_c_o,
-        grad_w_gate,
-        grad_w_up,
-        grad_w_down,
+        totals[8].T,
+        totals[9].T,
+        totals[10].T,
+        totals[3],
+        totals[4].T,
+        totals[5].T,
+        totals[6].T,
+        totals[7],
+        totals[0].T,
+        totals[1].T,
+        totals[2],
         small[3, 0] / token_count,
     )
 

time: 646 us -> 516 us (0.80)
  the two profiles are of different devices: /device:TPU:0 before, /device:TPU:9 now
where the time goes in v3:
time: 516 us; the launch traced here: 507 us
  Pallas kernels  281 us (54%)
  matrix products  85.8 us (17%)
  local copies, waits for them, and re-layouts  52.9 us (10%)
  other arithmetic  32.9 us (6%)
  waiting for transfers between devices  25.2 us (5%)
  starting transfers between devices  24.8 us (5%)
    pallas_call x1, Pallas kernels, reduce_all(): pl.pallas_call(functools.partial(reduce_kernel, len(grads), bits, chunks,...  135 us
    dot_general x40, matrix products, mm(): return lax.dot_general(left, right, dims, preferred_element_type=F32)  84.5 us
    pallas_call x1, Pallas kernels, gather_all(): pl.pallas_call(functools.partial(gather_kernel, len(own), bits, chunks),...  72.7 us
    pallas_call x4, Pallas kernels, run_heads(): pl.pallas_call(kernel, out_shape=outs, grid_spec=pltpu.PrefetchScalarGrid...  48.2 us
    unnamed x189, local copies, waits for them, and re-layouts  18.7 us
    ppermute x9, waiting for transfers between devices, from_ahead(): lax.ppermute(block, 'tensor', [((i + step) % count, i) for i in range(cou...  16.5 us
    pallas_call x1, Pallas kernels, on_device(): pl.pallas_call(cross_back, out_shape=shaped(((own_count, pairs * TILE), B...  14.5 us
    pallas_call x1, Pallas kernels, on_device(): pl.pallas_call(cross_fwd, out_shape=shaped(((own_count, pairs * TILE), BF...  10.3 us
  transfers between devices with their start and end apart: 22, of which 7 were waited for; matrix products, arithmetic and copies ran while one was open for 20% of the time, Pallas kernels for 51%

profile of v3, /device:TPU:9, one launch (start us, length us, event | category | flops | bytes accessed | tf_op | source)
XLA Modules:
  0.0 507.3 jit_solution(9432907347571362042)
XLA Ops:
  3.1 3.3 convert_multiply_fusion
  14.2 2.6 fusion.10.q_ref
  16.9 8.7 %prompt_fwd.1 = (bf16[1024,192]{1,0:T(8,128)(2,1)}, f32[1024,192]{1,0:T(8,128)}) custom-call(f32[3,1,1408]{2,1,0:T(1,128)} %reshape.373.line_ref, bf16[1536,192]{1,0:T(8,128)(2,1)} %fusion.10.q_ref, bf16[1536,192]{1,0:T(8,128)(2,1)} %copy-done.20, bf16[1536,192]{1,0:T(8,128)(2,1)} %copy-done.46), custom_call_target="tpu_custom_call" | custom-call | flops 2013265920 | bytes 2966016 | tf_op jit(solution)/shard_map/prompt_fwd/pallas_call | solution.py:713
  45.7 72.7 %gather_all.1 = (bf16[4,192,768]{2,1,0:T(8,128)(2,1)}, bf16[4,192,768]{2,1,0:T(8,128)(2,1)}, bf16[4,192,768]{2,1,0:T(8,128)(2,1)}, bf16[4,192,768]{2,1,0:T(8,128...) custom-call(bf16[192,768]{1,0:T(8,128)(2,1)} %refs_0_.1, ...), custom_call_target="tpu_custom_call" | custom-call | tf_op jit(solution)/shard_map/gather_all/pallas_call | solution.py:521
  124.4 9.3 %cont_fwd.1 = (bf16[512,192]{1,0:T(8,128)(2,1)}, f32[512,192]{1,0:T(8,128)}) custom-call(s32[4]{0:T(128)} %select_reduce_fusion.slot_ref, f32[3,1,1408]{2,1,0:T(1,128)} %reshape.373.line_ref, f32[4,128,128]{2,1,0:T(8,128)} %broadcast_in_dim.44.ok_ref, bf16[1536,192]{1,0:T(8,128)(2,1)} %fusion.10.q_ref, bf16[1536,192]{1,0:T(8,128)(2,1)} %copy-done.20, ...), custom_call_target="tpu_custom_call" | custom-call | flops 1811939328 | bytes 3424768 | tf_op jit(solution)/shard_map/cont_fwd/pallas_call | solution.py:713
  140.4 4.1 convolution_convert_fusion.7.k_ref
  151.3 10.3 %cross_fwd.1 = (bf16[384,768]{1,0:T(8,128)(2,1)}, f32[384,768]{1,0:T(8,128)}) custom-call(s32[1]{0:T(128)} %dynamic_slice.64.far_ref, bf16[384,768]{1,0:T(8,128)(2,1)} %fusion.15.q_ref, bf16[1024,768]{1,0:T(8,128)(2,1)} %convolution_convert_fusion.7.k_ref, bf16[1024,768]{1,0:T(8,128)(2,1)} %convolution_convert_fusion.6.v_ref), custom_call_target="tpu_custom_call" | custom-call | flops 2415919104 | bytes 3735552 | tf_op jit(solution)/shard_map/cross_fwd/pallas_call | solution.py:875
  171.9 3.9 fusion.8
  177.1 3.5 convolution_convert_fusion.2
  180.7 3.5 convolution_convert_fusion
  184.2 4.0 convolution_convert_fusion.1
  193.4 14.5 %cross_back.1 = (bf16[384,768]{1,0:T(8,128)(2,1)}, bf16[1024,768]{1,0:T(8,128)(2,1)}, bf16[1024,768]{1,0:T(8,128)(2,1)}) custom-call(s32[1]{0:T(128)} %dynamic_slice.64.far_ref, bf16[384,768]{1,0:T(8,128)(2,1)} %fusion.15.q_ref, bf16[1024,768]{1,0:T(8,128)(2,1)} %convolution_convert_fusion.7.k_ref, bf16[1024,768]{1,0:T(8,128)(2,1)} %convolution_convert_fusion.6.v_ref, ...), custom_call_target="tpu_custom_call" | custom-call | flops 6039797760 | bytes 3735552 | tf_op jit(solution)/shard_map/cross_back/pallas_call | solution.py:929
  229.2 2.8 collective-permute-start.15
  232.1 3.0 convolution_convert_fusion.12
  235.1 3.3 collective-permute-done.12
  238.4 4.2 collective-permute-done.11
  246.0 14.7 %prompt_back.1 = (bf16[1024,192]{1,0:T(8,128)(2,1)}, f32[1024,192]{1,0:T(8,128)}, f32[1024,192]{1,0:T(8,128)}, f32[3,1,1408]{2,1,0:T(1,128)}) custom-call(f32[3,1,1408]{2,1,0:T(1,128)} %reshape.373.line_ref, bf16[1536,192]{1,0:T(8,128)(2,1)} %fusion.10.q_ref, bf16[1536,192]{1,0:T(8,128)(2,1)} %copy-done.20, bf16[192,1536]{1,0:T(8,128)(2,1)} %copy.87.kt_ref, ...), custom_call_target="tpu_custom_call" | custom-call | flops 5033164800 | bytes 5538816 | tf_op jit(solution)/shard_map/prompt_back/pallas_call | solution.py:713
  264.9 15.5 %cont_back.1 = (bf16[512,192]{1,0:T(8,128)(2,1)}, bf16[512,192]{1,0:T(8,128)(2,1)}, bf16[512,192]{1,0:T(8,128)(2,1)}, f32[1024,192]{1,0:T(8,128)}, f32[1024,192]...) custom-call(s32[4]{0:T(128)} %select_reduce_fusion.slot_ref, ...), custom_call_target="tpu_custom_call" | custom-call | flops 4529848320 | bytes 7373824 | tf_op jit(solution)/shard_map/cont_back/pallas_call | solution.py:713
  291.0 3.4 fusion.82
  294.4 2.9 fusion.12
  319.2 3.9 fusion.9
  324.9 135.3 %reduce_all.1 = (bf16[512,768]{1,0:T(8,128)(2,1)}, bf16[512,768]{1,0:T(8,128)(2,1)}, bf16[512,768]{1,0:T(8,128)(2,1)}, bf16[192,768]{1,0:T(8,128)(2,1)}, bf16[19...) custom-call(bf16[4,512,768]{2,1,0:T(8,128)(2,1)} %bitcast.135, ...), custom_call_target="tpu_custom_call" | custom-call | tf_op jit(solution)/shard_map/reduce_all/pallas_call | solution.py:681
  490.1 10.8 %collective-permute-done.20 = bf16[128,768]{1,0:T(8,128)(2,1)S(1)} collective-permute-done((bf16[128,768]{1,0:T(8,128)(2,1)S(1)}, bf16[128,768]{1,0:T(8,128)(2,1)S(1)}, u32[]{:S(2)}, u32[]{:S(2)}) %collective-permute-start.20) | collective-permute-done | bytes 196640 | tf_op jit(solution)/shard_map/ppermute | solution.py:34
  500.9 2.9 collective-permute-done.19
  (360 shorter events, 159.2 us)
Async XLA Ops:
  12.3 107.4 %collective-permute-start.3 = (bf16[2048,192]{0,1:T(8,128)(2,1)}, bf16[2048,192]{0,1:T(8,128)(2,1)}, u32[]{:S(2)}, u32[]{:S(2)}) collective-permute-start(bf16[2048,192]{0,1:T(8,128)(2,1)} %copy.80), channel_id=1, source_target_pairs={{0,4},{4,0},{8,12},{12,8},{16,20},{20,16},{24,28},{28,24},{1,5},{5... | collective-permute-start | bytes 2359304 | tf_op jit(solution)/shard_map/ppermute | solution.py:44
  27.5 117.1 %collective-permute-start.2 = (bf16[256,192]{1,0:T(8,128)(2,1)}, bf16[256,192]{1,0:T(8,128)(2,1)}, u32[]{:S(2)}, u32[]{:S(2)}) collective-permute-start(bf16[256,192]{1,0:T(8,128)(2,1)} %get-tuple-element.260), channel_id=1, source_target_pairs={{3,0},{0,1},{1,2},{2,3},{7,4},{4,5},{5,6},{6,7},{11,8},{8,9},{9,10... | collective-permute-start | bytes 294920 | tf_op jit(solution)/shard_map/ppermute | solution.py:34
  28.8 118.4 %collective-permute-start.1 = (bf16[256,192]{1,0:T(8,128)(2,1)}, bf16[256,192]{1,0:T(8,128)(2,1)}, u32[]{:S(2)}, u32[]{:S(2)}) collective-permute-start(bf16[256,192]{1,0:T(8,128)(2,1)} %get-tuple-element.261), channel_id=1, source_target_pairs={{2,0},{3,1},{0,2},{1,3},{6,4},{7,5},{4,6},{5,7},{10,8},{11,9},{8,1... | collective-permute-start | bytes 294920 | tf_op jit(solution)/shard_map/ppermute | solution.py:34
  29.8 106.1 %collective-permute-start.7 = (bf16[512,768]{1,0:T(8,128)(2,1)}, bf16[512,768]{1,0:T(8,128)(2,1)}, u32[]{:S(2)}, u32[]{:S(2)}) collective-permute-start(bf16[512,768]{1,0:T(8,128)(2,1)} %param.36), channel_id=1, source_target_pairs={{0,4},{4,0},{8,12},{12,8},{16,20},{20,16},{24,28},{28,24},{1,5},{5... | collective-permute-start | bytes 2359304 | tf_op jit(solution)/shard_map/ppermute | solution.py:44
  31.3 4.6 collective-permute-start.8
  34.6 113.3 %copy-start.14 = (bf16[128,768]{1,0:T(8,128)(2,1)}, bf16[128,768]{1,0:T(8,128)(2,1)S(1)}, u32[]{:S(2)}) copy-start(bf16[128,768]{1,0:T(8,128)(2,1)S(1)} %constant_dynamic-slice_fusion.11) | copy-start | bytes 589828
  35.7 112.1 %copy-start.9 = (bf16[256,768]{1,0:T(8,128)(2,1)}, bf16[256,768]{1,0:T(8,128)(2,1)S(1)}, u32[]{:S(2)}) copy-start(bf16[256,768]{1,0:T(8,128)(2,1)S(1)} %constant_dynamic-slice_fusion.12) | copy-start | bytes 1179652
  36.6 2.5 collective-permute-start.9
  39.8 78.6 %collective-permute-start.10 = (f32[8,128]{1,0:T(8,128)S(1)}, f32[8,128]{1,0:T(8,128)S(1)}, u32[]{:S(2)}, u32[]{:S(2)}) collective-permute-start(f32[8,128]{1,0:T(8,128)S(1)} %fusion.149), channel_id=1, source_target_pairs={{0,16},{4,20},{8,24},{12,28},{16,0},{20,4},{24,8},{28,12},{1,17},{... | collective-permute-start | bytes 12296 | tf_op jit(solution)/shard_map/ppermute | solution.py:44
  118.4 28.7 %collective-permute-start = (bf16[256,192]{1,0:T(8,128)(2,1)S(1)}, bf16[256,192]{1,0:T(8,128)(2,1)S(1)}, u32[]{:S(2)}, u32[]{:S(2)}) collective-permute-start(bf16[256,192]{1,0:T(8,128)(2,1)S(1)} %copy-done.59), channel_id=1, source_target_pairs={{1,0},{2,1},{3,2},{0,3},{5,4},{6,5},{7,6},{4,7},{9,8},{10,9},{11,1... | collective-permute-start | bytes 294920 | tf_op jit(solution)/shard_map/ppermute | solution.py:34
  134.7 12.4 %collective-permute-start.6 = (bf16[128,192]{1,0:T(8,128)(2,1)S(1)}, bf16[128,192]{1,0:T(8,128)(2,1)S(1)}, u32[]{:S(2)}, u32[]{:S(2)}) collective-permute-start(bf16[128,192]{1,0:T(8,128)(2,1)S(1)} %get-tuple-element.264), channel_id=1, source_target_pairs={{3,0},{0,1},{1,2},{2,3},{7,4},{4,5},{5,6},{6,7},{11,8},{8,9},{9,10... | collective-permute-start | bytes 147464 | tf_op jit(solution)/shard_map/ppermute | solution.py:34
  135.9 11.3 %collective-permute-start.5 = (bf16[128,192]{1,0:T(8,128)(2,1)S(1)}, bf16[128,192]{1,0:T(8,128)(2,1)S(1)}, u32[]{:S(2)}, u32[]{:S(2)}) collective-permute-start(bf16[128,192]{1,0:T(8,128)(2,1)S(1)} %get-tuple-element.265), channel_id=1, source_target_pairs={{2,0},{3,1},{0,2},{1,3},{6,4},{7,5},{4,6},{5,7},{10,8},{11,9},{8,1... | collective-permute-start | bytes 147464 | tf_op jit(solution)/shard_map/ppermute | solution.py:34
  144.6 3.1 collective-permute-start.4
  222.7 12.4 %collective-permute-start.13 = (bf16[384,192]{1,0:T(8,128)(2,1)S(1)}, bf16[384,192]{1,0:T(8,128)(2,1)S(1)}, u32[]{:S(2)}, u32[]{:S(2)}) collective-permute-start(bf16[384,192]{1,0:T(8,128)(2,1)S(1)} %get-tuple-element.256), channel_id=1, source_target_pairs={{0,3},{1,0},{2,1},{3,2},{4,7},{5,4},{6,5},{7,6},{8,11},{9,8},{10,9... | collective-permute-start | bytes 442376 | tf_op jit(solution)/shard_map/ppermute | solution.py:39
  223.9 14.5 %collective-permute-start.12 = (bf16[384,192]{1,0:T(8,128)(2,1)S(1)}, bf16[384,192]{1,0:T(8,128)(2,1)S(1)}, u32[]{:S(2)}, u32[]{:S(2)}) collective-permute-start(bf16[384,192]{1,0:T(8,128)(2,1)S(1)} %get-tuple-element.257), channel_id=1, source_target_pairs={{0,2},{1,3},{2,0},{3,1},{4,6},{5,7},{6,4},{7,5},{8,10},{9,11},{10,... | collective-permute-start | bytes 442376 | tf_op jit(solution)/shard_map/ppermute | solution.py:39
  225.4 17.2 %collective-permute-start.11 = (bf16[384,192]{1,0:T(8,128)(2,1)S(1)}, bf16[384,192]{1,0:T(8,128)(2,1)S(1)}, u32[]{:S(2)}, u32[]{:S(2)}) collective-permute-start(bf16[384,192]{1,0:T(8,128)(2,1)S(1)} %get-tuple-element.258), channel_id=1, source_target_pairs={{0,1},{1,2},{2,3},{3,0},{4,5},{5,6},{6,7},{7,4},{8,9},{9,10},{10,1... | collective-permute-start | bytes 442376 | tf_op jit(solution)/shard_map/ppermute | solution.py:39
  229.2 68.1 %collective-permute-start.15 = (bf16[512,768]{1,0:T(8,128)(2,1)}, bf16[512,768]{1,0:T(8,128)(2,1)}, u32[]{:S(2)}, u32[]{:S(2)}) collective-permute-start(bf16[512,768]{1,0:T(8,128)(2,1)} %slice.265), channel_id=1, source_target_pairs={{0,4},{4,0},{8,12},{12,8},{16,20},{20,16},{24,28},{28,24},{1,5},{5... | collective-permute-start | bytes 2359304 | tf_op jit(solution)/shard_map/ppermute | solution.py:44
  287.5 16.6 %collective-permute-start.14 = (bf16[2048,192]{0,1:T(8,128)(2,1)}, bf16[2048,192]{0,1:T(8,128)(2,1)}, u32[]{:S(2)}, u32[]{:S(2)}) collective-permute-start(bf16[2048,192]{0,1:T(8,128)(2,1)} %copy.91), channel_id=1, source_target_pairs={{0,4},{4,0},{8,12},{12,8},{16,20},{20,16},{24,28},{28,24},{1,5},{5... | collective-permute-start | bytes 2359304 | tf_op jit(solution)/shard_map/ppermute | solution.py:44
  300.4 182.0 %collective-permute-start.18 = (bf16[128,768]{1,0:T(8,128)(2,1)}, bf16[128,768]{1,0:T(8,128)(2,1)}, u32[]{:S(2)}, u32[]{:S(2)}) collective-permute-start(bf16[128,768]{1,0:T(8,128)(2,1)} %get-tuple-element.248), channel_id=1, source_target_pairs={{0,3},{1,0},{2,1},{3,2},{4,7},{5,4},{6,5},{7,6},{8,11},{9,8},{10,9... | collective-permute-start | bytes 589832 | tf_op jit(solution)/shard_map/ppermute | solution.py:39
  301.5 180.9 %collective-permute-start.17 = (bf16[128,768]{1,0:T(8,128)(2,1)}, bf16[128,768]{1,0:T(8,128)(2,1)}, u32[]{:S(2)}, u32[]{:S(2)}) collective-permute-start(bf16[128,768]{1,0:T(8,128)(2,1)} %get-tuple-element.249), channel_id=1, source_target_pairs={{0,2},{1,3},{2,0},{3,1},{4,6},{5,7},{6,4},{7,5},{8,10},{9,11},{10,... | collective-permute-start | bytes 589832 | tf_op jit(solution)/shard_map/ppermute | solution.py:39
  303.8 178.6 %collective-permute-start.16 = (bf16[128,768]{1,0:T(8,128)(2,1)}, bf16[128,768]{1,0:T(8,128)(2,1)}, u32[]{:S(2)}, u32[]{:S(2)}) collective-permute-start(bf16[128,768]{1,0:T(8,128)(2,1)} %get-tuple-element.247), channel_id=1, source_target_pairs={{0,1},{1,2},{2,3},{3,0},{4,5},{5,6},{6,7},{7,4},{8,9},{9,10},{10,1... | collective-permute-start | bytes 589832 | tf_op jit(solution)/shard_map/ppermute | solution.py:39
  483.7 6.4 %collective-permute-start.21 = (bf16[128,768]{1,0:T(8,128)(2,1)S(1)}, bf16[128,768]{1,0:T(8,128)(2,1)S(1)}, u32[]{:S(2)}, u32[]{:S(2)}) collective-permute-start(bf16[128,768]{1,0:T(8,128)(2,1)S(1)} %add_convert_fusion.4), channel_id=1, source_target_pairs={{3,0},{0,1},{1,2},{2,3},{7,4},{4,5},{5,6},{6,7},{11,8},{8,9},{9,10... | collective-permute-start | bytes 589832 | tf_op jit(solution)/shard_map/ppermute | solution.py:34
  484.2 16.8 %collective-permute-start.20 = (bf16[128,768]{1,0:T(8,128)(2,1)S(1)}, bf16[128,768]{1,0:T(8,128)(2,1)S(1)}, u32[]{:S(2)}, u32[]{:S(2)}) collective-permute-start(bf16[128,768]{1,0:T(8,128)(2,1)S(1)} %add_convert_fusion.4), channel_id=1, source_target_pairs={{2,0},{3,1},{0,2},{1,3},{6,4},{7,5},{4,6},{5,7},{10,8},{11,9},{8,1... | collective-permute-start | bytes 589832 | tf_op jit(solution)/shard_map/ppermute | solution.py:34
  485.8 18.1 %collective-permute-start.19 = (bf16[128,768]{1,0:T(8,128)(2,1)S(1)}, bf16[128,768]{1,0:T(8,128)(2,1)S(1)}, u32[]{:S(2)}, u32[]{:S(2)}) collective-permute-start(bf16[128,768]{1,0:T(8,128)(2,1)S(1)} %add_convert_fusion.4), channel_id=1, source_target_pairs={{1,0},{2,1},{3,2},{0,3},{5,4},{6,5},{7,6},{4,7},{9,8},{10,9},{11,1... | collective-permute-start | bytes 589832 | tf_op jit(solution)/shard_map/ppermute | solution.py:34
  (89 other events, 426.1 us)

commit v4 on v3

--- a/solution.py
+++ b/solution.py
@@ -102,15 +102,15 @@
 
 
 def cont_rows(slot):
-    return pl.ds(pl.multiple_of(slot * CONT_LEN, CONT_LEN), CONT_LEN)
+    return pl.ds(slot * CONT_LEN, CONT_LEN)
 
 
 def late_rows(slot):
-    return pl.ds(pl.multiple_of(PROMPT + slot * CONT_LEN, CONT_LEN), CONT_LEN)
+    return pl.ds(PROMPT + slot * CONT_LEN, CONT_LEN)
 
 
 def cont_fwd(
-    slot_ref, line_ref, ok_ref, q_ref, k_ref, v_ref, kf_ref, vf_ref, o_ref, lse_ref, slab
+    line_ref, ok_ref, q_ref, k_ref, v_ref, kf_ref, vf_ref, o_ref, lse_ref, slab
 ):
     head = pl.program_id(0)
     slab[...] = make_slab(line_ref[0])
@@ -125,7 +125,7 @@
 
     for pair in range(2):
         keys_ref, values_ref = (k_ref, v_ref) if pair == 0 else (kf_ref, vf_ref)
-        slots = [slot_ref[2 * pair], slot_ref[2 * pair + 1]]
+        slots = [2 * pair, 2 * pair + 1]
         qs = [q_ref[late_rows(slot), :] * mask for slot in slots]
         s = mm(jnp.concatenate(qs, axis=0), keys_ref[0:PROMPT, :], NT)
         s = s + jnp.concatenate([slab[:, 0:PROMPT], slab[:, 0:PROMPT]], axis=0)
@@ -173,136 +173,6 @@
     for r in range(rows):
         line = line + pltpu.roll(block, rows - 1 - r, 1)[r : r + 1]
     return line
-
-
-def prompt_back(
-    line_ref, q_ref, k_ref, kt_ref, v_ref, do_ref, lse_ref, dq_ref, dk_ref, dv_ref, gl_ref,
-    slab, gslab, dqt,
-):
-    head = pl.program_id(0)
-    slab[...] = make_slab(line_ref[0]).T
-    gslab[...] = jnp.zeros_like(gslab)
-    width = q_ref.shape[1]
-    mask = head_mask(head, width, BF)
-
-    @pl.when(head == 0)
-    def _():
-        dk_ref[...] = jnp.zeros_like(dk_ref)
-        dv_ref[...] = jnp.zeros_like(dv_ref)
-
-    mine = pl.ds(pl.multiple_of(head * HEAD, HEAD), HEAD)
-    block = 2 * TILE
-    for idx in range(PROMPT // block):
-        keys = block * (idx + 1)
-        rows = pl.ds(idx * block, block)
-        q = q_ref[rows, :] * mask
-        do = do_ref[rows, :] * mask
-        s = mm(k_ref[0:keys, :], q, NT)
-        start = PROMPT - block * idx
-        s = s + jnp.concatenate(
-            [slab[start : start + keys, :], slab[start - TILE : start - TILE + keys, :]], axis=1
-        )
-        p = jnp.exp(s - row_of(lse_ref[rows, :], head))
-        dp = mm(v_ref[0:keys, :], do, NT)
-        centre = jnp.sum(p * dp, axis=0, keepdims=True)
-        ds = p * (dp - centre)
-        low = ds.astype(BF)
-        dv_ref[0:keys, :] = dv_ref[0:keys, :] + mm(p.astype(BF), do)
-        dk_ref[0:keys, :] = dk_ref[0:keys, :] + mm(low, q)
-        dqt[mine, rows] = mm(kt_ref[mine, 0:keys], low)
-        gslab[start : start + keys, :] = gslab[start : start + keys, :] + ds[:, 0:TILE]
-        gslab[start - TILE : start - TILE + keys, :] = (
-            gslab[start - TILE : start - TILE + keys, :] + ds[:, TILE:block]
-        )
-    gl_ref[0] = fold_slab(gslab[...].T)
-
-    @pl.when(head == pl.num_programs(0) - 1)
-    def _():
-        dq_ref[...] = (dqt[...].T * HEAD ** (-0.5)).astype(BF)
-
-
-def cont_back(
-    slot_ref, line_ref, ok_ref, q_ref, k_ref, kt_ref, v_ref, kf_ref, ktf_ref, vf_ref, do_ref,
-    lse_ref, dq_ref, dkc_ref, dvc_ref, dk_ref, dv_ref, dkf_ref, dvf_ref, gl_ref,
-    slab, gslab, dqt, dkc, dvc, dkf, dvf,
-):
-    head = pl.program_id(0)
-    slab[...] = make_slab(line_ref[0]).T
-    gslab[...] = jnp.zeros_like(gslab)
-    width = q_ref.shape[1]
-    mask = head_mask(head, width, BF)
-
-    @pl.when(head == 0)
-    def _():
-        for ref in (dk_ref, dv_ref, dkf, dvf, dkc, dvc):
-            ref[...] = jnp.zeros_like(ref)
-
-    mine = pl.ds(pl.multiple_of(head * HEAD, HEAD), HEAD)
-    for pair in range(2):
-        keys_ref, kt, values_ref = (
-            (k_ref, kt_ref, v_ref) if pair == 0 else (kf_ref, ktf_ref, vf_ref)
-        )
-        gk, gv = (dk_ref, dv_ref) if pair == 0 else (dkf, dvf)
-        slots = [slot_ref[2 * pair], slot_ref[2 * pair + 1]]
-        qs = [q_ref[late_rows(slot), :] * mask for slot in slots]
-        dos = [do_ref[cont_rows(slot), :] * mask for slot in slots]
-        q = jnp.concatenate(qs, axis=0)
-        do = jnp.concatenate(dos, axis=0)
-        lse = row_of(
-            jnp.concatenate([lse_ref[cont_rows(slot), :] for slot in slots], axis=0), head
-        )
-        s = mm(keys_ref[0:PROMPT, :], q, NT)
-        s = s + jnp.concatenate([slab[0:PROMPT, :], slab[0:PROMPT, :]], axis=1)
-        own = jnp.concatenate(
-            [
-                mm(k_ref[late_rows(slot), :], qc, NT) + slab[PROMPT:DIST, :] + ok_ref[slot]
-                for qc, slot in zip(qs, slots)
-            ],
-            axis=1,
-        )
-        p = jnp.exp(s - lse)
-        p_own = jnp.exp(own - lse)
-        dp = mm(values_ref[0:PROMPT, :], do, NT)
-        dp_own = jnp.concatenate(
-            [mm(v_ref[late_rows(slot), :], doc, NT) for doc, slot in zip(dos, slots)], axis=1
-        )
-        centre = jnp.sum(p * dp, axis=0, keepdims=True) + jnp.sum(
-            p_own * dp_own, axis=0, keepdims=True
-        )
-        ds = p * (dp - centre)
-        ds_own = p_own * (dp_own - centre)
-        low = ds.astype(BF)
-        low_own = ds_own.astype(BF)
-        p_low = p_own.astype(BF)
-        gv[...] = gv[...] + mm(p.astype(BF), do)
-        gk[...] = gk[...] + mm(low, q)
-        dq = mm(kt[mine, 0:PROMPT], low)
-        for i, slot in enumerate(slots):
-            part = slice(CONT_LEN * i, CONT_LEN * (i + 1))
-            here = cont_rows(slot)
-            dvc[here, :] = dvc[here, :] + mm(p_low[:, part], dos[i])
-            dkc[here, :] = dkc[here, :] + mm(low_own[:, part], qs[i])
-            kown = k_ref[late_rows(slot), :].T
-            head_keys = kown[0:HEAD, :]
-            for other in range(1, width // HEAD):
-                head_keys = jnp.where(
-                    head == other, kown[HEAD * other : HEAD * (other + 1), :], head_keys
-                )
-            dqt[slot, mine, :] = dq[:, part] + mm(head_keys, low_own[:, part])
-            gslab[0:PROMPT, :] = gslab[0:PROMPT, :] + ds[:, part]
-            gslab[PROMPT:DIST, :] = gslab[PROMPT:DIST, :] + ds_own[:, part]
-    gl_ref[0] = fold_slab(gslab[...].T)
-
-    @pl.when(head == pl.num_programs(0) - 1)
-    def _():
-        for slot in range(dqt.shape[0]):
-            dq_ref[slot * CONT_LEN : (slot + 1) * CONT_LEN, :] = (
-                dqt[slot].T * HEAD ** (-0.5)
-            ).astype(BF)
-        dkf_ref[...] = dkf[...].astype(BF)
-        dvf_ref[...] = dvf[...].astype(BF)
-        dkc_ref[...] = dkc[...].astype(BF)
-        dvc_ref[...] = dvc[...].astype(BF)
 
 
 def cross_fwd(far_ref, q_ref, k_ref, v_ref, o_ref, lse_ref):
@@ -443,15 +313,6 @@
     return pl.ds(pl.multiple_of(start, step), size)
 
 
-def run_pairs(streams, stages):
-    pairs = [streams[i : i + 2] for i in range(0, len(streams), 2)]
-    for step in range(len(pairs) + stages):
-        for index in reversed(range(len(pairs))):
-            if 0 <= step - index <= stages:
-                for stream in pairs[index]:
-                    next(stream, None)
-
-
 def bit_order(place):
     return (1, 2) if place % 2 == 0 else (2, 1)
 
@@ -510,7 +371,8 @@
         gather_stream(links, own[index], full[index], stages[place], first, rows, place)
         for place, (index, first, rows) in enumerate(chunks)
     ]
-    run_pairs(streams, 4)
+    for ignored in pair_steps(streams, 4):
+        pass
 
 
 def gather_all(own, bits):
@@ -536,8 +398,28 @@
     )(*own)
 
 
-def reduce_stream(links, grad, total, room, first, rows, place, slabs):
-    mine, from_core, from_one, from_two, from_far, from_more = room
+CORE_ROOMS = 8
+
+
+def flip_rank(rank, bits):
+    for bit in bits:
+        rank = rank + bit * (1 - 2 * (rank // bit % 2))
+    return rank
+
+
+def pair_steps(streams, stages):
+    pairs = [streams[i : i + 2] for i in range(0, len(streams), 2)]
+    for step in range(len(pairs) + stages):
+        for index in reversed(range(len(pairs))):
+            if 0 <= step - index <= stages:
+                for stream in pairs[index]:
+                    next(stream, None)
+        yield
+
+
+def reduce_stream(links, grad, total, core_room, room, first, rows, place, slabs):
+    mine, from_one, from_two, from_far, from_more = room
+    from_core = core_room.at[pl.ds(0, slabs), pl.ds(0, rows), :]
     one, two = bit_order(place)
     half = grad.shape[2] // 2
     whole_rows = pl.ds(first, rows)
@@ -568,19 +450,24 @@
     keep = span(base_two, rows // 4, 16)
     if slabs > 1:
         mine[:, keep, :] = mine[:, keep, :] + from_two[...]
+        slab = [
+            (flip_rank(links.tensor, flips) - links.tensor + slabs) % slabs
+            for flips in ((), (1,), (2,), (1, 2))
+        ]
         copies = [
-            links.send(mine.at[step, keep, :], from_far.at[step - 1], links.ahead(step))
-            for step in range(1, slabs)
+            links.send(mine.at[slab[1], keep, :], from_far.at[0], links.across(0)),
+            links.send(mine.at[slab[3], keep, :], from_far.at[1], links.across(0)),
         ]
         yield
         for copy in copies:
             copy.wait()
-        value = mine[0, keep, :].astype(F32)
-        for step in range(slabs - 1):
-            value = value + from_far[step].astype(F32)
-        value = value.astype(BF)
+        mine[slab[2], keep, :] = mine[slab[2], keep, :] + from_far[1]
+        copy = links.send(mine.at[slab[2], keep, :], from_far.at[2], links.across(1))
+        yield
+        copy.wait()
+        value = mine[0, keep, :].astype(F32) + from_far[0].astype(F32)
+        value = (value + from_far[2].astype(F32)).astype(BF)
     else:
-        yield
         value = mine[0, keep, :] + from_two[0]
     quarter = span(first + base_two, rows // 4, 16)
     for index in range(3, links.bits):
@@ -604,8 +491,7 @@
     copy.wait()
 
 
-def small_stream(links, small, held, came, grouped, final):
-    held[0] = small[...]
+def small_stream(links, held, came, grouped, final):
     tensor_bits = links.ranks.bit_length() - 1
     for index in range(links.bits + tensor_bits):
         device = links.partner(index) if index < links.bits else links.across(index - links.bits)
@@ -617,92 +503,358 @@
         if index == links.bits - 1:
             grouped[...] = value
     final[...] = value
-    yield
-
-
-def reduce_kernel(count, bits, chunks, parts, *refs):
+
+
+def rows_stream(links, parts, came, out, rows):
+    copy = links.send(
+        parts.at[pl.ds(2, 2), rows, :], came.at[pl.ds(0, 2), rows, :], links.across(0)
+    )
+    yield
+    copy.wait()
+    parts[1, rows, :] = parts[1, rows, :] + came[1, rows, :]
+    copy = links.send(parts.at[1, rows, :], came.at[2, rows, :], links.across(1))
+    yield
+    copy.wait()
+    out[rows, :] = (
+        parts[0, rows, :].astype(F32) + came[0, rows, :].astype(F32) + came[2, rows, :].astype(F32)
+    )
+
+
+def rows_streams(links, parts, came, out, pieces):
+    size = out.shape[0] // pieces
+    active = []
+    for piece in range(pieces + 2):
+        if piece < pieces:
+            active.append(rows_stream(links, parts, came, out, pl.ds(piece * size, size)))
+        for stream in reversed(active):
+            next(stream, None)
+        yield
+
+
+def encoder_stream(links, enc, from_core, total, came, final):
+    count = from_core.shape[0]
+    here = [flip_rank(links.tensor, flips) for flips in ((), (1,), (2,), (1, 2))]
+    kept = links.local(enc.at[pl.ds(0, count)], total)
+    copy = links.send(enc.at[pl.ds(count, count)], from_core, links.partner(0))
+    yield
+    kept.wait()
+    copy.wait()
+    total[...] = total[...] + from_core[...]
+    copies = [
+        links.send(total.at[here[1]], came.at[0], links.across(0)),
+        links.send(total.at[here[3]], came.at[1], links.across(0)),
+    ]
+    yield
+    for copy in copies:
+        copy.wait()
+    total[here[2]] = total[here[2]] + came[1]
+    copy = links.send(total.at[here[2]], came.at[2], links.across(1))
+    yield
+    copy.wait()
+    value = total[here[0]].astype(F32) + came[0].astype(F32) + came[2].astype(F32)
+    final[here[0]] = value.astype(BF)
+    copies = [links.send(final.at[here[0]], final.at[here[0]], links.across(1))]
+    yield
+    copies[0].wait()
+    copies = [
+        links.send(final.at[place], final.at[place], links.across(0))
+        for place in (here[0], here[2])
+    ]
+    yield
+    for copy in copies:
+        copy.wait()
+
+
+def attend_back(ins, work, heads):
+    line_ref, ok_ref, q_ref, k_ref, v_ref, kt_ref, kf_ref, vf_ref, ktf_ref, lse_ref, late_ref = ins
+    do_ref, do_late, slab, gslab, dqt, dqc, dk, dv, dkc, dvc, dkf, dvf, held = work
+    width = q_ref.shape[1]
+    block = 2 * TILE
+    for ref in (dk, dv, dkf, dvf, dkc, dvc):
+        ref[...] = jnp.zeros_like(ref)
+    for head in range(heads):
+        slab[...] = make_slab(line_ref[head]).T
+        gslab[...] = jnp.zeros_like(gslab)
+        mask = head_mask(head, width, BF)
+        mine = pl.ds(head * HEAD, HEAD)
+        for pair in range(2):
+            keys_ref, kt, values_ref = (
+                (k_ref, kt_ref, v_ref) if pair == 0 else (kf_ref, ktf_ref, vf_ref)
+            )
+            gk, gv = (dk, dv) if pair == 0 else (dkf, dvf)
+            slots = [2 * pair, 2 * pair + 1]
+            qs = [q_ref[late_rows(slot), :] * mask for slot in slots]
+            dos = [do_late[slot] * mask for slot in slots]
+            q = jnp.concatenate(qs, axis=0)
+            do = jnp.concatenate(dos, axis=0)
+            lse = row_of(
+                jnp.concatenate([late_ref[cont_rows(slot), :] for slot in slots], axis=0), head
+            )
+            s = mm(keys_ref[0:PROMPT, :], q, NT)
+            s = s + jnp.concatenate([slab[0:PROMPT, :], slab[0:PROMPT, :]], axis=1)
+            keys_own = [k_ref[late_rows(slot), :] for slot in slots]
+            own = jnp.concatenate(
+                [
+                    mm(keys, qc, NT) + slab[PROMPT:DIST, :] + ok_ref[slot]
+                    for keys, qc, slot in zip(keys_own, qs, slots)
+                ],
+                axis=1,
+            )
+            p = jnp.exp(s - lse)
+            p_own = jnp.exp(own - lse)
+            dp = mm(values_ref[0:PROMPT, :], do, NT)
+            dp_own = jnp.concatenate(
+                [mm(v_ref[late_rows(slot), :], doc, NT) for doc, slot in zip(dos, slots)], axis=1
+            )
+            centre = jnp.sum(p * dp, axis=0, keepdims=True) + jnp.sum(
+                p_own * dp_own, axis=0, keepdims=True
+            )
+            ds = p * (dp - centre)
+            ds_own = p_own * (dp_own - centre)
+            low = ds.astype(BF)
+            low_own = ds_own.astype(BF)
+            p_low = p_own.astype(BF)
+            gv[...] = gv[...] + mm(p.astype(BF), do)
+            gk[...] = gk[...] + mm(low, q)
+            dq = mm(kt[mine, 0:PROMPT], low)
+            for i in range(2):
+                part = slice(CONT_LEN * i, CONT_LEN * (i + 1))
+                spot = 2 * pair + i
+                here = pl.ds(spot * CONT_LEN, CONT_LEN)
+                dvc[here, :] = dvc[here, :] + mm(p_low[:, part], dos[i])
+                dkc[here, :] = dkc[here, :] + mm(low_own[:, part], qs[i])
+                head_keys = keys_own[i].T[head * HEAD : (head + 1) * HEAD, :]
+                dqc[spot, mine, :] = dq[:, part] + mm(head_keys, low_own[:, part])
+                gslab[0:PROMPT, :] = gslab[0:PROMPT, :] + ds[:, part]
+                gslab[PROMPT:DIST, :] = gslab[PROMPT:DIST, :] + ds_own[:, part]
+            yield
+        for idx in range(PROMPT // block):
+            keys = block * (idx + 1)
+            rows = pl.ds(idx * block, block)
+            q = q_ref[rows, :] * mask
+            do = do_ref[idx, pl.ds(0, block), :] * mask
+            s = mm(k_ref[0:keys, :], q, NT)
+            start = PROMPT - block * idx
+            s = s + jnp.concatenate(
+                [slab[start : start + keys, :], slab[start - TILE : start - TILE + keys, :]],
+                axis=1,
+            )
+            p = jnp.exp(s - row_of(lse_ref[rows, :], head))
+            dp = mm(v_ref[0:keys, :], do, NT)
+            centre = jnp.sum(p * dp, axis=0, keepdims=True)
+            ds = p * (dp - centre)
+            low = ds.astype(BF)
+            dv[0:keys, :] = dv[0:keys, :] + mm(p.astype(BF), do)
+            dk[0:keys, :] = dk[0:keys, :] + mm(low, q)
+            dqt[mine, rows] = mm(kt_ref[mine, 0:keys], low)
+            gslab[start : start + keys, :] = gslab[start : start + keys, :] + ds[:, 0:TILE]
+            gslab[start - TILE : start - TILE + keys, :] = (
+                gslab[start - TILE : start - TILE + keys, :] + ds[:, TILE:block]
+            )
+            yield
+        held[0, pl.ds(4 + head, 1), :] = fold_slab(gslab[...].T)
+
+
+def reduce_kernel(count, bits, chunks, heads, pace, *refs):
     refs = list(refs)
-    grads = [refs.pop(0) for _ in range(count)]
-    sends_in = [refs.pop(0) for _ in range(parts)]
-    small = refs.pop(0)
-    totals = [refs.pop(0) for _ in range(count)]
-    came_in = [refs.pop(0) for _ in range(parts)]
-    grouped, final = refs.pop(0), refs.pop(0)
-    local, receives, sends = refs.pop(), refs.pop(), refs.pop()
-    came, held = refs.pop(), refs.pop()
-    rooms = [refs[6 * i : 6 * i + 6] for i in range(len(chunks))]
+
+    def take(number):
+        taken, refs[:number] = refs[:number], []
+        return taken
+
+    (hot_ref,) = take(1)
+    ins = take(11)
+    n1_ref, unit_ref, wq_ref, wk_ref, wv_ref, small_ref, do_in, enc_in = take(8)
+    grads = take(count)
+    totals = take(count + 3)
+    enc_final, out, grouped, final = take(4)
+    do_ref, do_late, slab, gslab, dqt, dqc, dk, dv, dkc, dvc, dkf, dvf = take(12)
+    lent_out, lent_in, dq_all, dk_all, dv_all, parts, came_rows = take(7)
+    grads = grads + take(3)
+    held, came, enc_core, enc_total, enc_came = take(5)
+    core_rooms = take(CORE_ROOMS)
+    sends, receives, local = refs[-3:]
+    rooms = [refs[5 * i : 5 * i + 5] for i in range(len(chunks))]
     links = Links(sends, receives, local, bits)
     links.barrier()
-    rows_moved = [
-        links.send(source.at[(links.tensor + step) % links.ranks], target.at[step - 1],
-                   links.ahead(step))
-        for source, target in zip(sends_in, came_in)
-        for step in range(1, links.ranks)
+    ranks = links.ranks
+    width = n1_ref.shape[1]
+    moved = [
+        links.send(do_in.at[step], do_ref.at[links.tensor], links.ahead(step))
+        for step in range(1, ranks)
     ]
-    streams = [small_stream(links, small, held, came, grouped, final)]
+    stay = links.local(do_in.at[0], do_ref.at[links.tensor])
     streams = [
         reduce_stream(
-            links, grads[index], totals[index], rooms[place], first, rows, place,
-            grads[index].shape[0],
+            links, grads[index], totals[index], core_rooms[place % CORE_ROOMS], rooms[place], first,
+            rows, place, grads[index].shape[0],
         )
         for place, (index, first, rows) in enumerate(chunks)
-    ] + streams
-    run_pairs(streams, max(7, bits + links.ranks.bit_length() - 1))
-    for copy in rows_moved:
+    ]
+    encoder = encoder_stream(links, enc_in, enc_core, enc_total, enc_came, enc_final)
+    pairs = pair_steps(streams, 8)
+
+    def steps():
+        for ignored in pairs:
+            next(encoder, None)
+            yield
+
+    comm = steps()
+    next(comm)
+    next(comm)
+    next(comm)
+    held[0] = small_ref[...]
+    stay.wait()
+    for copy in moved:
         copy.wait()
-
-
-def reduce_all(grads, parts, small, bits):
+    conts = dqc.shape[0]
+    share = PROMPT // ranks
+    for i in range(conts):
+        value = 0.0
+        for cont in range(conts):
+            late = do_ref[cont, pl.ds(share, CONT_LEN), :].astype(F32)
+            value = value + late * hot_ref[cont, i][0:1, 0:1]
+        do_late[i] = value.astype(BF)
+    work = (do_ref, do_late, slab, gslab, dqt, dqc, dk, dv, dkc, dvc, dkf, dvf, held)
+    for number, ignored in enumerate(attend_back(ins, work, heads)):
+        if number % pace == pace - 1:
+            next(comm)
+
+    lent_out[0] = dkf[...].astype(BF)
+    lent_out[1] = dvf[...].astype(BF)
+    lent = links.send(lent_out, lent_in, links.partner(0))
+    dq_all[0:PROMPT, :] = (dqt[...].T * HEAD ** (-0.5)).astype(BF)
+    for i in range(conts):
+        here = late_rows(i)
+        spot = cont_rows(i)
+        dq_all[here, :] = (dqc[i].T * HEAD ** (-0.5)).astype(BF)
+        dk_all[here, :] = dkc[spot, :].astype(BF)
+        dv_all[here, :] = dvc[spot, :].astype(BF)
+    lent.wait()
+    dk_all[0:PROMPT, :] = (dk[...] + lent_in[0].astype(F32)).astype(BF)
+    dv_all[0:PROMPT, :] = (dv[...] + lent_in[1].astype(F32)).astype(BF)
+    gain = jnp.zeros((1, width), F32)
+
+    def input_grad(rows):
+        value = (
+            mm(dq_all[rows, :], wq_ref[...], NT)
+            + mm(dk_all[rows, :], wk_ref[...], NT)
+            + mm(dv_all[rows, :], wv_ref[...], NT)
+        )
+        return value, jnp.sum(value * unit_ref[rows, :].astype(F32), axis=0, keepdims=True)
+
+    late = []
+    for i in range(conts):
+        value, term = input_grad(late_rows(i))
+        late.append(value)
+        gain = gain + term
+    for place, flips in ((2, (1,)), (3, (1, 2)), (1, (2,)), (0, ())):
+        rank = flip_rank(links.tensor, flips)
+        value, term = input_grad(span(rank * share, share, 16))
+        gain = gain + term
+        parts[place, pl.ds(0, share), :] = value.astype(BF)
+        total = 0.0
+        for i in range(conts):
+            total = total + late[i] * hot_ref[rank, i][0:1, 0:1]
+        parts[place, pl.ds(share, CONT_LEN), :] = total.astype(BF)
+    held[0, 0:1, 0:width] = gain
+    extras = [
+        rows_streams(links, parts, came_rows, out, 8),
+        small_stream(links, held, came, grouped, final),
+    ]
+    for stream in extras:
+        next(stream)
+    for index, whole_ref in enumerate((dq_all, dk_all, dv_all)):
+        grads[count + index][0] = mm(whole_ref[...], n1_ref[...], TN).astype(BF)
+    for ignored in comm:
+        for stream in extras:
+            next(stream, None)
+    for stream in extras:
+        for ignored in stream:
+            pass
+
+
+def reduce_all(hot, ins, mats, small, do_in, enc, grads, bits, heads, pace):
     ranks = lax.axis_size("tensor")
+    width = mats[0].shape[1]
+    cols = heads * HEAD
+    half = width // 2
     chunks = split_chunks([a.shape[1] for a in grads], 200)
-    chunks = [c for c in chunks if grads[c[0]].shape[0] > 1] + [
-        c for c in chunks if grads[c[0]].shape[0] == 1
-    ]
-    width = small.shape[1]
-    half = width // 2
+    chunks += [(len(grads) + i, 0, cols) for i in range(3)]
     more = max(bits - 3, 1)
+    conts = hot.shape[0]
+    late = conts * CONT_LEN
+    own = PROMPT // ranks + CONT_LEN
     rooms = []
     for index, _, rows in chunks:
-        slabs = grads[index].shape[0]
+        slabs = grads[index].shape[0] if index < len(grads) else 1
         rooms += [
-            pltpu.VMEM((slabs, rows, half), BF),
             pltpu.VMEM((slabs, rows, half), BF),
             pltpu.VMEM((slabs, rows // 2, half), BF),
             pltpu.VMEM((slabs, rows // 4, half), BF),
-            pltpu.VMEM((ranks - 1, rows // 4, half), BF),
+            pltpu.VMEM((3, rows // 4, half), BF),
             pltpu.VMEM((more, rows // 4, half), BF),
         ]
     small_steps = bits + ranks.bit_length() - 1
-    copies = (
-        len(chunks) * (6 + ranks - 1 + bits - 3) + len(parts) * (ranks - 1) + small_steps
-    )
+    copies = len(chunks) * (9 + bits - 3) + small_steps + ranks + 24
+    enc_block = (enc.shape[1], width)
     any_space = pl.BlockSpec(memory_space=pl.ANY)
     vmem = pl.BlockSpec(memory_space=pltpu.VMEM)
     out = pl.pallas_call(
-        functools.partial(reduce_kernel, len(grads), bits, chunks, len(parts)),
+        functools.partial(reduce_kernel, len(grads), bits, chunks, heads, pace),
         out_shape=shaped(
             *[(a.shape[1:], BF) for a in grads],
-            *[((ranks - 1,) + a.shape[1:], a.dtype) for a in parts],
+            *[((cols, width), BF)] * 3,
+            ((ranks,) + enc_block, BF),
+            ((own, width), F32),
             (small.shape, F32),
             (small.shape, F32),
         ),
-        in_specs=[any_space] * (len(grads) + len(parts)) + [vmem],
-        out_specs=[vmem] * len(grads) + [any_space] * len(parts) + [vmem] * 2,
-        scratch_shapes=rooms
-        + [
+        in_specs=[vmem] * (len(ins) + len(mats) + 2)
+        + [any_space] * (2 + len(grads)),
+        out_specs=[vmem] * (len(grads) + 7),
+        scratch_shapes=[
+            pltpu.VMEM(do_in.shape, BF),
+            pltpu.VMEM((conts, CONT_LEN, cols), BF),
+            pltpu.VMEM((SLAB, TILE), F32),
+            pltpu.VMEM((SLAB, TILE), F32),
+            pltpu.VMEM((cols, PROMPT), F32),
+            pltpu.VMEM((conts, cols, CONT_LEN), F32),
+            pltpu.VMEM((PROMPT, cols), F32),
+            pltpu.VMEM((PROMPT, cols), F32),
+            pltpu.VMEM((late, cols), F32),
+            pltpu.VMEM((late, cols), F32),
+            pltpu.VMEM((PROMPT, cols), F32),
+            pltpu.VMEM((PROMPT, cols), F32),
+            pltpu.VMEM((2, PROMPT, cols), BF),
+            pltpu.VMEM((2, PROMPT, cols), BF),
+            pltpu.VMEM((PROMPT + late, cols), BF),
+            pltpu.VMEM((PROMPT + late, cols), BF),
+            pltpu.VMEM((PROMPT + late, cols), BF),
+            pltpu.VMEM((ranks, own, width), BF),
+            pltpu.VMEM((ranks - 1, own, width), BF),
+            pltpu.VMEM((1, cols, width), BF),
+            pltpu.VMEM((1, cols, width), BF),
+            pltpu.VMEM((1, cols, width), BF),
             pltpu.VMEM((small_steps + 1,) + small.shape, F32),
             pltpu.VMEM((small_steps,) + small.shape, F32),
+            pltpu.VMEM((ranks,) + enc_block, BF),
+            pltpu.VMEM((ranks,) + enc_block, BF),
+            pltpu.VMEM((ranks - 1,) + enc_block, BF),
+        ]
+        + [pltpu.VMEM((ranks, max(c[2] for c in chunks), half), BF)] * CORE_ROOMS
+        + rooms
+        + [
             pltpu.SemaphoreType.DMA((copies,)),
             pltpu.SemaphoreType.DMA((copies,)),
-            pltpu.SemaphoreType.DMA((len(chunks),)),
+            pltpu.SemaphoreType.DMA((len(chunks) + 2,)),
         ],
         compiler_params=pltpu.CompilerParams(
-            collective_id=2, has_side_effects=True, vmem_limit_bytes=60 * 2**20
+            collective_id=2, has_side_effects=True, vmem_limit_bytes=67043328
         ),
         name="reduce_all",
-    )(*grads, *parts, small)
-    count = len(grads)
-    return out[:count], out[count:-2], out[-2], out[-1]
+    )(hot, *ins, *mats, small, do_in, enc, *grads)
+    return out[: len(grads) + 3], out[-4], out[-3], out[-2], out[-1]
 
 
 def run_heads(kernel, heads, scalars, lines, arrays, outs, scratch, out_heads, cells, name):
@@ -775,6 +927,19 @@
     far_rank = jnp.sum(jnp.where(before, far[None, :], 0), axis=1)
     spot = jnp.where(far == 0, near_rank, cont_count // 2 + far_rank)
     slots = jnp.sum(jnp.where(spot[None, :] == index[:, None], index[None, :], 0), axis=1)
+    hot = jnp.broadcast_to(
+        (spot[:, None] == index[None, :]).astype(F32)[:, :, None, None],
+        (cont_count, cont_count, 8, 128),
+    )
+
+    def by_place(rows):
+        return jnp.concatenate(
+            [
+                lax.dynamic_slice_in_dim(rows, slots[i] * CONT_LEN, CONT_LEN, 0)
+                for i in range(cont_count)
+            ]
+        )
+
     far_here = lax.dynamic_slice_in_dim(far, tensor_rank, 1, 0)
 
     def own_rows(prompt_rows, conts):
@@ -800,7 +965,7 @@
     line = jnp.concatenate(
         [table, jnp.full((heads, LINE - DIST), masked_value, F32)], axis=1
     ).reshape(heads, 1, LINE)
-    ok = jnp.where(valid > 0, 0.0, masked_value).astype(F32)
+    ok = jnp.where(by_place(valid) > 0, 0.0, masked_value).astype(F32)
     ok_rows = jnp.broadcast_to(
         ok.reshape(cont_count, 1, CONT_LEN), (cont_count, CONT_LEN, CONT_LEN)
     )
@@ -808,7 +973,7 @@
         ok.reshape(cont_count, CONT_LEN, 1), (cont_count, CONT_LEN, CONT_LEN)
     )
 
-    stream = jnp.concatenate([x_prompt, x_cont]).astype(F32)
+    stream = jnp.concatenate([x_prompt, by_place(x_cont)]).astype(F32)
     n1 = rms_norm(stream, gain_self).astype(BF)
     key_s = mm(n1, w_k).astype(BF)
     value_s = mm(n1, w_v).astype(BF)
@@ -828,31 +993,21 @@
         PROMPT * PROMPT * 5 // 8, "prompt_fwd",
     )
     o_cont, lse_cont = run_heads(
-        cont_fwd, heads, [slots], [line], [ok_rows, query_s, key_s, value_s, key_far, value_far],
+        cont_fwd, heads, [], [line], [ok_rows, query_s, key_s, value_s, key_far, value_far],
         shaped(((rows_late, cols), BF), ((rows_late, cols), F32)), [slab], (),
         rows_late * DIST, "cont_fwd",
     )
 
-    def heads_to_rows(block, rows):
+    def heads_to_rows(block, rows, places):
         out = []
         for step in range(ranks):
             dest = (tensor_rank - step + ranks) % ranks
-            piece = lax.dynamic_slice_in_dim(block, dest * rows, rows, 0)
+            piece = lax.dynamic_slice_in_dim(block, places[dest] * rows, rows, 0)
             out.append(piece if step == 0 else from_ahead(piece, step))
         return jnp.concatenate(out, axis=1)
 
-    def rows_to_heads(block):
-        out = []
-        for step in range(ranks):
-            piece = block[:, step * cols : (step + 1) * cols]
-            out.append(piece if step == 0 else to_ahead(piece, step))
-        rows = block.shape[0]
-        held = jnp.concatenate(out, axis=0).reshape(ranks, rows, cols)
-        pick = (tensor_rank - jnp.arange(ranks) + ranks) % ranks
-        return (held, pick)
-
     mixed_self = jnp.concatenate(
-        [heads_to_rows(o_prompt, share), heads_to_rows(o_cont, CONT_LEN)]
+        [heads_to_rows(o_prompt, share, index), heads_to_rows(o_cont, CONT_LEN, spot)]
     )
 
     wo_full, cq_t, ck_t, cv_t, co_full = (
@@ -959,106 +1114,32 @@
         mm(d_value_c, enc_pair, TN).astype(BF),
         mm(mixed_cross, g2_low, TN).astype(BF),
     ]
-    d_mixed_s = mm(g1_low, wo_full, NT).astype(BF)
-    held, pick = rows_to_heads(d_mixed_s)
-    place = (pick[None, :] == jnp.arange(ranks)[:, None]).astype(BF)
-    ordered = jnp.einsum("ns,src->nrc", place, held, preferred_element_type=F32).astype(BF)
-    do_prompt = ordered[:, :share].reshape(PROMPT, cols)
-    do_cont = ordered[:, share:].reshape(rows_late, cols)
-
-    key_far_t = key_far.T
-    (dq_cont, dk_cont, dv_cont, dk_near, dv_near, dk_far, dv_far, line_cont) = run_heads(
-        cont_back, heads, [slots], [line],
-        [ok_cols, query_s, key_s, key_t, value_s, key_far, key_far_t, value_far, do_cont, lse_cont],
-        shaped(
-            ((rows_late, cols), BF), ((rows_late, cols), BF), ((rows_late, cols), BF),
-            ((PROMPT, cols), F32), ((PROMPT, cols), F32),
-            ((PROMPT, cols), BF), ((PROMPT, cols), BF), ((heads, 1, LINE), F32),
-        ),
-        [slab_t, slab_t, pltpu.VMEM((cont_count, cols, CONT_LEN), F32)]
-        + [pltpu.VMEM((rows_late, cols), F32)] * 2 + [pltpu.VMEM((PROMPT, cols), F32)] * 2,
-        (7,), rows_late * DIST, "cont_back",
-    )
-    lent = flip_bit(jnp.concatenate([dk_far, dv_far], axis=0), 0)
-    dq_prompt, dk_prompt, dv_prompt, line_prompt = run_heads(
-        prompt_back, heads, [], [line],
-        [query_s, key_s, key_t, value_s, do_prompt, lse_prompt],
-        shaped(
-            ((PROMPT, cols), BF), ((PROMPT, cols), F32), ((PROMPT, cols), F32),
-            ((heads, 1, LINE), F32),
-        ),
-        [slab_t, slab_t, pltpu.VMEM((cols, PROMPT), F32)], (3,),
-        PROMPT * PROMPT * 5 // 8, "prompt_back",
-    )
-    dk_prompt = (dk_prompt + dk_near + lent[:PROMPT].astype(F32)).astype(BF)
-    dv_prompt = (dv_prompt + dv_near + lent[PROMPT:].astype(F32)).astype(BF)
-
-    def three(q, k, v):
-        return mm(q, w_q, NT) + mm(k, w_k, NT) + mm(v, w_v, NT)
-
-    def scatter_rows(block, rows):
-        total = lax.dynamic_slice_in_dim(block, tensor_rank * rows, rows, 0).astype(F32)
-        for step in range(1, ranks):
-            dest = (tensor_rank + step) % ranks
-            piece = lax.dynamic_slice_in_dim(block, dest * rows, rows, 0)
-            total = total + to_ahead(piece, step).astype(F32)
-        return total
-
-    part_cont = three(dq_cont, dk_cont, dv_cont).astype(BF)
-    part_prompt = three(dq_prompt, dk_prompt, dv_prompt).astype(BF)
-    unit = stream * norm_scale(stream)
-    gain_self_part = jnp.sum(part_prompt.astype(F32) * unit[:PROMPT], axis=0) + jnp.sum(
-        part_cont.astype(F32) * unit[PROMPT:], axis=0
-    )
-
-    enc_part = mm(d_key_c, ck_t) + mm(d_value_c, cv_t)
-    enc_sum = (enc_part[:ENC_LEN] + flip_bit(enc_part[ENC_LEN:].astype(BF), 0).astype(F32)).astype(
-        BF
-    )
-    enc_rows = ENC_LEN // ranks
-    enc_own = scatter_rows(enc_sum, enc_rows).astype(BF)
-    enc_all = jnp.concatenate(
-        [enc_own] + [from_ahead(enc_own, step) for step in range(1, ranks)]
-    )
-    enc_place = jnp.arange(ENC_LEN)
-    enc_from = (tensor_rank + enc_place // enc_rows) % ranks * enc_rows + enc_place % enc_rows
-    enc_hot = (enc_from[:, None] == enc_place[None, :]).astype(BF)
-    grad_enc = mm(enc_hot, enc_all, TN)
-
-    def by_rows(prompt_part, cont_part):
-        return mm(prompt_part, n1[:PROMPT], TN) + mm(cont_part, n1[PROMPT:], TN)
-
-    qkv_grads = [
-        by_rows(dq_prompt, dq_cont).astype(BF),
-        by_rows(dk_prompt, dk_cont).astype(BF),
-        by_rows(dv_prompt, dv_cont).astype(BF),
-    ]
-
-    line_grad = (line_cont + line_prompt).reshape(heads, LINE)[:, :DIST]
-    table_part = jnp.dot(line_grad, bucket_hot, precision=lax.Precision.HIGHEST)
-    small = jnp.zeros((8, width), F32)
-    small = small.at[0].set(gain_self_part).at[1].set(gain_cross_part).at[2].set(gain_ffn_part)
+    d_mixed_s = jnp.einsum("nd,zcd->znc", g1_low, wo_all, preferred_element_type=F32).astype(BF)
+    enc_part = (mm(d_key_c, ck_t) + mm(d_value_c, cv_t)).astype(BF)
+
+    small = jnp.zeros((8, LINE), F32)
+    small = small.at[1, :width].set(gain_cross_part).at[2, :width].set(gain_ffn_part)
     small = small.at[3, 0].set(loss_part)
-    small = small.at[4, : table_part.size].set(table_part.reshape(-1))
-
-    totals, came, grouped, small = reduce_all(
+    unit = (stream * norm_scale(stream)).astype(BF)
+    totals, enc_sum, d_n1, grouped, small = reduce_all(
+        hot,
+        [line, ok_cols, query_s, key_s, value_s, key_t, key_far, value_far, key_far.T,
+         lse_prompt, lse_cont],
+        [n1, unit, w_q, w_k, w_v],
+        small,
+        d_mixed_s,
+        enc_part.reshape(2 * ranks, ENC_LEN // ranks, width),
         [a.reshape(ranks, hidden_here, width) for a in ffn_grads]
-        + [a.reshape(ranks, cols, width) for a in attn_grads]
-        + [a.reshape(1, cols, width) for a in qkv_grads],
-        [part_prompt.reshape(ranks, share, width), part_cont.reshape(ranks, CONT_LEN, width)],
-        small,
+        + [a.reshape(ranks, cols, width) for a in attn_grads],
         bits,
+        heads,
+        4,
     )
     totals = [total.astype(F32) for total in totals]
-    grad_table = grouped[4, : table_part.size].reshape(table_part.shape).T
-
-    def own_total(block, rows, others):
-        total = lax.dynamic_slice_in_dim(block, tensor_rank * rows, rows, 0).astype(F32)
-        return total + jnp.sum(others.astype(F32), axis=0)
-
-    d_n1 = jnp.concatenate(
-        [own_total(part_prompt, share, came[0]), own_total(part_cont, CONT_LEN, came[1])]
-    )
+    grad_enc = enc_sum.reshape(ENC_LEN, width).astype(F32)
+    grad_table = jnp.dot(
+        grouped[4 : 4 + heads, :DIST], bucket_hot, precision=lax.Precision.HIGHEST
+    ).T
     back1, ignored = norm_back(x_own, gain_self, d_n1)
     grad_x = g1 + back1
     return (
@@ -1067,9 +1148,9 @@
         grad_x[:share],
         grad_x[share:],
         grad_enc,
-        small[0],
-        small[1],
-        small[2],
+        small[0, :width],
+        small[1, :width],
+        small[2, :width],
         grad_table,
         totals[8].T,
         totals[9].T,

time: 516 us -> 426 us (0.83)
  the two profiles are of different devices: /device:TPU:9 before, /device:TPU:0 now
where the time goes in v4:
time: 426 us; the launch traced here: 418 us
  Pallas kernels  256 us (60%)
  matrix products  63.7 us (15%)
  local copies, waits for them, and re-layouts  45.4 us (11%)
  other arithmetic  23.9 us (6%)
  starting transfers between devices  17.3 us (4%)
  between operations  9.75 us (2%)
    pallas_call x1, Pallas kernels, reduce_all(): pl.pallas_call(functools.partial(reduce_kernel, len(grads), bits, chunks,...  145 us
    pallas_call x1, Pallas kernels, gather_all(): pl.pallas_call(functools.partial(gather_kernel, len(own), bits, chunks),...  68.7 us
    dot_general x26, matrix products, mm(): return lax.dot_general(left, right, dims, preferred_element_type=F32)  61.4 us
    pallas_call x2, Pallas kernels, run_heads(): pl.pallas_call(kernel, out_shape=outs, grid_spec=pltpu.PrefetchScalarGrid...  17.1 us
    unnamed x180, local copies, waits for them, and re-layouts  15.8 us
    pallas_call x1, Pallas kernels, on_device(): pl.pallas_call(cross_back, out_shape=shaped(((own_count, pairs * TILE), B...  14.8 us
    ppermute x6, starting transfers between devices, from_ahead(): lax.ppermute(block, 'tensor', [((i + step) % count, i) for i in range(cou...  13 us
    pallas_call x1, Pallas kernels, on_device(): pl.pallas_call(cross_fwd, out_shape=shaped(((own_count, pairs * TILE), BF...  10.3 us
  transfers between devices with their start and end apart: 11, of which 2 were waited for; matrix products, arithmetic and copies ran while one was open for 9% of the time, Pallas kernels for 21%

profile of v4, /device:TPU:0, one launch (start us, length us, event | category | flops | bytes accessed | tf_op | source)
XLA Modules:
  0.0 418.4 jit_solution(1085768342891124887)
XLA Ops:
  16.1 2.2 copy.85.v_ref.refs_5_
  21.8 8.7 %prompt_fwd.1 = (bf16[1024,192]{1,0:T(8,128)(2,1)}, f32[1024,192]{1,0:T(8,128)}) custom-call(f32[3,1,1408]{2,1,0:T(1,128)} %reshape.354.line_ref.refs_1_, bf16[1536,192]{1,0:T(8,128)(2,1)} %fusion.12.q_ref.refs_3_, bf16[1536,192]{1,0:T(8,128)(2,1)} %copy.84.k_ref.refs_4_, bf16[1536,192]{1,0:T(8,128)(2,1)} %copy.85.v_ref.refs_5_), custom_call_target="tpu_custom_call" | custom-call | flops 2013265920 | bytes 2966016 | tf_op jit(solution)/shard_map/prompt_fwd/pallas_call | solution.py:865
  32.4 2.6 collective-permute-start.2
  35.0 2.6 collective-permute-start.1
  39.4 2.1 constant_dynamic-update-slice_fusion.2
  60.4 68.7 %gather_all.1 = (bf16[4,192,768]{2,1,0:T(8,128)(2,1)}, bf16[4,192,768]{2,1,0:T(8,128)(2,1)}, bf16[4,192,768]{2,1,0:T(8,128)(2,1)}, bf16[4,192,768]{2,1,0:T(8,128...) custom-call(bf16[192,768]{1,0:T(8,128)(2,1)} %refs_0_.1, ...), custom_call_target="tpu_custom_call" | custom-call | tf_op jit(solution)/shard_map/gather_all/pallas_call | solution.py:383
  129.1 3.9 collective-permute-start
  138.3 8.4 %cont_fwd.1 = (bf16[512,192]{1,0:T(8,128)(2,1)}, f32[512,192]{1,0:T(8,128)}) custom-call(f32[3,1,1408]{2,1,0:T(1,128)} %reshape.354.line_ref.refs_1_, f32[4,128,128]{2,1,0:T(8,128)} %broadcast_in_dim.43.ok_ref, bf16[1536,192]{1,0:T(8,128)(2,1)} %fusion.12.q_ref.refs_3_, bf16[1536,192]{1,0:T(8,128)(2,1)} %copy.84.k_ref.refs_4_, ...), custom_call_target="tpu_custom_call" | custom-call | flops 1811939328 | bytes 3424768 | tf_op jit(solution)/shard_map/cont_fwd/pallas_call | solution.py:865
  150.5 4.1 convolution_convert_fusion.7.k_ref
  154.6 3.2 collective-permute-start.4
  157.9 2.6 convolution_convert_fusion.6.v_ref
  164.2 10.3 %cross_fwd.1 = (bf16[384,768]{1,0:T(8,128)(2,1)}, f32[384,768]{1,0:T(8,128)}) custom-call(s32[1]{0:T(128)} %dynamic_slice.110.far_ref, bf16[384,768]{1,0:T(8,128)(2,1)} %fusion.15.q_ref, bf16[1024,768]{1,0:T(8,128)(2,1)} %convolution_convert_fusion.7.k_ref, bf16[1024,768]{1,0:T(8,128)(2,1)} %convolution_convert_fusion.6.v_ref), custom_call_target="tpu_custom_call" | custom-call | flops 2415919104 | bytes 3735552 | tf_op jit(solution)/shard_map/cross_fwd/pallas_call | solution.py:1030
  184.7 3.7 fusion.11
  189.8 3.5 convolution_convert_fusion.2
  193.3 3.6 convolution_convert_fusion
  196.8 4.1 convolution_convert_fusion.1
  201.0 2.9 multiply_reduce_fusion
  205.7 14.8 %cross_back.1 = (bf16[384,768]{1,0:T(8,128)(2,1)}, bf16[1024,768]{1,0:T(8,128)(2,1)}, bf16[1024,768]{1,0:T(8,128)(2,1)}) custom-call(s32[1]{0:T(128)} %dynamic_slice.110.far_ref, bf16[384,768]{1,0:T(8,128)(2,1)} %fusion.15.q_ref, bf16[1024,768]{1,0:T(8,128)(2,1)} %convolution_convert_fusion.7.k_ref, bf16[1024,768]{1,0:T(8,128)(2,1)} %convolution_convert_fusion.6.v_ref, ...), custom_call_target="tpu_custom_call" | custom-call | flops 6039797760 | bytes 3735552 | tf_op jit(solution)/shard_map/cross_back/pallas_call | solution.py:1084
  224.3 3.1 fusion.45
  227.5 2.5 convolution_convert_fusion.10
  235.7 4.0 convolution_convert_fusion.9
  239.8 2.6 add_convert_fusion
  243.7 3.0 convolution_convert_fusion.12
  248.3 145.1 %reduce_all.1 = (bf16[512,768]{1,0:T(8,128)(2,1)}, bf16[512,768]{1,0:T(8,128)(2,1)}, bf16[512,768]{1,0:T(8,128)(2,1)}, bf16[192,768]{1,0:T(8,128)(2,1)}, bf16[19...) custom-call(f32[4,4,8,128]{3,2,1,0:T(8,128)} %broadcast_in_dim.45.re, ...), custom_call_target="tpu_custom_call" | custom-call | tf_op jit(solution)/shard_map/reduce_all/pallas_call | solution.py:803
  (290 shorter events, 96.2 us)
Async XLA Ops:
  7.6 153.1 %copy-start.8 = (bf16[128,768]{1,0:T(8,128)(2,1)}, bf16[128,768]{1,0:T(8,128)(2,1)S(1)}, u32[]{:S(2)}) copy-start(bf16[128,768]{1,0:T(8,128)(2,1)S(1)} %get-tuple-element.203) | copy-start | bytes 589828
  14.3 119.2 %collective-permute-start.3 = (bf16[2048,192]{0,1:T(8,128)(2,1)}, bf16[2048,192]{0,1:T(8,128)(2,1)}, u32[]{:S(2)}, u32[]{:S(2)}) collective-permute-start(bf16[2048,192]{0,1:T(8,128)(2,1)} %pad_maximum_fusion.1), channel_id=1, source_target_pairs={{0,4},{4,0},{8,12},{12,8},{16,20},{20,16},{24,28},{28,24},{1,5},{5... | collective-permute-start | bytes 2359304 | tf_op jit(solution)/shard_map/ppermute | solution.py:44
  21.8 15.7 %copy-start.57 = (s32[512]{0:T(512)S(1)}, s32[512]{0:T(512)}, u32[]{:S(2)}) copy-start(s32[512]{0:T(512)} %param.36) | copy-start | bytes 6148
  32.4 128.3 %copy-start.46 = (bf16[256,192]{1,0:T(8,128)(2,1)}, bf16[256,192]{1,0:T(8,128)(2,1)S(1)}, u32[]{:S(2)}) copy-start(bf16[256,192]{1,0:T(8,128)(2,1)S(1)} %get-tuple-element.204) | copy-start | bytes 294916
  32.4 122.2 %collective-permute-start.2 = (bf16[256,192]{1,0:T(8,128)(2,1)}, bf16[256,192]{1,0:T(8,128)(2,1)}, u32[]{:S(2)}, u32[]{:S(2)}) collective-permute-start(bf16[256,192]{1,0:T(8,128)(2,1)} %get-tuple-element.205), channel_id=1, source_target_pairs={{3,0},{0,1},{1,2},{2,3},{7,4},{4,5},{5,6},{6,7},{11,8},{8,9},{9,10... | collective-permute-start | bytes 294920 | tf_op jit(solution)/shard_map/ppermute | solution.py:34
  35.0 125.5 %collective-permute-start.1 = (bf16[256,192]{1,0:T(8,128)(2,1)}, bf16[256,192]{1,0:T(8,128)(2,1)}, u32[]{:S(2)}, u32[]{:S(2)}) collective-permute-start(bf16[256,192]{1,0:T(8,128)(2,1)} %get-tuple-element.206), channel_id=1, source_target_pairs={{2,0},{3,1},{0,2},{1,3},{6,4},{7,5},{4,6},{5,7},{10,8},{11,9},{8,1... | collective-permute-start | bytes 294920 | tf_op jit(solution)/shard_map/ppermute | solution.py:34
  37.6 110.3 %collective-permute-start.7 = (bf16[512,768]{1,0:T(8,128)(2,1)}, bf16[512,768]{1,0:T(8,128)(2,1)}, u32[]{:S(2)}, u32[]{:S(2)}) collective-permute-start(bf16[512,768]{1,0:T(8,128)(2,1)} %param.32), channel_id=1, source_target_pairs={{0,4},{4,0},{8,12},{12,8},{16,20},{20,16},{24,28},{28,24},{1,5},{5... | collective-permute-start | bytes 2359304 | tf_op jit(solution)/shard_map/ppermute | solution.py:44
  38.8 5.3 %collective-permute-start.8 = (f32[8,128]{1,0:T(8,128)S(1)}, f32[8,128]{1,0:T(8,128)S(1)}, u32[]{:S(2)}, u32[]{:S(2)}) collective-permute-start(f32[8,128]{1,0:T(8,128)S(1)} %broadcast_in_dim.44), channel_id=1, source_target_pairs={{0,4},{4,0},{8,12},{12,8},{16,20},{20,16},{24,28},{28,24},{1,5},{5... | collective-permute-start | bytes 12296 | tf_op jit(solution)/shard_map/ppermute | solution.py:44
  39.4 16.0 %copy-start.40 = (bf16[768,192]{0,1:T(8,128)(2,1)S(1)}, bf16[768,192]{0,1:T(8,128)(2,1)}, u32[]{:S(2)}) copy-start(bf16[768,192]{0,1:T(8,128)(2,1)} %param.44) | copy-start | bytes 884740
  41.5 14.9 %copy-start.42 = (bf16[768,192]{0,1:T(8,128)(2,1)S(1)}, bf16[768,192]{0,1:T(8,128)(2,1)}, u32[]{:S(2)}) copy-start(bf16[768,192]{0,1:T(8,128)(2,1)} %param.45) | copy-start | bytes 884740
  42.2 15.2 %copy-start.20 = (bf16[768,512]{1,0:T(8,128)(2,1)S(1)}, bf16[768,512]{1,0:T(8,128)(2,1)}, u32[]{:S(2)}) copy-start(bf16[768,512]{1,0:T(8,128)(2,1)} %param.51) | copy-start | bytes 2359300
  43.3 117.4 %copy-start.4 = (bf16[256,768]{1,0:T(8,128)(2,1)}, bf16[256,768]{1,0:T(8,128)(2,1)S(1)}, u32[]{:S(2)}) copy-start(bf16[256,768]{1,0:T(8,128)(2,1)S(1)} %constant_dynamic-slice_fusion.9) | copy-start | bytes 1179652
  44.8 3.7 collective-permute-start.9
  49.1 80.0 %collective-permute-start.10 = (f32[8,128]{1,0:T(8,128)S(1)}, f32[8,128]{1,0:T(8,128)S(1)}, u32[]{:S(2)}, u32[]{:S(2)}) collective-permute-start(f32[8,128]{1,0:T(8,128)S(1)} %fusion.89), channel_id=1, source_target_pairs={{0,16},{4,20},{8,24},{12,28},{16,0},{20,4},{24,8},{28,12},{1,17},{... | collective-permute-start | bytes 12296 | tf_op jit(solution)/shard_map/ppermute | solution.py:44
  60.3 132.9 %copy-start.10 = (f32[256,768]{1,0:T(8,128)}, f32[256,768]{1,0:T(8,128)S(1)}, u32[]{:S(2)}) copy-start(f32[256,768]{1,0:T(8,128)S(1)} %convert_element_type.164) | copy-start | bytes 2359300
  60.4 68.7 %copy-start.48 = (bf16[256,192]{1,0:T(8,128)(2,1)S(1)}, bf16[256,192]{1,0:T(8,128)(2,1)}, u32[]{:S(2)}) copy-start(bf16[256,192]{1,0:T(8,128)(2,1)} %get-tuple-element.207) | copy-start | bytes 294916
  129.1 31.4 %collective-permute-start = (bf16[256,192]{1,0:T(8,128)(2,1)S(1)}, bf16[256,192]{1,0:T(8,128)(2,1)S(1)}, u32[]{:S(2)}, u32[]{:S(2)}) collective-permute-start(bf16[256,192]{1,0:T(8,128)(2,1)S(1)} %copy-done.48), channel_id=1, source_target_pairs={{1,0},{2,1},{3,2},{0,3},{5,4},{6,5},{7,6},{4,7},{9,8},{10,9},{11,1... | collective-permute-start | bytes 294920 | tf_op jit(solution)/shard_map/ppermute | solution.py:34
  147.8 12.9 %copy-start.49 = (bf16[128,192]{1,0:T(8,128)(2,1)}, bf16[128,192]{1,0:T(8,128)(2,1)S(1)}, u32[]{:S(2)}) copy-start(bf16[128,192]{1,0:T(8,128)(2,1)S(1)} %get-tuple-element.208) | copy-start | bytes 147460
  147.8 12.7 %collective-permute-start.6 = (bf16[128,192]{1,0:T(8,128)(2,1)S(1)}, bf16[128,192]{1,0:T(8,128)(2,1)S(1)}, u32[]{:S(2)}, u32[]{:S(2)}) collective-permute-start(bf16[128,192]{1,0:T(8,128)(2,1)S(1)} %get-tuple-element.209), channel_id=1, source_target_pairs={{3,0},{0,1},{1,2},{2,3},{7,4},{4,5},{5,6},{6,7},{11,8},{8,9},{9,10... | collective-permute-start | bytes 147464 | tf_op jit(solution)/shard_map/ppermute | solution.py:34
  147.9 12.6 %collective-permute-start.5 = (bf16[128,192]{1,0:T(8,128)(2,1)S(1)}, bf16[128,192]{1,0:T(8,128)(2,1)S(1)}, u32[]{:S(2)}, u32[]{:S(2)}) collective-permute-start(bf16[128,192]{1,0:T(8,128)(2,1)S(1)} %get-tuple-element.210), channel_id=1, source_target_pairs={{2,0},{3,1},{0,2},{1,3},{6,4},{7,5},{4,6},{5,7},{10,8},{11,9},{8,1... | collective-permute-start | bytes 147464 | tf_op jit(solution)/shard_map/ppermute | solution.py:34
  154.6 6.1 %collective-permute-start.4 = (bf16[128,192]{1,0:T(8,128)(2,1)S(1)}, bf16[128,192]{1,0:T(8,128)(2,1)S(1)}, u32[]{:S(2)}, u32[]{:S(2)}) collective-permute-start(bf16[128,192]{1,0:T(8,128)(2,1)S(1)} %get-tuple-element.211), channel_id=1, source_target_pairs={{1,0},{2,1},{3,2},{0,3},{5,4},{6,5},{7,6},{4,7},{9,8},{10,9},{11,1... | collective-permute-start | bytes 147464 | tf_op jit(solution)/shard_map/ppermute | solution.py:34
  164.2 10.3 %copy-start.6 = (bf16[4,192,768]{2,1,0:T(8,128)(2,1)S(1)}, bf16[4,192,768]{2,1,0:T(8,128)(2,1)}, u32[]{:S(2)}) copy-start(bf16[4,192,768]{2,1,0:T(8,128)(2,1)} %get-tuple-element.96) | copy-start | bytes 3538948
  205.7 14.8 %copy-start.17 = (bf16[4,192,768]{2,1,0:T(8,128)(2,1)S(1)}, bf16[4,192,768]{2,1,0:T(8,128)(2,1)}, u32[]{:S(2)}) copy-start(bf16[4,192,768]{2,1,0:T(8,128)(2,1)} %get-tuple-element.92) | copy-start | bytes 3538948
  233.7 9.9 %copy-start = (f32[384,768]{1,0:T(8,128)}, f32[384,768]{1,0:T(8,128)S(1)}, u32[]{:S(2)}) copy-start(f32[384,768]{1,0:T(8,128)S(1)} %multiply_add_fusion) | copy-start | bytes 3538948
  (71 other events, 212.3 us)
